TPU v7x, 32 devices: a whole 2x2x4 slice. The times are simulated.
32 devices in a mesh: dp: 8 (over z, x), expert: 4 (over y, core).
Axes of the slice: x: 2, y: 2, z: 4, core: 2. Of those that a mesh axis runs over, the one named last changes fastest.
Arguments:
- tokens: bfloat16 [37632, 384], P(('dp', 'expert')), may hold values from -6 to 6
- cotangent: float32 [37632, 384], P(('dp', 'expert')), may hold values from -6 to 6
- routes: int32 [37632, 1], P(('dp', 'expert')), may hold values from 0 to 3; in each aligned block of 1176 rows (0 to 1175, 1176 to 2351, ...) at most 588 rows name the same one
- valid_mask: int32 [37632], P(('dp', 'expert')), may hold values from 0 to 1, as said below
- shift_region: int32 [37632], P(('dp', 'expert')), may hold values from 0 to 8, as said below
- qkv_weight: float32 [384, 1152], P('dp'), may hold values from -0.4375 to 0.4375
- proj_weight: float32 [384, 384], P('dp'), may hold values from -1.25 to 1.25
- router_weight: float32 [384, 4], P('dp'), may hold values from -0.21875 to 0.21875
- norm_params: float32 [384, 4], P('dp'), may hold values from -0.9 to 1.4, as said below
- expert_in: float32 [4, 384, 1536], P('expert', 'dp'), may hold values from -0.3125 to 0.3125
- expert_out: float32 [4, 384, 1536], P('expert', 'dp'), may hold values from -1.75 to 1.75
- qkv_first: float32 [384, 1152], P('dp'), may hold values from -121.46295 to 121.46295
- qkv_second: float32 [384, 1152], P('dp'), may hold values from 3.7632 to 15.0528
- proj_first: float32 [384, 384], P('dp'), may hold values from -85.887279 to 85.887279
- proj_second: float32 [384, 384], P('dp'), may hold values from 1.8816 to 7.5264
- router_first: float32 [384, 4], P('dp'), may hold values from -5008.046 to 5008.046
- router_second: float32 [384, 4], P('dp'), may hold values from 6397.44 to 25589.76
- norm_first: float32 [384, 4], P('dp'), may hold values from -384.09959 to 384.09959
- norm_second: float32 [384, 4], P('dp'), may hold values from 37.632 to 150.528
- in_first: float32 [4, 384, 1536], P('expert', 'dp'), may hold values from -66.528 to 66.528
- in_second: float32 [4, 384, 1536], P('expert', 'dp'), may hold values from 1.12896 to 4.51584
- out_first: float32 [4, 384, 1536], P('expert', 'dp'), may hold values from -12.1462954 to 12.1462954
- out_second: float32 [4, 384, 1536], P('expert', 'dp'), may hold values from 0.037632 to 0.150528
Outputs:
- block_output: bfloat16 [37632, 384], P(('dp', 'expert'))
- input_grad: float32 [37632, 384], P(('dp', 'expert'))
- qkv_weight_new: float32 [384, 1152], P('dp')
- proj_weight_new: float32 [384, 384], P('dp')
- router_weight_new: float32 [384, 4], P('dp')
- norm_params_new: float32 [384, 4], P('dp')
- expert_in_new: float32 [4, 384, 1536], P('expert', 'dp')
- expert_out_new: float32 [4, 384, 1536], P('expert', 'dp')
- qkv_first_new: float32 [384, 1152], P('dp')
- proj_first_new: float32 [384, 384], P('dp')
- router_first_new: float32 [384, 4], P('dp')
- norm_first_new: float32 [384, 4], P('dp')
- in_first_new: float32 [4, 384, 1536], P('expert', 'dp')
- out_first_new: float32 [4, 384, 1536], P('expert', 'dp')
- qkv_second_new: float32 [384, 1152], P('dp')
- proj_second_new: float32 [384, 384], P('dp')
- router_second_new: float32 [384, 4], P('dp')
- norm_second_new: float32 [384, 4], P('dp')
- in_second_new: float32 [4, 384, 1536], P('expert', 'dp')
- out_second_new: float32 [4, 384, 1536], P('expert', 'dp')
- trust_norms: float32 [4, 6, 2], P('expert')
Inputs may be any that keep to these rules, and one draw needn't show every extreme that they name: `routes`: in each aligned block of 1176 rows (the rows of one device) at most 588 rows name one expert, a bound that some block reaches. `valid_mask`: windows come from images of 12 x 12, 14 x 14 or 16 x 16 patches, padded to whole windows; padding is 0. `shift_region`: region of the grid after a cyclic shift by 3 patches; 0 in windows away from the grid's last row and column of windows. `norm_params`: columns 0 and 2 are gains, columns 1 and 3 shifts.
All inputs are finite; a program needn't handle non-finite values.
Results may differ from a plain program's by a relative error of at most 0.014.
The roundings to bfloat16 on the way count: a program that leaves them out, or rounds other values in their place, can miss the bound.
Values may be sent and summed in bfloat16 or wider, within the bound.
A program may use at most 128 MiB of HBM per device.

v0:
```python
import jax
import jax.numpy as jnp
from jax import lax
from jax.sharding import PartitionSpec as P

HEADS = 12
HEAD_DIM = 32
WINDOW = 49
STEP = 5


NORM_EPS = 1e-05
MASKED = -1e30
BETA_ONE = 0.9
BETA_TWO = 0.999
ADAM_EPS = 1e-06
DECAY = 0.01
RATE = 0.3


def layer_norm(values, gain, shift):
    average = jnp.mean(values, axis=-1, keepdims=True)
    centred = values - average
    variance = jnp.mean(centred * centred, axis=-1, keepdims=True)
    return centred * lax.rsqrt(variance + NORM_EPS) * gain + shift


def allowed_pairs(valid_mask, shift_region, groups):
    valid_w = valid_mask.reshape(groups, WINDOW)
    region_w = shift_region.reshape(groups, WINDOW)
    same_region = region_w[:, :, None] == region_w[:, None, :]
    keeps = same_region & (valid_w[:, None, :] == 1)
    diagonal = jnp.eye(WINDOW, dtype=jnp.bool_)
    return keeps | diagonal[None]


def lamb_direction(weight, grad, first, second):
    first_new = BETA_ONE * first + (1.0 - BETA_ONE) * grad
    second_new = BETA_TWO * second + (1.0 - BETA_TWO) * grad * grad
    first_hat = first_new / (1.0 - BETA_ONE**STEP)
    second_hat = second_new / (1.0 - BETA_TWO**STEP)
    direction = first_hat / (jnp.sqrt(second_hat) + ADAM_EPS) + DECAY * weight
    return (first_new, second_new, direction)


def per_device(
    tokens,
    cotangent,
    routes,
    valid_mask,
    shift_region,
    qkv_weight,
    proj_weight,
    router_weight,
    norm_params,
    expert_in,
    expert_out,
    qkv_first,
    qkv_second,
    proj_first,
    proj_second,
    router_first,
    router_second,
    norm_first,
    norm_second,
    in_first,
    in_second,
    out_first,
    out_second,
):
    f32 = jnp.float32
    bf16 = jnp.bfloat16
    width = tokens.shape[1]
    rows_here = tokens.shape[0]
    experts = lax.axis_size("expert") * expert_in.shape[0]
    capacity = 2 * rows_here // experts
    groups = rows_here // WINDOW
    weights_now = (qkv_weight, proj_weight, router_weight, norm_params, expert_in[0], expert_out[0])
    firsts_now = (qkv_first, proj_first, router_first, norm_first, in_first[0], out_first[0])
    seconds_now = (qkv_second, proj_second, router_second, norm_second, in_second[0], out_second[0])
    weight_sq = jnp.stack([jnp.sum(weight_now * weight_now) for weight_now in weights_now])
    weight_total = lax.psum(weight_sq, "dp")
    w_qkv, w_proj, w_router, w_norm, w_up, w_down = (
        lax.all_gather(qkv_weight.astype(bf16), "dp", axis=0, tiled=True),
        lax.all_gather(proj_weight.astype(bf16), "dp", axis=0, tiled=True),
        lax.all_gather(router_weight.astype(bf16), "dp", axis=0, tiled=True),
        lax.all_gather(norm_params.astype(bf16), "dp", axis=0, tiled=True),
        lax.all_gather(expert_in[0].astype(bf16), "dp", axis=0, tiled=True),
        lax.all_gather(expert_out[0].astype(bf16), "dp", axis=0, tiled=True),
    )
    norm_f = w_norm.astype(f32)
    x_f = tokens.astype(f32)
    h1_f, pull_one = jax.vjp(layer_norm, x_f, norm_f[:, 0], norm_f[:, 1])
    h1_b = h1_f.astype(bf16)
    raw = jnp.dot(h1_b, w_qkv, preferred_element_type=f32)
    col_scale = jnp.concatenate(
        [jnp.full((width,), HEAD_DIM ** (-0.5), f32), jnp.ones((2 * width,), f32)]
    )
    qkv_b = (raw * col_scale).astype(bf16)
    query_heads = qkv_b[:, :width].reshape(groups, WINDOW, HEADS, HEAD_DIM)
    key_heads = qkv_b[:, width : 2 * width].reshape(groups, WINDOW, HEADS, HEAD_DIM)
    value_heads = qkv_b[:, 2 * width :].reshape(groups, WINDOW, HEADS, HEAD_DIM)
    allowed = allowed_pairs(valid_mask, shift_region, groups)

    def window_scores():
        scores = jnp.einsum("wqhd,wkhd->whqk", query_heads, key_heads, preferred_element_type=f32)
        return jnp.where(allowed[:, None], scores, MASKED)

    scores = window_scores()
    top_score = jnp.max(scores, axis=-1, keepdims=True)
    log_total = top_score + jnp.log(jnp.sum(jnp.exp(scores - top_score), axis=-1, keepdims=True))
    probs_b = jnp.exp(scores - log_total).astype(bf16)
    mixed = jnp.einsum("whqk,wkhd->wqhd", probs_b, value_heads, preferred_element_type=f32)
    mixed_b = mixed.reshape(rows_here, width).astype(bf16)
    y_one = x_f + jnp.dot(mixed_b, w_proj, preferred_element_type=f32)
    h2_f, pull_two = jax.vjp(layer_norm, y_one, norm_f[:, 2], norm_f[:, 3])
    h2_b = h2_f.astype(bf16)
    logits = jnp.dot(h2_b, w_router, preferred_element_type=f32)
    route_ids = routes[:, 0]
    onehot = route_ids[:, None] == jnp.arange(experts, dtype=jnp.int32)[None, :]
    onehot_f = onehot.astype(f32)

    def gate_fn(values):
        return jnp.sum(jax.nn.softmax(values, axis=-1) * onehot_f, axis=-1)

    gate_prob, pull_gate = jax.vjp(gate_fn, logits)
    counts_int = onehot.astype(jnp.int32)
    slot_index = jnp.sum((jnp.cumsum(counts_int, axis=0) - 1) * counts_int, axis=1)
    send = jnp.zeros((experts, capacity, width), bf16).at[route_ids, slot_index].set(h2_b)
    received = lax.all_to_all(send, "expert", split_axis=0, concat_axis=0, tiled=True)
    up_proj = jnp.einsum("scd,df->scf", received, w_up, preferred_element_type=f32)
    hidden_b = jax.nn.gelu(up_proj, approximate=False).astype(bf16)
    result_b = jnp.einsum("scf,df->scd", hidden_b, w_down, preferred_element_type=f32).astype(bf16)
    result_b, up_proj, hidden_b, received = (result_b, up_proj, hidden_b, received)
    returned = lax.all_to_all(result_b, "expert", split_axis=0, concat_axis=0, tiled=True)
    expert_tok = returned[route_ids, slot_index].astype(f32)
    block_output = (y_one + gate_prob[:, None] * expert_tok).astype(bf16)
    grad_out = cotangent * valid_mask.astype(f32)[:, None]
    grad_gate = jnp.sum(grad_out * expert_tok, axis=-1)
    grad_send = (
        jnp.zeros((experts, capacity, width), bf16)
        .at[route_ids, slot_index]
        .set((gate_prob[:, None] * grad_out).astype(bf16))
    )
    grad_recv = lax.all_to_all(grad_send, "expert", split_axis=0, concat_axis=0, tiled=True)
    grad_hidden = jnp.einsum("scd,df->scf", grad_recv, w_down, preferred_element_type=f32)
    grad_down = jnp.einsum("scd,scf->df", grad_recv, hidden_b, preferred_element_type=f32)
    normal_cdf = 0.5 * (1.0 + jax.scipy.special.erf(up_proj * 2.0 ** (-0.5)))
    normal_pdf = jnp.exp(-0.5 * up_proj * up_proj) * (2.0 * jnp.pi) ** (-0.5)
    grad_up_b = (grad_hidden * (normal_cdf + up_proj * normal_pdf)).astype(bf16)
    grad_in = jnp.einsum("scd,scf->df", received, grad_up_b, preferred_element_type=f32)
    grad_sent = jnp.einsum("scf,df->scd", grad_up_b, w_up, preferred_element_type=f32).astype(bf16)
    grad_back = lax.all_to_all(grad_sent, "expert", split_axis=0, concat_axis=0, tiled=True)
    (grad_logits,) = pull_gate(grad_gate)
    grad_logits_b = grad_logits.astype(bf16)
    grad_router = jnp.einsum("td,te->de", h2_b, grad_logits_b, preferred_element_type=f32)
    grad_h2 = jnp.einsum("te,de->td", grad_logits_b, w_router, preferred_element_type=f32)
    grad_h2 = grad_h2 + grad_back[route_ids, slot_index].astype(f32)
    grad_y1, grad_g2, grad_s2 = pull_two(grad_h2)
    grad_y1 = grad_y1 + grad_out
    grad_a_b = grad_y1.astype(bf16)
    grad_proj = jnp.einsum("td,te->de", mixed_b, grad_a_b, preferred_element_type=f32)
    grad_mixed_b = jnp.einsum("te,de->td", grad_a_b, w_proj, preferred_element_type=f32).astype(
        bf16
    )
    grad_mixed_h = grad_mixed_b.reshape(groups, WINDOW, HEADS, HEAD_DIM)
    probs_f = jnp.exp(window_scores() - log_total)
    grad_probs = jnp.einsum(
        "wqhd,wkhd->whqk", grad_mixed_h, value_heads, preferred_element_type=f32
    )
    grad_value = jnp.einsum(
        "whqk,wqhd->wkhd", probs_f.astype(bf16), grad_mixed_h, preferred_element_type=f32
    )
    grad_scores_b = (
        probs_f * (grad_probs - jnp.sum(grad_probs * probs_f, axis=-1, keepdims=True))
    ).astype(bf16)
    grad_query = jnp.einsum("whqk,wkhd->wqhd", grad_scores_b, key_heads, preferred_element_type=f32)
    grad_key = jnp.einsum("whqk,wqhd->wkhd", grad_scores_b, query_heads, preferred_element_type=f32)
    grad_qkv_f = jnp.concatenate(
        [
            grad_query.reshape(rows_here, width),
            grad_key.reshape(rows_here, width),
            grad_value.reshape(rows_here, width),
        ],
        axis=1,
    )
    grad_qkv_b = (grad_qkv_f * col_scale).astype(bf16)
    grad_qkv = jnp.einsum("td,te->de", h1_b, grad_qkv_b, preferred_element_type=f32)
    grad_h1 = jnp.einsum("te,de->td", grad_qkv_b, w_qkv, preferred_element_type=f32)
    grad_x_ln, grad_g1, grad_s1 = pull_one(grad_h1)
    input_grad = grad_y1 + grad_x_ln
    grad_norm = jnp.stack([grad_g1, grad_s1, grad_g2, grad_s2], axis=1)
    shared = lax.psum((grad_qkv, grad_proj, grad_router, grad_norm), "expert")
    reduced = (
        lax.psum_scatter(shared[0], "dp", scatter_dimension=0, tiled=True),
        lax.psum_scatter(shared[1], "dp", scatter_dimension=0, tiled=True),
        lax.psum_scatter(shared[2], "dp", scatter_dimension=0, tiled=True),
        lax.psum_scatter(shared[3], "dp", scatter_dimension=0, tiled=True),
        lax.psum_scatter(grad_in, "dp", scatter_dimension=0, tiled=True),
        lax.psum_scatter(grad_down, "dp", scatter_dimension=0, tiled=True),
    )
    updated = [
        lamb_direction(weight_now, grad_now, first_now, second_now)
        for weight_now, grad_now, first_now, second_now in zip(
            weights_now, reduced, firsts_now, seconds_now
        )
    ]
    update_sq = jnp.stack([jnp.sum(entry[2] * entry[2]) for entry in updated])
    update_total = lax.psum(update_sq, "dp")
    weight_norm = jnp.sqrt(weight_total)
    update_norm = jnp.sqrt(update_total)
    ratios = weight_norm / (update_norm + 1e-06)
    new_weights = [
        weight_now - RATE * ratios[index] * updated[index][2]
        for index, weight_now in enumerate(weights_now)
    ]
    trust_norms = jnp.stack([weight_norm, update_norm], axis=1)[None]
    return (
        block_output,
        input_grad,
        new_weights[0],
        new_weights[1],
        new_weights[2],
        new_weights[3],
        new_weights[4][None],
        new_weights[5][None],
        updated[0][0],
        updated[1][0],
        updated[2][0],
        updated[3][0],
        updated[4][0][None],
        updated[5][0][None],
        updated[0][1],
        updated[1][1],
        updated[2][1],
        updated[3][1],
        updated[4][1][None],
        updated[5][1][None],
        trust_norms,
    )


def solution(mesh):
    placed = (
        P(("dp", "expert"), None),
        P(("dp", "expert"), None),
        P(("dp", "expert"), None),
        P(("dp", "expert")),
        P(("dp", "expert")),
        P("dp", None),
        P("dp", None),
        P("dp", None),
        P("dp", None),
        P("expert", "dp", None),
        P("expert", "dp", None),
        P("dp", None),
        P("dp", None),
        P("dp", None),
        P("dp", None),
        P("dp", None),
        P("dp", None),
        P("dp", None),
        P("dp", None),
        P("expert", "dp", None),
        P("expert", "dp", None),
        P("expert", "dp", None),
        P("expert", "dp", None),
    )
    return jax.shard_map(
        per_device,
        mesh=mesh,
        in_specs=placed,
        out_specs=(
            P(("dp", "expert"), None),
            P(("dp", "expert"), None),
            P("dp", None),
            P("dp", None),
            P("dp", None),
            P("dp", None),
            P("expert", "dp", None),
            P("expert", "dp", None),
            P("dp", None),
            P("dp", None),
            P("dp", None),
            P("dp", None),
            P("expert", "dp", None),
            P("expert", "dp", None),
            P("dp", None),
            P("dp", None),
            P("dp", None),
            P("dp", None),
            P("expert", "dp", None),
            P("expert", "dp", None),
            P("expert", None, None),
        ),
        check_vma=False,
    )
```

profile of v0, /device:TPU:0, one launch (start us, length us, event | category | flops | bytes accessed | tf_op | source)
XLA Modules:
  0.0 942.9 jit_solution(9083092402659633593)
XLA Ops:
  12.4 22.2 %all-gather = bf16[8,48,4]{1,2,0:T(4,128)(2,1)S(1)} all-gather(bf16[1,48,4]{1,2,0:T(4,128)(2,1)S(1)} %get-tuple-element.77), channel_id=1, replica_groups=mesh['dp'=8,'expert'=4] {'dp'}, dimensions={0}, use_global_device_ids=true | all-gather | bytes 3456 | tf_op jit(solution)/shard_map/all_gather | solution.py:87
  40.6 33.1 %all_gather.20 = bf16[384,384]{1,0:T(8,128)(2,1)} all-gather(bf16[48,384]{1,0:T(8,128)(2,1)S(1)} %convert_element_type.101), channel_id=1, replica_groups=mesh['dp'=8,'expert'=4] {'dp'}, dimensions={0}, use_global_device_ids=true | all-gather | bytes 331776 | tf_op jit(solution)/shard_map/all_gather | solution.py:85
  73.7 32.3 %all_gather.19 = bf16[384,1152]{1,0:T(8,128)(2,1)S(1)} all-gather(bf16[48,1152]{1,0:T(8,128)(2,1)S(1)} %convert_element_type.95), channel_id=1, replica_groups=mesh['dp'=8,'expert'=4] {'dp'}, dimensions={0}, use_global_device_ids=true | all-gather | bytes 995328 | tf_op jit(solution)/shard_map/all_gather | solution.py:84
  146.4 10.8 %scatter_custom_fusion = bf16[2352,384]{1,0:T(8,128)(2,1)} fusion(s32[1176]{0:T(1024)S(1)} %broadcast_select_fusion, bf16[]{:T(256)} %constant.60.clone.1, f32[1176,384]{1,0:T(8,128)S(1)} %get-tuple-element.92, f32[384]{0:T(512)S(1)} %get-tuple-element.36, f32[384]{0:T(512)S(1)} %get-tuple-element.35, f32[1176]{0:T(1024)S(1)} %fusion.86, ...), kind=kCustom, calls=%fused_computation.103 | custom fusion | flops 2257920 | bytes 3633154
  169.5 22.0 %all-to-all-done = bf16[4,588,384]{2,1,0:T(8,128)(2,1)} async-done(((bf16[4,588,384]{2,1,0:T(8,128)(2,1)}), bf16[4,588,384]{2,1,0:T(8,128)(2,1)}, u32[]{:S(2)}, u32[]{:S(2)}) %all-to-all-start) | async-done | bytes 1806368 | tf_op jit(solution)/shard_map/all_to_all | solution.py:130
  191.5 9.5 %fusion.19 = (u8[588,1536]{1,0:T(8,128)(4,1)S(1)}, u8[588,1536]{1,0:T(8,128)(4,1)S(1)}, f32[4,588,1536]{2,1,0:T(8,128)S(1)}) fusion(bf16[4,588,384]{2,1,0:T(8,128)(2,1)} %all-to-all-done, bf16[384,1536]{1,0:T(8,128)(2,1)} %all-gather.5.cloned.1.call-done), kind=kOutput, calls=%fused_computation.44 | convolution fusion | flops 2819690496 | bytes 19243008 | tf_op jit(solution)/shard_map/scd,df->scf/dot_general | solution.py:131
  206.3 34.0 %fusion.2 = bf16[4,588,1536]{2,1,0:T(8,128)(2,1)} fusion(f32[4,588,1536]{2,1,0:T(8,128)S(1)} %get-tuple-element.95, u8[588,1536]{1,0:T(8,128)(4,1)S(1)} %get-tuple-element.22, u8[588,1536]{1,0:T(8,128)(4,1)S(1)} %get-tuple-element.21), kind=kLoop, calls=%fused_computation.8 | loop fusion | flops 252887040 | bytes 23482368 | tf_op jit(solution)/shard_map/convert_element_type | solution.py:132
  240.3 8.6 convolution_convert_fusion.2
  254.0 16.9 %all-gather.1 = bf16[8,48,4]{1,2,0:T(4,128)(2,1)S(1)} all-gather(bf16[1,48,4]{1,2,0:T(4,128)(2,1)S(1)} %get-tuple-element.79), channel_id=1, replica_groups=mesh['dp'=8,'expert'=4] {'dp'}, dimensions={0}, use_global_device_ids=true | all-gather | bytes 3456 | tf_op jit(solution)/shard_map/all_gather | solution.py:86
  279.6 22.8 %gather_fusion = bf16[1176,384]{1,0:T(8,128)(2,1)} fusion(bf16[4,588,384]{2,0,1:T(4,128)(2,1)} %copy.130, s32[1176]{0:T(1024)S(1)} %get-tuple-element.63), kind=kCustom, calls=%fused_computation | custom fusion | bytes 1815744 | tf_op jit(solution)/shard_map/gather | solution.py:136
  304.8 10.9 %scatter_custom_fusion.1 = bf16[2352,384]{1,0:T(8,128)(2,1)} fusion(s32[1176]{0:T(1024)S(1)} %broadcast_select_fusion, f32[1176,384]{1,0:T(8,128)} %param.24, bf16[]{:T(256)} %constant.60.clone.1, f32[1176]{0:T(1024)S(1)} %convert_element_type.110, f32[1176]{0:T(1024)S(1)} %get-tuple-element.34), kind=kCustom, calls=%fused_computation.101 | custom fusion | flops 1354752 | bytes 3629058
  321.5 25.3 %all_to_all.20 = bf16[4,588,384]{2,1,0:T(8,128)(2,1)S(1)} all-to-all(bf16[4,588,384]{2,1,0:T(8,128)(2,1)S(1)} %bitcast.190), channel_id=1, replica_groups=mesh['dp'=8,'expert'=4] {'expert'}, dimensions={0} | all-to-all | bytes 3612672 | tf_op jit(solution)/shard_map/all_to_all | solution.py:145
  346.8 11.6 %fusion.8 = bf16[4,588,1536]{2,1,0:T(8,128)(2,1)S(1)} fusion(f32[4,588,1536]{2,1,0:T(8,128)} %copy-done.6, bf16[4,588,384]{2,1,0:T(8,128)(2,1)S(1)} %all_to_all.20, bf16[384,1536]{1,0:T(8,128)(2,1)S(1)} %copy-done.48), kind=kOutput, calls=%fused_computation.14 | convolution fusion | flops 2810658816 | bytes 24662016 | tf_op jit(solution)/shard_map/scd,df->scf/dot_general | solution.py:146
  373.4 20.3 %all-to-all-done.3 = bf16[4,588,384]{2,1,0:T(8,128)(2,1)} async-done(((bf16[4,588,384]{2,1,0:T(8,128)(2,1)}), bf16[4,588,384]{2,1,0:T(8,128)(2,1)}, u32[]{:S(2)}, u32[]{:S(2)}) %all-to-all-start.3) | async-done | bytes 1806368 | tf_op jit(solution)/shard_map/all_to_all | solution.py:153
  397.0 23.1 %gather_fusion.1 = bf16[1176,384]{1,0:T(8,128)(2,1)} fusion(bf16[4,588,384]{2,0,1:T(4,128)(2,1)} %copy.132, s32[1176]{0:T(1024)S(1)} %get-tuple-element.63), kind=kCustom, calls=%fused_computation.1 | custom fusion | bytes 1815744 | tf_op jit(solution)/shard_map/gather | solution.py:158
  434.8 8.6 convolution_bitcast_fusion.2
  443.3 9.0 multiply_reduce_fusion
  543.9 31.0 %reduce-scatter.21.cloned.1.call-done = f32[48,4]{1,0:T(8,128)} async-done(((f32[384,4]{1,0:T(8,128)}), f32[48,4]{1,0:T(8,128)}) %reduce-scatter.21.cloned.1.call-update) | async-done | bytes 784
  582.7 63.6 %reduce-scatter.11.cloned.1.call-done = f32[48,1536]{1,0:T(8,128)} async-done(((f32[384,1536]{1,0:T(8,128)}), f32[48,1536]{1,0:T(8,128)}) %reduce-scatter.11.cloned.1.call-update) | async-done | bytes 294928 | tf_op jit(solution)/shard_map/reduce_scatter | solution.py:199
  649.2 61.4 %reduce-scatter.17.cloned.1.call-done = f32[48,384]{1,0:T(8,128)} async-done(((f32[384,384]{1,0:T(8,128)}), f32[48,384]{1,0:T(8,128)}) %reduce-scatter.17.cloned.1.call-update) | async-done | bytes 73744 | tf_op jit(solution)/shard_map/reduce_scatter | solution.py:196
  710.6 69.1 %reduce-scatter.15.cloned.1.call-done = f32[48,1152]{1,0:T(8,128)} async-done(((f32[384,1152]{1,0:T(8,128)}), f32[48,1152]{1,0:T(8,128)}) %reduce-scatter.15.cloned.1.call-update) | async-done | bytes 221200 | tf_op jit(solution)/shard_map/reduce_scatter | solution.py:195
  779.8 71.8 %reduce-scatter.13.cloned.1.call-done = f32[48,1536]{1,0:T(8,128)} async-done(((f32[384,1536]{1,0:T(8,128)}), f32[48,1536]{1,0:T(8,128)}) %reduce-scatter.13.cloned.1.call-update) | async-done | bytes 294928 | tf_op jit(solution)/shard_map/reduce_scatter | solution.py:200
  854.4 31.1 %all-reduce.6.cloned.1.call-done = (f32[48,1152]{1,0:T(8,128)}, f32[48,384]{1,0:T(8,128)}) async-done(((f32[48,1152]{1,0:T(8,128)}, f32[48,384]{1,0:T(8,128)}), (f32[48,1152]{1,0:T(8,128)}, f32[48,384]{1,0:T(8,128)})) %all-reduce.6.cloned.1.call-update) | async-done | bytes 294928 | tf_op jit(solution)/shard_map/psum | solution.py:193
  901.7 21.3 %all-reduce.1 = (f32[6]{0:T(128)S(1)}, f32[6]{0:T(128)S(1)}) all-reduce(f32[6]{0:T(128)S(1)} %stack.84, f32[6]{0:T(128)S(1)} %stack.72), channel_id=1, replica_groups=mesh['dp'=8,'expert'=4] {'dp'}, use_global_device_ids=true, to_apply=%region_48.49 | all-reduce | flops 12 | bytes 96 | tf_op jit(solution)/shard_map/psum | solution.py:209
  (260 shorter events, 253.7 us)
Async XLA Ops:
  7.2 99.7 %copy-start.49 = (f32[1152]{0:T(1024)S(1)}, f32[1152]{0:T(1024)}, u32[]{:S(2)}) copy-start(f32[1152]{0:T(1024)} %constant.56.clone.1) | copy-start | bytes 13828
  7.2 99.7 %copy-start.1 = (bf16[1176,384]{1,0:T(8,128)(2,1)S(1)}, bf16[1176,384]{1,0:T(8,128)(2,1)}, u32[]{:S(2)}) copy-start(bf16[1176,384]{1,0:T(8,128)(2,1)} %param.23) | copy-start | bytes 2709508
  7.3 184.3 %all-gather.5.cloned.1.call-start = ((), (), s32[]{:S(2)}) async-start(), calls=%async_computation.10 | async-start | bytes 1327104 | tf_op jit(solution)/shard_map/all_gather | solution.py:88
  35.5 73.3 %copy-start.33 = (f32[384]{0:T(512)}, f32[384]{0:T(512)S(1)}, u32[]{:S(2)}) copy-start(f32[384]{0:T(512)S(1)} %get-tuple-element.38) | copy-start | bytes 4612
  35.5 73.3 %copy-start.39 = (f32[384]{0:T(512)}, f32[384]{0:T(512)S(1)}, u32[]{:S(2)}) copy-start(f32[384]{0:T(512)S(1)} %get-tuple-element.37) | copy-start | bytes 4612
  35.5 110.8 %copy-start.28 = (f32[384]{0:T(512)}, f32[384]{0:T(512)S(1)}, u32[]{:S(2)}) copy-start(f32[384]{0:T(512)S(1)} %get-tuple-element.36) | copy-start | bytes 4612
  38.6 70.2 %copy-start.23 = (f32[1176]{0:T(1024)}, f32[1176]{0:T(1024)S(1)}, u32[]{:S(2)}) copy-start(f32[1176]{0:T(1024)S(1)} %fusion.45) | copy-start | bytes 14116
  164.2 27.3 %all-to-all-start = ((bf16[4,588,384]{2,1,0:T(8,128)(2,1)}), bf16[4,588,384]{2,1,0:T(8,128)(2,1)}, u32[]{:S(2)}, u32[]{:S(2)}) async-start(bf16[4,588,384]{2,1,0:T(8,128)(2,1)} %bitcast.189), calls=%async_computation | async-start | bytes 3637248 | tf_op jit(solution)/shard_map/all_to_all | solution.py:130
  168.8 71.5 %all-gather.7.cloned.1.call-start = ((), (), s32[]{:S(2)}) async-start(), calls=%async_computation.11 | async-start | bytes 1327104 | tf_op jit(solution)/shard_map/all_gather | solution.py:89
  248.9 27.3 %all-to-all-start.1 = ((bf16[4,588,384]{2,1,0:T(8,128)(2,1)}), bf16[4,588,384]{2,1,0:T(8,128)(2,1)}, u32[]{:S(2)}, u32[]{:S(2)}) async-start(bf16[4,588,384]{2,1,0:T(8,128)(2,1)} %convolution_convert_fusion.2), calls=%async_computation.1 | async-start | bytes 3637248 | tf_op jit(solution)/shard_map/all_to_all | solution.py:135
  366.4 27.2 %all-to-all-start.3 = ((bf16[4,588,384]{2,1,0:T(8,128)(2,1)}), bf16[4,588,384]{2,1,0:T(8,128)(2,1)}, u32[]{:S(2)}, u32[]{:S(2)}) async-start(bf16[4,588,384]{2,1,0:T(8,128)(2,1)} %convolution_convert_fusion.1), calls=%async_computation.3 | async-start | bytes 3637248 | tf_op jit(solution)/shard_map/all_to_all | solution.py:153
  370.9 172.1 %reduce-scatter.19.cloned.1.call-start = ((), (), s32[]{:S(2)}) async-start(), calls=%async_computation.16 | async-start | bytes 221184
  373.3 201.6 %reduce-scatter.21.cloned.1.call-start = ((), (), s32[]{:S(2)}) async-start(), calls=%async_computation.17 | async-start | bytes 221184
  517.2 129.1 %reduce-scatter.11.cloned.1.call-start = ((), (), s32[]{:S(2)}) async-start(), calls=%async_computation.12 | async-start | bytes 2654208 | tf_op jit(solution)/shard_map/reduce_scatter | solution.py:199
  525.7 184.9 %reduce-scatter.17.cloned.1.call-start = ((), (), s32[]{:S(2)}) async-start(), calls=%async_computation.15 | async-start | bytes 663552 | tf_op jit(solution)/shard_map/reduce_scatter | solution.py:196
  528.5 251.3 %reduce-scatter.15.cloned.1.call-start = ((), (), s32[]{:S(2)}) async-start(), calls=%async_computation.14 | async-start | bytes 1990656 | tf_op jit(solution)/shard_map/reduce_scatter | solution.py:195
  534.2 317.4 %reduce-scatter.13.cloned.1.call-start = ((), (), s32[]{:S(2)}) async-start(), calls=%async_computation.13 | async-start | bytes 2654208 | tf_op jit(solution)/shard_map/reduce_scatter | solution.py:200
  542.8 38.6 %copy-start.43 = (f32[48,4]{0,1:T(4,128)S(1)}, f32[48,4]{0,1:T(4,128)}, u32[]{:S(2)}) copy-start(f32[48,4]{0,1:T(4,128)} %param.39) | copy-start | bytes 2308
  542.8 38.5 %copy-start.44 = (f32[48,4]{0,1:T(4,128)S(1)}, f32[48,4]{0,1:T(4,128)}, u32[]{:S(2)}) copy-start(f32[48,4]{0,1:T(4,128)} %param.38) | copy-start | bytes 2308
  542.8 103.5 %copy-start.17 = (f32[1,48,1536]{2,1,0:T(8,128)S(1)}, f32[1,48,1536]{2,1,0:T(8,128)}, u32[]{:S(2)}) copy-start(f32[1,48,1536]{2,1,0:T(8,128)} %param.32) | copy-start | bytes 884740
  542.9 308.7 %copy-start.16 = (f32[1,48,1536]{2,1,0:T(8,128)S(1)}, f32[1,48,1536]{2,1,0:T(8,128)}, u32[]{:S(2)}) copy-start(f32[1,48,1536]{2,1,0:T(8,128)} %param.33) | copy-start | bytes 884740
  542.9 342.6 %copy-start.21 = (f32[48,384]{1,0:T(8,128)S(1)}, f32[48,384]{1,0:T(8,128)}, u32[]{:S(2)}) copy-start(f32[48,384]{1,0:T(8,128)} %param.29) | copy-start | bytes 221188
  542.9 342.6 %all-reduce.6.cloned.1.call-start = ((), (), s32[]{:S(2)}) async-start(), calls=%async_computation.18 | async-start | bytes 589824 | tf_op jit(solution)/shard_map/psum | solution.py:193
  887.7 44.9 %copy-start.22 = (f32[48,384]{1,0:T(8,128)}, f32[48,384]{1,0:T(8,128)S(1)}, u32[]{:S(2)}) copy-start(f32[48,384]{1,0:T(8,128)S(1)} %get-tuple-element.57) | copy-start | bytes 221188
  (43 other events, 501.2 us)
Sparse Core Ops, SparseCore 0:
  10.9 45.0 all-gather.4
  172.4 38.9 all-gather.6
  375.5 58.9 reduce-scatter.18
  517.3 57.5 reduce-scatter.20
  578.2 68.0 reduce-scatter.10
  649.5 61.1 reduce-scatter.16
  714.5 65.2 reduce-scatter.14
  783.3 68.2 reduce-scatter.12
  854.0 31.4 all-reduce.5
where the time goes:
time: 951 us; the launch traced here: 943 us
  waiting for transfers between devices  374 us (39%)
  local copies, waits for them, and re-layouts  166 us (17%)
  blocking collectives  157 us (17%)
  matrix products  109 us (11%)
  other arithmetic  105 us (11%)
  between operations  18.8 us (2%)
  starting transfers between devices  14.1 us (1%)
    reduce_scatter x1, waiting for transfers between devices, per_device(): lax.psum_scatter(grad_down, 'dp', scatter_dimension=0, tiled=True)  71.8 us
    reduce_scatter x1, waiting for transfers between devices, per_device(): lax.psum_scatter(shared[0], 'dp', scatter_dimension=0, tiled=True)  69.1 us
    reduce_scatter x1, waiting for transfers between devices, per_device(): lax.psum_scatter(grad_in, 'dp', scatter_dimension=0, tiled=True)  63.6 us
    reduce_scatter x1, waiting for transfers between devices, per_device(): lax.psum_scatter(shared[1], 'dp', scatter_dimension=0, tiled=True)  61.4 us
    convert_element_type x1, other arithmetic, per_device(): hidden_b = jax.nn.gelu(up_proj, approximate=False).astype(bf16)  34 us
    all_gather x1, blocking collectives, per_device(): lax.all_gather(proj_weight.astype(bf16), 'dp', axis=0, tiled=True)  33.1 us
    all_gather x1, blocking collectives, per_device(): lax.all_gather(qkv_weight.astype(bf16), 'dp', axis=0, tiled=True)  32.3 us
    unnamed x11, waiting for transfers between devices  31.1 us
  transfers between devices with their start and end apart: 12, of which 9 were waited for; matrix products, arithmetic and copies ran while one was open for 29% of the time, Pallas kernels for 0%

commit v1 on v0

v1 whole, which is shorter than its diff:
```python
import functools

import jax
import jax.numpy as jnp
from jax import lax
from jax.experimental import pallas as pl
from jax.experimental.pallas import tpu as pltpu
from jax.sharding import PartitionSpec as P

HEADS = 12
HEAD_DIM = 32
WINDOW = 49
PAD = 64
STEP = 5
TILE = 128
NORM_EPS = 1e-05
MASKED = -1e30
BETA_ONE = 0.9
BETA_TWO = 0.999
ADAM_EPS = 1e-06
DECAY = 0.01
RATE = 0.3
VMEM_BYTES = 60 * 1024 * 1024

f32 = jnp.float32
bf16 = jnp.bfloat16


def dot_nn(a, b):
    return lax.dot_general(a, b, (((1,), (0,)), ((), ())), preferred_element_type=f32)


def dot_nt(a, b):
    return lax.dot_general(a, b, (((1,), (1,)), ((), ())), preferred_element_type=f32)


def dot_tn(a, b):
    return lax.dot_general(a, b, (((0,), (0,)), ((), ())), preferred_element_type=f32)


def norm_stats(v):
    width = v.shape[-1]
    mean = jnp.sum(v, axis=-1, keepdims=True) * (1.0 / width)
    centred = v - mean
    var = jnp.sum(centred * centred, axis=-1, keepdims=True) * (1.0 / width)
    rstd = lax.rsqrt(var + NORM_EPS)
    return centred * rstd, rstd


def norm_back(d, normed, rstd, gain):
    width = d.shape[-1]
    dn = d * gain
    m1 = jnp.sum(dn, axis=-1, keepdims=True) * (1.0 / width)
    m2 = jnp.sum(dn * normed, axis=-1, keepdims=True) * (1.0 / width)
    return rstd * (dn - m1 - normed * m2)


def head_masks():
    lane = lax.broadcasted_iota(jnp.int32, (PAD, 128), 1)
    return [lane // HEAD_DIM == h for h in range(4)]


def spread_heads(v, masks):
    zero = jnp.zeros_like(v)
    return jnp.concatenate([jnp.where(m, v, zero) for m in masks], axis=0)


def gather_heads(v, masks):
    out = jnp.where(masks[0], v[0:PAD], 0.0)
    for h in range(1, 4):
        out = jnp.where(masks[h], v[h * PAD : (h + 1) * PAD], out)
    return out


def weight_part(w_ref, part):
    width = w_ref.shape[1]
    at = (part % 2) * width
    return w_ref[part // 2, :, at : at + width]


def load_windows(src_ref, dst_ref, per_group):
    width = dst_ref.shape[-1]
    for k in range(per_group):
        dst_ref[k * PAD : k * PAD + WINDOW, :] = src_ref[0, k * WINDOW : (k + 1) * WINDOW, :]
        dst_ref[k * PAD + WINDOW : (k + 1) * PAD, :] = jnp.zeros((PAD - WINDOW, width), f32)


def forward_kernel(
    experts,
    slots,
    per_group,
    x_ref,
    g_ref,
    meta_ref,
    row_ref,
    w_ref,
    hz_ref,
    y1_ref,
    pr_ref,
    attn_ref,
    qkv_ref,
    p_ref,
    key_ref,
    count_ref,
    xp,
    gp,
    carry,
):
    step = pl.program_id(0)
    rows = per_group * PAD
    width = x_ref.shape[-1]
    groups = width // 128
    load_windows(x_ref, xp, per_group)
    load_windows(g_ref, gp, per_group)

    @pl.when(step == 0)
    def _():
        carry[...] = jnp.zeros_like(carry)

    small = w_ref[0, :, 2 * width :]
    small_t = jnp.transpose(small.astype(f32))
    a1, b1, a2, b2 = (small_t[experts + i : experts + i + 1, :] for i in range(4))
    normed, _ = norm_stats(xp[...])
    h1 = (normed * a1 + b1).astype(bf16)
    for part in range(3):
        raw = dot_nn(h1, weight_part(w_ref, part))
        if part == 0:
            raw = raw * (HEAD_DIM**-0.5)
        qkv_ref[:, :, part * width : (part + 1) * width] = raw.astype(bf16).reshape(per_group, PAD, width)

    meta = meta_ref[...]
    valid = meta[:, 2:3].astype(f32)
    masks = head_masks()
    key_i = lax.broadcasted_iota(jnp.int32, (PAD, 4 * PAD), 0)
    lane_i = lax.broadcasted_iota(jnp.int32, (PAD, 4 * PAD), 1)
    diagonal = key_i == lax.rem(lane_i, PAD)

    def window(w, _):
        code = meta_ref[pl.ds(pl.multiple_of(w * PAD, PAD), PAD), 0:1]
        allowed = (code == row_ref[w]) | diagonal
        for lg in range(groups):
            q = qkv_ref[w, :, lg * 128 : (lg + 1) * 128]
            k = qkv_ref[w, :, width + lg * 128 : width + (lg + 1) * 128]
            v = qkv_ref[w, :, 2 * width + lg * 128 : 2 * width + (lg + 1) * 128]
            s = dot_nt(k, spread_heads(q, masks))
            s = jnp.where(allowed, s, MASKED)
            e = jnp.exp(s - jnp.max(s, axis=0, keepdims=True))
            p = e * (1.0 / jnp.sum(e, axis=0, keepdims=True))
            p_ref[w, lg] = p
            o = dot_tn(p.astype(bf16), v)
            attn_ref[pl.ds(pl.multiple_of(w * PAD, PAD), PAD), lg * 128 : (lg + 1) * 128] = gather_heads(
                o, masks
            ).astype(bf16)
        return 0

    lax.fori_loop(0, per_group, window, 0)

    y1 = xp[...] + dot_nn(attn_ref[...], weight_part(w_ref, 3))
    y1_ref[...] = y1
    normed2, _ = norm_stats(y1)
    h2 = (normed2 * a2 + b2).astype(bf16)
    lane = lax.broadcasted_iota(jnp.int32, (rows, 128), 1)
    logits = jnp.where(lane < experts, dot_nn(h2, small), MASKED)
    e = jnp.exp(logits - jnp.max(logits, axis=-1, keepdims=True))
    pr = e * (1.0 / jnp.sum(e, axis=-1, keepdims=True))
    pr_ref[...] = pr
    chosen = lane == meta[:, 1:2]
    gate = jnp.sum(jnp.where(chosen, pr, 0.0), axis=-1, keepdims=True)
    gv = gp[...] * valid
    hz_ref[:, 0:width] = h2
    hz_ref[:, width : 2 * width] = (gate * gv).astype(bf16)

    onehot = jnp.where(chosen, 1.0, 0.0)
    before = lax.broadcasted_iota(jnp.int32, (rows, rows), 1) < lax.broadcasted_iota(jnp.int32, (rows, rows), 0)
    ranks = dot_nn(jnp.where(before, 1.0, 0.0).astype(bf16), onehot.astype(bf16)) + carry[0:1, :]
    slot = jnp.sum(ranks * onehot, axis=-1, keepdims=True)
    seen = jnp.sum(onehot, axis=-1, keepdims=True)
    key = (meta[:, 1:2].astype(f32) * slots + slot) * seen + (seen - 1.0)
    key_ref[...] = jnp.broadcast_to(key, (rows, 128)).astype(jnp.int32)
    carry[...] = carry[...] + jnp.sum(onehot, axis=0, keepdims=True)
    count_ref[...] = carry[...].astype(jnp.int32)


def expert_kernel(slots, counts_ref, hz_ref, keyrow_ref, keycol_ref, we_ref, grad_ref, tok_ref, acc):
    e = pl.program_id(0)
    width = hz_ref.shape[-1] // 2
    total = hz_ref.shape[0]

    @pl.when(e == 0)
    def _():
        tok_ref[...] = jnp.zeros_like(tok_ref)

    acc[...] = jnp.zeros_like(acc)
    used = counts_ref[e]

    def tile(t, _):
        base = e * slots + t * TILE
        pick = keyrow_ref[...] == base + lax.broadcasted_iota(jnp.int32, (TILE, total), 0)
        both = dot_nn(jnp.where(pick, 1.0, 0.0).astype(bf16), hz_ref[...]).astype(bf16)
        rows, dz = both[:, 0:width], both[:, width : 2 * width]
        up = dot_nn(rows, we_ref[0, 0])
        cdf = 0.5 * (1.0 + lax.erf(up * 2.0**-0.5))
        hidden = (up * cdf).astype(bf16)
        slope = cdf + up * (jnp.exp(-0.5 * up * up) * (2.0 * jnp.pi) ** -0.5)
        ret = dot_nt(hidden, we_ref[0, 1]).astype(bf16)
        dup = (dot_nn(dz, we_ref[0, 1]) * slope).astype(bf16)
        back = dot_nt(dup, we_ref[0, 0]).astype(bf16)
        acc[1] += dot_tn(dz, hidden)
        acc[0] += dot_tn(rows, dup)
        put = keycol_ref[...] == base + lax.broadcasted_iota(jnp.int32, (total, TILE), 1)
        tok_ref[...] += dot_nn(jnp.where(put, 1.0, 0.0).astype(bf16), jnp.concatenate([ret, back], axis=1))
        return 0

    lax.fori_loop(0, (used + TILE - 1) // TILE, tile, 0)
    grad_ref[0] = acc[...].astype(bf16)


def backward_kernel(
    experts,
    per_group,
    x_ref,
    g_ref,
    meta_ref,
    w_ref,
    tok_ref,
    hz_ref,
    y1_ref,
    pr_ref,
    attn_ref,
    qkv_ref,
    p_ref,
    out_ref,
    dx_ref,
    shared_ref,
    small_ref,
    xp,
    gp,
    outp,
    dattn,
    dqkv,
    acc,
    acc_s,
):
    step = pl.program_id(0)
    rows = per_group * PAD
    width = x_ref.shape[-1]
    groups = width // 128
    scale = HEAD_DIM**-0.5

    @pl.when(step == 0)
    def _():
        acc[...] = jnp.zeros_like(acc)
        acc_s[...] = jnp.zeros_like(acc_s)

    load_windows(x_ref, xp, per_group)
    load_windows(g_ref, gp, per_group)
    meta = meta_ref[...]
    valid = meta[:, 2:3].astype(f32)
    small = w_ref[0, :, 2 * width :]
    small_t = jnp.transpose(small.astype(f32))
    a1, b1, a2, b2 = (small_t[experts + i : experts + i + 1, :] for i in range(4))
    y1 = y1_ref[...]
    gv = gp[...] * valid
    z = tok_ref[:, 0:width]
    lane = lax.broadcasted_iota(jnp.int32, (rows, 128), 1)
    chosen = lane == meta[:, 1:2]
    pr = pr_ref[...]
    gate = jnp.sum(jnp.where(chosen, pr, 0.0), axis=-1, keepdims=True)
    outp[...] = y1 + gate * z
    for k in range(per_group):
        out_ref[0, k * WINDOW : (k + 1) * WINDOW, :] = outp[k * PAD : k * PAD + WINDOW, :]
    dgate = jnp.sum(gv * z, axis=-1, keepdims=True)
    kept = jnp.where(lane < experts, jnp.where(chosen, 1.0, 0.0) - pr, 0.0)
    dlogits = (dgate * gate * kept).astype(bf16)
    h2 = hz_ref[:, 0:width]
    acc_s[0:128] += dot_tn(dlogits, h2)
    dh2 = dot_nt(dlogits, small) + tok_ref[:, width : 2 * width]
    n2, r2 = norm_stats(y1)
    acc_s[130:131] += jnp.sum(dh2 * n2, axis=0, keepdims=True)
    acc_s[131:132] += jnp.sum(dh2, axis=0, keepdims=True)
    dy1 = gv + norm_back(dh2, n2, r2, a2)
    gp[...] = dy1
    da = dy1.astype(bf16)
    acc[3] += dot_tn(attn_ref[...], da)
    dattn[...] = dot_nt(da, weight_part(w_ref, 3)).astype(bf16)

    masks = head_masks()

    def window(w, _):
        at = pl.ds(pl.multiple_of(w * PAD, PAD), PAD)
        for lg in range(groups):
            cols = slice(lg * 128, (lg + 1) * 128)
            q = qkv_ref[w, :, lg * 128 : (lg + 1) * 128]
            k = qkv_ref[w, :, width + lg * 128 : width + (lg + 1) * 128]
            v = qkv_ref[w, :, 2 * width + lg * 128 : 2 * width + (lg + 1) * 128]
            d_all = spread_heads(dattn[at, cols], masks)
            q_all = spread_heads(q, masks)
            p = p_ref[w, lg]
            dp = dot_nt(v, d_all)
            ds = (p * (dp - jnp.sum(dp * p, axis=0, keepdims=True))).astype(bf16)
            dv = dot_nn(p.astype(bf16), d_all)
            dk = dot_nn(ds, q_all)
            dq = gather_heads(dot_tn(ds, k), masks) * scale
            dqkv[0, at, cols] = dq.astype(bf16)
            dqkv[1, at, cols] = dk.astype(bf16)
            dqkv[2, at, cols] = dv.astype(bf16)
        return 0

    lax.fori_loop(0, per_group, window, 0)

    n1, r1 = norm_stats(xp[...])
    h1 = (n1 * a1 + b1).astype(bf16)
    dh1 = jnp.zeros((rows, width), f32)
    for part in range(3):
        dpart = dqkv[part]
        acc[part] += dot_tn(h1, dpart)
        dh1 = dh1 + dot_nt(dpart, weight_part(w_ref, part))
    acc_s[128:129] += jnp.sum(dh1 * n1, axis=0, keepdims=True)
    acc_s[129:130] += jnp.sum(dh1, axis=0, keepdims=True)
    outp[...] = gp[...] + norm_back(dh1, n1, r1, a1)
    for k in range(per_group):
        dx_ref[0, k * WINDOW : (k + 1) * WINDOW, :] = outp[k * PAD : k * PAD + WINDOW, :]

    @pl.when(step == pl.num_programs(0) - 1)
    def _():
        for part in range(4):
            shared_ref[part] = acc[part].astype(bf16)
        small_ref[0:8] = acc_s[0:8]
        small_ref[8:16] = acc_s[128:136]


def place():
    dp, ex = lax.axis_index("dp"), lax.axis_index("expert")
    return lax.div(dp, 2), lax.rem(dp, 2), lax.div(ex, 2), lax.rem(ex, 2)


def at(z, x, y, c):
    return (z * 2 + x, y * 2 + c)


def push(src, dst, send_sem, recv_sem, device):
    copy = pltpu.make_async_remote_copy(
        src_ref=src,
        dst_ref=dst,
        send_sem=send_sem,
        recv_sem=recv_sem,
        device_id=device,
        device_id_type=pl.DeviceIdType.MESH,
    )
    return copy


def meet(z, x, y, c, depth):
    barrier = pltpu.get_barrier_semaphore()

    def greet(device):
        pl.semaphore_signal(barrier, inc=1, device_id=device, device_id_type=pl.DeviceIdType.MESH)

    greet(at(z, x, y, 1 - c))
    greet(at(z, 1 - x, y, c))
    greet(at(z, x, 1 - y, c))
    for other in range(depth):
        @pl.when(z != other)
        def _():
            greet(at(other, x, y, c))

    pl.semaphore_wait(barrier, 3 + depth - 1)


class Gather:
    def __init__(self, depth, ex_ref, we_ref, sems):
        self.depth = depth
        self.ex, self.we = ex_ref, we_ref
        (self.loc, self.zs, self.zr, self.xs, self.xr, self.ys, self.yr, self.cs, self.cr) = sems
        self.z, self.x, self.y, self.c = place()

    @staticmethod
    def semaphores(depth):
        dma = pltpu.SemaphoreType.DMA
        return [
            dma((1,)),
            dma((2, depth)),
            dma((depth,)),
            dma((3, depth)),
            dma((3, depth)),
            dma((3, depth)),
            dma((3, depth)),
            dma((7, depth)),
            dma((7, depth)),
        ]

    def e(self, y, c):
        return y * 2 + c

    def block(self, y, c, s, z, x):
        return self.we.at[y * 2 + c, s, z * 2 + x]

    def pair(self, y, c, z, x):
        return self.we.at[y * 2 + c, :, z * 2 + x]

    def z_copy(self, up, zo, first=False):
        mine = self.ex if first else self.pair(self.y, self.c, zo, self.x)
        target = self.z + 1 if up else self.z - 1
        return push(
            mine,
            self.pair(self.y, self.c, zo, self.x),
            self.zs.at[0 if up else 1, zo],
            self.zr.at[zo],
            at(target, self.x, self.y, self.c),
        )

    def x_copy(self, kind, zo, y, first=False):
        s = 0 if kind == 0 else 1
        dst = self.block(y, self.c, s, zo, self.x)
        src = self.ex.at[s] if first else dst
        return push(src, dst, self.xs.at[kind, zo], self.xr.at[kind, zo], at(self.z, 1 - self.x, self.y, self.c))

    def y_copy(self, kind, zo, x, first=False):
        s = 1 if kind == 0 else 0
        dst = self.block(self.y, self.c, s, zo, x)
        src = self.ex.at[s] if first else dst
        return push(src, dst, self.ys.at[kind, zo], self.yr.at[kind, zo], at(self.z, self.x, 1 - self.y, self.c))

    def c_copy(self, kind, zo, c, first=False):
        x, y = self.x, self.y
        if kind == 0:
            dst = self.pair(y, c, zo, x)
        elif kind == 1:
            dst = self.block(y, c, 0, zo, 1 - x)
        elif kind == 2:
            dst = self.block(1 - y, c, 1, zo, x)
        elif kind in (3, 4):
            dst = self.block(1 - y, c, 0, zo, x if kind == 3 else 1 - x)
        else:
            dst = self.block(y if kind == 5 else 1 - y, c, 1, zo, 1 - x)
        src = self.ex if first else dst
        return push(src, dst, self.cs.at[kind, zo], self.cr.at[kind, zo], at(self.z, x, y, 1 - self.c))

    def spread(self, zo, first=False):
        self.x_copy(0, zo, self.y, first).start()
        self.y_copy(0, zo, self.x, first).start()
        self.y_copy(1, zo, self.x, first).start()
        self.x_copy(1, zo, self.y, first).start()
        self.c_copy(0, zo, self.c, first).start()

    def begin(self):
        z = self.z
        self.local = pltpu.make_async_copy(self.ex, self.pair(self.y, self.c, z, self.x), self.loc.at[0])
        self.local.start()

        @pl.when(z < self.depth - 1)
        def _():
            self.z_copy(True, z, True).start()

        @pl.when(z > 0)
        def _():
            self.z_copy(False, z, True).start()

        self.spread(z, True)

    def line(self, s):
        z = self.z

        @pl.when(z - s >= 0)
        def _():
            self.z_copy(True, z - s).wait_recv()

            @pl.when(z < self.depth - 1)
            def _():
                self.z_copy(True, z - s).start()

            self.spread(z - s)

        @pl.when(z + s < self.depth)
        def _():
            self.z_copy(True, z + s).wait_recv()

            @pl.when(z > 0)
            def _():
                self.z_copy(False, z + s).start()

            self.spread(z + s)

    def turn(self, zo):
        self.x_copy(0, zo, self.y).wait_recv()
        self.y_copy(2, zo, 1 - self.x).start()
        self.c_copy(1, zo, self.c).start()
        self.y_copy(0, zo, self.x).wait_recv()
        self.x_copy(2, zo, 1 - self.y).start()
        self.c_copy(2, zo, self.c).start()

    def turns(self, s):
        z = self.z
        if s == 0:
            self.turn(z)
            return

        @pl.when(z - s >= 0)
        def _():
            self.turn(z - s)

        @pl.when(z + s < self.depth)
        def _():
            self.turn(z + s)

    def last(self):
        for zo in range(self.depth):
            for kind, ck in ((1, 3), (2, 4)):
                self.y_copy(kind, zo, self.x).wait_recv()
                self.c_copy(ck, zo, self.c).start()
            for kind, ck in ((1, 5), (2, 6)):
                self.x_copy(kind, zo, self.y).wait_recv()
                self.c_copy(ck, zo, self.c).start()

    def finish(self):
        z = self.z
        for zo in range(self.depth):
            for kind in range(7):
                self.c_copy(kind, zo, 1 - self.c).wait_recv()
        self.local.wait()
        for zo in range(self.depth):
            @pl.when((z < self.depth - 1) & (zo <= z))
            def _():
                self.z_copy(True, zo).wait_send()

            @pl.when((z > 0) & (zo >= z))
            def _():
                self.z_copy(False, zo).wait_send()

            for kind in range(3):
                self.x_copy(kind, zo, self.y).wait_send()
                self.y_copy(kind, zo, self.x).wait_send()
            for kind in range(7):
                self.c_copy(kind, zo, self.c).wait_send()


def shared_gather_kernel(depth, sh_ref, ws_ref, loc, zs, zr, xs, xr, cs, cr):
    z, x, y, c = place()

    def slot(h, zo, xo):
        return ws_ref.at[h, zo * 2 + xo]

    def z_copy(up, zo, first=False):
        dst = slot(c, zo, x)
        src = sh_ref.at[c] if first else dst
        return push(src, dst, zs.at[0 if up else 1, zo], zr.at[zo], at(z + 1 if up else z - 1, x, y, c))

    def x_copy(zo, first=False):
        dst = slot(c, zo, x)
        return push(sh_ref.at[c] if first else dst, dst, xs.at[zo], xr.at[zo], at(z, 1 - x, y, c))

    def c_copy(zo, xo, first=False):
        dst = slot(c, zo, xo)
        return push(
            sh_ref.at[c] if first else dst, dst, cs.at[xo, zo], cr.at[xo, zo], at(z, x, y, 1 - c)
        )

    meet(z, x, y, c, depth)
    local = pltpu.make_async_copy(sh_ref.at[c], slot(c, z, x), loc.at[0])
    local.start()

    @pl.when(z < depth - 1)
    def _():
        z_copy(True, z, True).start()

    @pl.when(z > 0)
    def _():
        z_copy(False, z, True).start()

    x_copy(z, True).start()
    c_copy(z, x, True).start()
    for s in range(1, depth):

        def step(zo, up, more):
            z_copy(True, zo).wait_recv()

            @pl.when(more)
            def _():
                z_copy(up, zo).start()

            x_copy(zo).start()
            c_copy(zo, x).start()

        @pl.when(z - s >= 0)
        def _():
            step(z - s, True, z < depth - 1)

        @pl.when(z + s < depth)
        def _():
            step(z + s, False, z > 0)

    for j in range(depth):
        zo = lax.rem(z + j, depth)
        x_copy(zo).wait_recv()
        c_copy(zo, 1 - x).start()
    for zo in range(depth):
        for xo in range(2):
            c_copy(zo, xo).wait_recv()
    local.wait()
    for zo in range(depth):
        @pl.when((z < depth - 1) & (zo <= z))
        def _():
            z_copy(True, zo).wait_send()

        @pl.when((z > 0) & (zo >= z))
        def _():
            z_copy(False, zo).wait_send()

        x_copy(zo).wait_send()
        for xo in range(2):
            c_copy(zo, xo).wait_send()


def expert_gather_kernel(depth, ex_ref, we_ref, *sems):
    gather = Gather(depth, ex_ref, we_ref, sems)
    meet(gather.z, gather.x, gather.y, gather.c, depth)
    gather.begin()
    gather.turns(0)
    for s in range(1, depth):
        gather.line(s)
        if s > 1:
            gather.turns(s - 1)
    gather.turns(depth - 1)
    gather.last()
    gather.finish()


class Scatter:
    def __init__(self, depth, ge_ref, bufs, sems):
        self.depth = depth
        self.ge = ge_ref
        self.t, self.rc, self.r1, self.r2, self.r3 = bufs
        (self.ls, self.cs, self.cr, self.s1, self.q1, self.s2, self.q2, self.s3, self.q3) = sems
        self.z, self.x, self.y, self.c = place()

    @staticmethod
    def scratch(depth, cols, shard):
        dma = pltpu.SemaphoreType.DMA
        bufs = [
            pltpu.VMEM((2, 2, depth, 2, shard, cols), bf16),
            pltpu.VMEM((2, 2, depth, 2, shard, cols), bf16),
            pltpu.VMEM((2, depth, 2, shard, cols), bf16),
            pltpu.VMEM((2, depth, shard, cols), bf16),
            pltpu.VMEM((2, depth, shard, cols), bf16),
        ]
        sems = [
            dma((2, 2)),
            dma((2, 2)),
            dma((2, 2)),
            dma((2, depth, 2)),
            dma((2, depth, 2)),
            dma((2, depth)),
            dma((2, depth)),
            dma((2, depth)),
            dma((2, depth)),
        ]
        return bufs + sems

    def local(self, i, s):
        y = self.y if i == 0 else 1 - self.y
        return pltpu.make_async_copy(self.ge.at[y * 2 + self.c, s], self.t.at[i, s], self.ls.at[i, s])

    def core(self, i, s):
        y = self.y if i == 0 else 1 - self.y
        return push(
            self.ge.at[y * 2 + 1 - self.c, s],
            self.rc.at[i, s],
            self.cs.at[i, s],
            self.cr.at[i, s],
            at(self.z, self.x, self.y, 1 - self.c),
        )

    def one(self, s, zo, k):
        if s == 0:
            src, device = self.t.at[1, 0, zo, k], at(self.z, self.x, 1 - self.y, self.c)
        else:
            src, device = self.t.at[k, 1, zo, 1 - self.x], at(self.z, 1 - self.x, self.y, self.c)
        return push(src, self.r1.at[s, zo, k], self.s1.at[s, zo, k], self.q1.at[s, zo, k], device)

    def two(self, s, zo):
        if s == 0:
            src, device = self.t.at[0, 0, zo, 1 - self.x], at(self.z, 1 - self.x, self.y, self.c)
        else:
            src, device = self.t.at[1, 1, zo, self.x], at(self.z, self.x, 1 - self.y, self.c)
        return push(src, self.r2.at[s, zo], self.s2.at[s, zo], self.q2.at[s, zo], device)

    def three(self, s, zo):
        return push(
            self.t.at[0, s, zo, self.x],
            self.r3.at[s, self.z],
            self.s3.at[s, zo],
            self.q3.at[s, self.z],
            at(zo, self.x, self.y, self.c),
        )

    def arrived(self, s, zo):
        return push(
            self.r3.at[s, zo], self.r3.at[s, zo], self.s3.at[s, zo], self.q3.at[s, zo], at(zo, self.x, self.y, self.c)
        )

    def begin(self):
        for i, s in ((1, 0), (0, 1), (1, 1), (0, 0)):
            self.core(i, s).start()
            self.local(i, s).start()

    def order(self, j):
        return lax.rem(self.z + j + 1, self.depth)

    def fold(self, ref, other):
        ref[...] = (ref[...].astype(f32) + other[...].astype(f32)).astype(bf16)

    def merge(self, i, s):
        self.core(i, s).wait_recv()
        self.local(i, s).wait()

        def body(j, _):
            zo = self.order(j)
            for xo in range(2):
                self.fold(self.t.at[i, s, zo, xo], self.rc.at[i, s, zo, xo])
            if (i, s) == (1, 0):
                self.one(0, zo, 0).start()
                self.one(0, zo, 1).start()
            if s == 1:
                self.one(1, zo, i).start()
            return 0

        lax.fori_loop(0, self.depth, body, 0)

    def second(self):
        def body(j, _):
            zo = self.order(j)
            for k in range(2):
                self.one(0, zo, k).wait_recv()
                self.fold(self.t.at[0, 0, zo, k], self.r1.at[0, zo, k])
            self.two(0, zo).start()
            for k in range(2):
                self.one(1, zo, k).wait_recv()
                self.fold(self.t.at[k, 1, zo, self.x], self.r1.at[1, zo, k])
            self.two(1, zo).start()
            return 0

        lax.fori_loop(0, self.depth, body, 0)

    def third(self):
        def body(j, _):
            zo = self.order(j)
            for s in range(2):
                self.two(s, zo).wait_recv()
                self.fold(self.t.at[0, s, zo, self.x], self.r2.at[s, zo])

                @pl.when(zo != self.z)
                def _():
                    self.three(s, zo).start()

            return 0

        lax.fori_loop(0, self.depth, body, 0)

    def result(self, s):
        total = self.t[0, s, self.z, self.x].astype(f32)
        for j in range(1, self.depth):
            zo = lax.rem(self.z + j, self.depth)
            self.arrived(s, zo).wait_recv()
            total = total + self.r3[s, zo].astype(f32)
        return total

    def finish(self):
        for i in range(2):
            for s in range(2):
                self.core(i, s).wait_send()

        def body(j, _):
            zo = self.order(j)
            for s in range(2):
                for k in range(2):
                    self.one(s, zo, k).wait_send()
                self.two(s, zo).wait_send()

                @pl.when(zo != self.z)
                def _():
                    self.three(s, zo).wait_send()

            return 0

        lax.fori_loop(0, self.depth, body, 0)


def expert_scatter_kernel(depth, ge_ref, out_ref, *scratch):
    scatter = Scatter(depth, ge_ref, scratch[:5], scratch[5:])
    meet(scatter.z, scatter.x, scatter.y, scatter.c, depth)
    scatter.begin()
    scatter.merge(1, 0)
    scatter.merge(0, 1)
    scatter.merge(1, 1)
    scatter.merge(0, 0)
    scatter.second()
    scatter.third()
    for s in range(2):
        out_ref[s] = scatter.result(s)
    scatter.finish()


def lamb_parts(weight, grad, first, second):
    first_new = BETA_ONE * first + (1.0 - BETA_ONE) * grad
    second_new = BETA_TWO * second + (1.0 - BETA_TWO) * grad * grad
    first_hat = first_new / (1.0 - BETA_ONE**STEP)
    second_hat = second_new / (1.0 - BETA_TWO**STEP)
    direction = first_hat / (jnp.sqrt(second_hat) + ADAM_EPS) + DECAY * weight
    return first_new, second_new, direction


def row_norms(values, lane0):
    lane = lax.broadcasted_iota(jnp.int32, (1, 128), 1)
    out = jnp.zeros((1, 128), f32)
    for i, v in enumerate(values):
        out = out + jnp.where(lane == lane0 + i, jnp.sum(v * v), 0.0)
    return out


def shared_scatter_kernel(depth, experts, *refs):
    (gs_ref, sm_ref, ge_ref), weights, firsts, seconds = refs[:3], refs[3:9], refs[9:15], refs[15:21]
    fs_ref, gsm_ref, norm_ref = refs[21:24]
    (t, rc, r1, r2, r3, src_c, src_y, src_x, sz, cur, wide, nb) = refs[24:36]
    (ccs, ccr, s1, q1, s2, q2, s3, q3, s4, q4, ms, mr, zs, zr, ns, nr) = refs[36:]
    z, x, y, c = place()
    dp, ex = z * 2 + x, y * 2 + c
    shard = fs_ref.shape[1]
    width = fs_ref.shape[2]

    barrier = pltpu.get_barrier_semaphore()

    def greet(device):
        pl.semaphore_signal(barrier, inc=1, device_id=device, device_id_type=pl.DeviceIdType.MESH)

    def peers(n, me):
        return [lax.rem(me + j, n) for j in range(1, n)]

    n_dp, n_ex = 2 * depth, 4
    for other in peers(n_dp, dp):
        greet((other, ex))
    for other in peers(n_ex, ex):
        greet((dp, other))
    pl.semaphore_wait(barrier, n_dp + n_ex - 2)

    near = [at(z, x, y, 1 - c), at(z, x, 1 - y, c), at(z, 1 - x, y, c)]
    y_of = [y, 1 - y]

    def core(i):
        return push(gs_ref.at[y_of[i], 1 - c], rc.at[i], ccs.at[i], ccr.at[i], near[0])

    def one(zo, k):
        if zo % 2 == 0:
            return push(t.at[1, zo, k], r1.at[zo, k], s1.at[zo, k], q1.at[zo, k], near[1])
        return push(t.at[k, zo, 1 - x], r1.at[zo, k], s1.at[zo, k], q1.at[zo, k], near[2])

    def two(zo):
        if zo % 2 == 0:
            return push(t.at[0, zo, 1 - x], r2.at[zo], s2.at[zo], q2.at[zo], near[2])
        return push(t.at[1, zo, x], r2.at[zo], s2.at[zo], q2.at[zo], near[1])

    def three(zo):
        return push(t.at[0, zo, x], r3.at[z], s3.at[zo], q3.at[z], at(zo, x, y, c))

    def arrived(zo):
        return push(r3.at[zo], r3.at[zo], s3.at[zo], q3.at[zo], at(zo, x, y, c))

    def small_hop(k):
        src = sm_ref if k == 0 else cur.at[k - 1]
        return push(src, (src_c, src_y, src_x)[k], ms.at[k], mr.at[k], near[k])

    def small_z(zo):
        return push(cur.at[2], sz.at[z], zs.at[zo], zr.at[z], at(zo, x, y, c))

    def small_from(zo):
        return push(sz.at[zo], sz.at[zo], zs.at[zo], zr.at[zo], at(zo, x, y, c))

    def fold(ref, a, b):
        ref[...] = (a[...].astype(f32) + b[...].astype(f32)).astype(bf16)

    small_hop(0).start()
    core(1).start()
    core(0).start()
    totals = row_norms([w[...] for w in weights], 0)
    for i in range(2):
        direction = lamb_parts(weights[4 + i][...], ge_ref[i], firsts[4 + i][...], seconds[4 + i][...])[2]
        totals = totals + row_norms([direction], 10 + i)
    small_hop(0).wait_recv()
    cur[0] = sm_ref[...] + src_c[...]
    small_hop(1).start()
    for i in (1, 0):
        core(i).wait_recv()
        for zo in range(depth):
            for k in range(2):
                fold(t.at[i, zo, k], gs_ref.at[y_of[i], c, zo, k], rc.at[i, zo, k])
            if zo % 2 == 0:
                if i == 1:
                    one(zo, 0).start()
                    one(zo, 1).start()
            else:
                one(zo, i).start()
    small_hop(1).wait_recv()
    cur[1] = cur[0] + src_y[...]
    small_hop(2).start()
    for zo in range(depth):
        for k in range(2):
            one(zo, k).wait_recv()
            target = t.at[0, zo, k] if zo % 2 == 0 else t.at[k, zo, x]
            fold(target, target, r1.at[zo, k])
        two(zo).start()
    small_hop(2).wait_recv()
    cur[2] = cur[1] + src_x[...]
    sz[z] = cur[2]
    for zo in range(depth):
        @pl.when(zo != z)
        def _():
            small_z(zo).start()

    for zo in range(depth):
        two(zo).wait_recv()
        target = t.at[0, zo, x]
        fold(target, target, r2.at[zo])

        @pl.when(zo != z)
        def _():
            three(zo).start()

    total = t[0, z, x].astype(f32)
    for zo in peers(depth, z):
        arrived(zo).wait_recv()
        total = total + r3[zo].astype(f32)
    fs_ref[ex] = total

    def four(e):
        return push(fs_ref.at[ex], fs_ref.at[ex], s4.at[e], q4.at[ex], (dp, e))

    def four_from(e):
        return push(fs_ref.at[e], fs_ref.at[e], s4.at[e], q4.at[e], (dp, e))

    for e in peers(n_ex, ex):
        four(e).start()
    for zo in peers(depth, z):
        small_from(zo).wait_recv()
    small = sz[0]
    for zo in range(1, depth):
        small = small + sz[zo]
    wide[...] = jnp.transpose(jnp.concatenate([small, jnp.zeros((128 - 16, small.shape[1]), f32)], axis=0))
    mine = jnp.transpose(wide[pl.ds(pl.multiple_of(dp * shard, 16), shard), :])[0:16]
    gsm_ref[...] = mine
    for i, g in ((2, mine[0:experts]), (3, mine[8:12])):
        direction = lamb_parts(weights[i][...], g, firsts[i][...], seconds[i][...])[2]
        totals = totals + row_norms([direction], 6 + i)
    for e in peers(n_ex, ex):
        four_from(e).wait_recv()
    for part in range(4):
        i = 1 if part == 3 else 0
        cols = slice(0, width) if part == 3 else slice(part * width, (part + 1) * width)
        direction = lamb_parts(weights[i][:, cols], fs_ref[part], firsts[i][:, cols], seconds[i][:, cols])[2]
        totals = totals + row_norms([direction], 6 + i)
    nb[dp] = jnp.broadcast_to(totals, (8, 128))

    def norm_push(r):
        return push(nb.at[dp], nb.at[dp], ns.at[r], nr.at[dp], (r, ex))

    def norm_from(r):
        return push(nb.at[r], nb.at[r], ns.at[r], nr.at[r], (r, ex))

    for r in peers(n_dp, dp):
        norm_push(r).start()
    for r in peers(n_dp, dp):
        norm_from(r).wait_recv()
    summed = nb[0]
    for r in range(1, n_dp):
        summed = summed + nb[r]
    norm_ref[...] = summed

    for r in peers(n_dp, dp):
        norm_push(r).wait_send()
    for e in peers(n_ex, ex):
        four(e).wait_send()
    for i in range(2):
        core(i).wait_send()
    for k in range(3):
        small_hop(k).wait_send()
    for zo in range(depth):
        for k in range(2):
            one(zo, k).wait_send()
        two(zo).wait_send()

        @pl.when(zo != z)
        def _():
            three(zo).wait_send()
            small_z(zo).wait_send()


def shared_scatter_scratch(depth, shard, width):
    dma = pltpu.SemaphoreType.DMA
    return [
        pltpu.VMEM((2, depth, 2, shard, width), bf16),
        pltpu.VMEM((2, depth, 2, shard, width), bf16),
        pltpu.VMEM((depth, 2, shard, width), bf16),
        pltpu.VMEM((depth, shard, width), bf16),
        pltpu.VMEM((depth, shard, width), bf16),
        pltpu.VMEM((16, width), f32),
        pltpu.VMEM((16, width), f32),
        pltpu.VMEM((16, width), f32),
        pltpu.VMEM((depth, 16, width), f32),
        pltpu.VMEM((3, 16, width), f32),
        pltpu.VMEM((width, 128), f32),
        pltpu.VMEM((2 * depth, 8, 128), f32),
        dma((2,)),
        dma((2,)),
        dma((depth, 2)),
        dma((depth, 2)),
        dma((depth,)),
        dma((depth,)),
        dma((depth,)),
        dma((depth,)),
        dma((4,)),
        dma((4,)),
        dma((3,)),
        dma((3,)),
        dma((depth,)),
        dma((depth,)),
        dma((2 * depth,)),
        dma((2 * depth,)),
    ]


def update_kernel(experts, *refs):
    (gsh_ref, gsm_ref, ge_ref, norm_ref), weights, firsts, seconds = refs[:4], refs[4:10], refs[10:16], refs[16:22]
    w_out, m_out, s_out = refs[22:28], refs[28:34], refs[34:40]
    trust_ref = refs[40]
    width = gsh_ref.shape[2]
    totals = norm_ref[0:1, :]
    lane = lax.broadcasted_iota(jnp.int32, (1, 128), 1)

    def pick(i):
        return jnp.sqrt(jnp.sum(jnp.where(lane == i, totals, 0.0), axis=-1, keepdims=True))

    row = lax.broadcasted_iota(jnp.int32, (6, 2), 0)
    col = lax.broadcasted_iota(jnp.int32, (6, 2), 1)
    trust = jnp.zeros((6, 2), f32)
    whole = slice(None)
    jobs = [(0, slice(p * width, (p + 1) * width), lambda p=p: gsh_ref[p]) for p in range(3)]
    jobs += [(1, whole, lambda: gsh_ref[3]), (2, whole, lambda: gsm_ref[0:experts]), (3, whole, lambda: gsm_ref[8:12])]
    jobs += [(4, whole, lambda: ge_ref[0]), (5, whole, lambda: ge_ref[1])]
    ratios = []
    for i in range(6):
        wn, un = pick(i), pick(6 + i)
        ratios.append(wn / (un + 1e-06))
        trust = jnp.where((row == i) & (col == 0), wn, jnp.where((row == i) & (col == 1), un, trust))
    trust_ref[...] = trust
    for i, cols, grad in jobs:
        weight = weights[i][:, cols]
        first, second, direction = lamb_parts(weight, grad(), firsts[i][:, cols], seconds[i][:, cols])
        w_out[i][:, cols] = weight - RATE * ratios[i] * direction
        m_out[i][:, cols] = first
        s_out[i][:, cols] = second


def per_device(
    dims,
    tokens,
    cotangent,
    routes,
    valid_mask,
    shift_region,
    qkv_weight,
    proj_weight,
    router_weight,
    norm_params,
    expert_in,
    expert_out,
    qkv_first,
    qkv_second,
    proj_first,
    proj_second,
    router_first,
    router_second,
    norm_first,
    norm_second,
    in_first,
    in_second,
    out_first,
    out_second,
):
    rows_here, width = tokens.shape
    experts = router_weight.shape[1]
    hidden = expert_in.shape[2]
    shard = qkv_weight.shape[0]
    capacity = 2 * rows_here // experts
    slots = -(-capacity // TILE) * TILE
    windows = rows_here // WINDOW
    per_group = 8
    steps = windows // per_group
    group_rows = per_group * WINDOW
    padded = windows * PAD

    fast = dims == (8, 4)
    depth = dims[0] // 2
    vmem = pl.BlockSpec(memory_space=pltpu.VMEM)
    anywhere = pl.BlockSpec(memory_space=pl.ANY)

    def remote(collective_id):
        return pltpu.CompilerParams(
            vmem_limit_bytes=VMEM_BYTES, collective_id=collective_id, has_side_effects=True
        )

    pack = jnp.concatenate([router_weight, norm_params], axis=1)
    pack = jnp.pad(pack, ((0, 0), (0, 128 - pack.shape[1])))
    shared_shard = jnp.concatenate([qkv_weight[:, : 2 * width], pack, qkv_weight[:, 2 * width :], proj_weight, pack], axis=1)
    shared_shard = jnp.stack(jnp.split(shared_shard.astype(bf16), 2, axis=1))
    expert_shard = jnp.stack([expert_in[0], expert_out[0]]).astype(bf16)
    if fast:
        dma = pltpu.SemaphoreType.DMA
        w_all = pl.pallas_call(
            functools.partial(shared_gather_kernel, depth),
            in_specs=[vmem],
            out_specs=anywhere,
            out_shape=jax.ShapeDtypeStruct((2, 2 * depth, shard, 2 * width + 128), bf16),
            scratch_shapes=[dma((1,)), dma((2, depth)), dma((depth,)), dma((depth,)), dma((depth,)), dma((2, depth)), dma((2, depth))],
            compiler_params=remote(0),
            name="shared_gather",
        )(shared_shard)
        w_exp = pl.pallas_call(
            functools.partial(expert_gather_kernel, depth),
            in_specs=[vmem],
            out_specs=anywhere,
            out_shape=jax.ShapeDtypeStruct((experts, 2, 2 * depth, shard, hidden), bf16),
            scratch_shapes=Gather.semaphores(depth),
            compiler_params=remote(1),
            name="expert_gather",
        )(expert_shard)
    else:
        w_all = lax.all_gather(shared_shard, "dp", axis=1, tiled=True)
        w_exp = lax.all_gather(lax.all_gather(expert_shard, "dp", axis=1, tiled=True), "expert", axis=0, tiled=False)
    w_all = w_all.reshape(2, width, 2 * width + 128)
    w_exp = w_exp.reshape(experts, 2, width, hidden)

    x3 = tokens.astype(f32).reshape(steps, group_rows, width)
    g3 = cotangent.reshape(steps, group_rows, width)
    fill = ((0, 0), (0, PAD - WINDOW))
    valid_w = valid_mask.reshape(windows, WINDOW)
    region_w = shift_region.reshape(windows, WINDOW)
    code = jnp.pad(jnp.where(valid_w == 1, region_w, -1), fill, constant_values=-2)
    route_p = jnp.pad(routes.reshape(windows, WINDOW), fill, constant_values=-1)
    meta = jnp.stack([code.reshape(-1), route_p.reshape(-1), jnp.pad(valid_w, fill).reshape(-1)], axis=1)
    region_row = jnp.tile(jnp.pad(region_w, fill, constant_values=-3), (1, 4)).reshape(windows, 1, 4 * PAD)

    rows = per_group * PAD
    params = pltpu.CompilerParams(vmem_limit_bytes=VMEM_BYTES, dimension_semantics=("arbitrary",))

    def by_step(*shape):
        zeros = (0,) * (len(shape) - 1)
        return pl.BlockSpec(shape, lambda i: (i,) + zeros)

    def whole(*shape):
        zeros = (0,) * len(shape)
        return pl.BlockSpec(shape, lambda i, *_: zeros)

    lanes = width // 128
    hz, y1, pr, attn, qkv, probs, key, counts = pl.pallas_call(
        functools.partial(forward_kernel, experts, slots, per_group),
        grid=(steps,),
        in_specs=[
            by_step(1, group_rows, width),
            by_step(1, group_rows, width),
            by_step(rows, 3),
            by_step(per_group, 1, 4 * PAD),
            whole(2, width, 2 * width + 128),
        ],
        out_specs=[
            by_step(rows, 2 * width),
            by_step(rows, width),
            by_step(rows, 128),
            by_step(rows, width),
            by_step(per_group, PAD, 3 * width),
            by_step(per_group, lanes, PAD, 4 * PAD),
            by_step(rows, 128),
            whole(1, 128),
        ],
        out_shape=[
            jax.ShapeDtypeStruct((padded, 2 * width), bf16),
            jax.ShapeDtypeStruct((padded, width), f32),
            jax.ShapeDtypeStruct((padded, 128), f32),
            jax.ShapeDtypeStruct((padded, width), bf16),
            jax.ShapeDtypeStruct((windows, PAD, 3 * width), bf16),
            jax.ShapeDtypeStruct((windows, lanes, PAD, 4 * PAD), f32),
            jax.ShapeDtypeStruct((padded, 128), jnp.int32),
            jax.ShapeDtypeStruct((1, 128), jnp.int32),
        ],
        scratch_shapes=[pltpu.VMEM((rows, width), f32), pltpu.VMEM((rows, width), f32), pltpu.VMEM((1, 128), f32)],
        compiler_params=params,
        name="attention_forward",
    )(x3, g3, meta, region_row, w_all)

    key_row = key[:, 0].reshape(1, padded)
    grads, tok = pl.pallas_call(
        functools.partial(expert_kernel, slots),
        grid_spec=pltpu.PrefetchScalarGridSpec(
            num_scalar_prefetch=1,
            grid=(experts,),
            in_specs=[
                whole(padded, 2 * width),
                whole(1, padded),
                whole(padded, 128),
                pl.BlockSpec((1, 2, width, hidden), lambda e, *_: (e, 0, 0, 0)),
            ],
            out_specs=[
                pl.BlockSpec((1, 2, width, hidden), lambda e, *_: (e, 0, 0, 0)),
                whole(padded, 2 * width),
            ],
            scratch_shapes=[pltpu.VMEM((2, width, hidden), f32)],
        ),
        out_shape=[
            jax.ShapeDtypeStruct((experts, 2, width, hidden), bf16),
            jax.ShapeDtypeStruct((padded, 2 * width), f32),
        ],
        compiler_params=params,
        name="experts",
    )(counts[0], hz, key_row, key, w_exp)

    out3, dx3, shared_grad, small_grad = pl.pallas_call(
        functools.partial(backward_kernel, experts, per_group),
        grid=(steps,),
        in_specs=[
            by_step(1, group_rows, width),
            by_step(1, group_rows, width),
            by_step(rows, 3),
            whole(2, width, 2 * width + 128),
            by_step(rows, 2 * width),
            by_step(rows, 2 * width),
            by_step(rows, width),
            by_step(rows, 128),
            by_step(rows, width),
            by_step(per_group, PAD, 3 * width),
            by_step(per_group, lanes, PAD, 4 * PAD),
        ],
        out_specs=[
            by_step(1, group_rows, width),
            by_step(1, group_rows, width),
            whole(4, width, width),
            whole(16, width),
        ],
        out_shape=[
            jax.ShapeDtypeStruct((steps, group_rows, width), f32),
            jax.ShapeDtypeStruct((steps, group_rows, width), f32),
            jax.ShapeDtypeStruct((4, width, width), bf16),
            jax.ShapeDtypeStruct((16, width), f32),
        ],
        scratch_shapes=[
            pltpu.VMEM((rows, width), f32),
            pltpu.VMEM((rows, width), f32),
            pltpu.VMEM((rows, width), f32),
            pltpu.VMEM((rows, width), bf16),
            pltpu.VMEM((3, rows, width), bf16),
            pltpu.VMEM((4, width, width), f32),
            pltpu.VMEM((136, width), f32),
        ],
        compiler_params=params,
        name="attention_backward",
    )(x3, g3, meta, w_all, tok, hz, y1, pr, attn, qkv, probs)
    block_output = out3.reshape(rows_here, width).astype(bf16)
    input_grad = dx3.reshape(rows_here, width)

    weights_now = (qkv_weight, proj_weight, router_weight.T, norm_params.T, expert_in[0], expert_out[0])
    firsts_now = (qkv_first, proj_first, router_first.T, norm_first.T, in_first[0], out_first[0])
    seconds_now = (qkv_second, proj_second, router_second.T, norm_second.T, in_second[0], out_second[0])
    state = (*weights_now, *firsts_now, *seconds_now)
    if fast:
        g_exp = pl.pallas_call(
            functools.partial(expert_scatter_kernel, depth),
            in_specs=[anywhere],
            out_specs=vmem,
            out_shape=jax.ShapeDtypeStruct((2, shard, hidden), f32),
            scratch_shapes=Scatter.scratch(depth, hidden, shard),
            compiler_params=remote(2),
            name="expert_scatter",
        )(grads.reshape(experts, 2, depth, 2, shard, hidden))
        shared, small, norms = pl.pallas_call(
            functools.partial(shared_scatter_kernel, depth, experts),
            in_specs=[vmem] * (3 + len(state)),
            out_specs=[vmem] * 3,
            out_shape=[
                jax.ShapeDtypeStruct((4, shard, width), f32),
                jax.ShapeDtypeStruct((16, shard), f32),
                jax.ShapeDtypeStruct((8, 128), f32),
            ],
            scratch_shapes=shared_scatter_scratch(depth, shard, width),
            compiler_params=remote(3),
            name="shared_scatter",
        )(shared_grad.reshape(2, 2, depth, 2, shard, width), small_grad, g_exp, *state)
    else:
        shared = lax.psum(shared_grad.astype(f32), ("expert", "dp"))
        small = lax.psum(small_grad, ("expert", "dp"))
        g_exp = lax.psum(grads.astype(f32), ("expert", "dp"))
        start = lax.axis_index("dp") * shard
        shared = lax.dynamic_slice_in_dim(shared, start, shard, axis=1)
        small = lax.dynamic_slice_in_dim(small, start, shard, axis=1)
        g_exp = lax.dynamic_index_in_dim(g_exp, lax.axis_index("expert"), 0, keepdims=False)
        g_exp = lax.dynamic_slice_in_dim(g_exp, start, shard, axis=1)
        reduced = (
            jnp.concatenate([shared[0], shared[1], shared[2]], axis=1),
            shared[3],
            small[0:experts],
            small[8:12],
            g_exp[0],
            g_exp[1],
        )
        steps_now = [lamb_parts(*entry)[2] for entry in zip(weights_now, reduced, firsts_now, seconds_now)]
        sums = jnp.stack([jnp.sum(v * v) for v in (*weights_now, *steps_now)])
        norms = jnp.broadcast_to(jnp.pad(lax.psum(sums, "dp"), (0, 128 - 12)), (8, 128))
    results = pl.pallas_call(
        functools.partial(update_kernel, experts),
        in_specs=[vmem] * (4 + len(state)),
        out_specs=[vmem] * (len(state) + 1),
        out_shape=[jax.ShapeDtypeStruct(v.shape, f32) for v in weights_now] * 3 + [jax.ShapeDtypeStruct((6, 2), f32)],
        compiler_params=pltpu.CompilerParams(vmem_limit_bytes=VMEM_BYTES),
        name="lamb_update",
    )(shared, small, g_exp, norms, *state)

    def restore(values):
        return (values[0], values[1], values[2].T, values[3].T, values[4][None], values[5][None])

    return (
        block_output,
        input_grad,
        *restore(results[0:6]),
        *restore(results[6:12]),
        *restore(results[12:18]),
        results[18][None],
    )


def solution(mesh):
    tok2 = P(("dp", "expert"), None)
    tok1 = P(("dp", "expert"))
    row = P("dp", None)
    exp = P("expert", "dp", None)
    shared4 = (row, row, row, row)
    placed = (tok2, tok2, tok2, tok1, tok1, *shared4, exp, exp, *shared4, *shared4, exp, exp, exp, exp)
    results = (tok2, tok2, *((*shared4, exp, exp) * 3), P("expert", None, None))
    dims = (mesh.shape["dp"], mesh.shape["expert"])
    return jax.shard_map(
        functools.partial(per_device, dims),
        mesh=mesh,
        in_specs=placed,
        out_specs=results,
        check_vma=False,
    )
```

time: 951 us -> 294 us (0.31)
  waiting for transfers between devices: 374 us -> 0 us
  Pallas kernels: 0 us -> 276 us
  local copies, waits for them, and re-layouts: 166 us -> 7.29 us
  blocking collectives: 157 us -> 0 us
  matrix products: 109 us -> 0 us
  other arithmetic: 105 us -> 9.64 us
  between operations: 18.8 us -> 0.84 us
  starting transfers between devices: 14.1 us -> 0 us
    pallas_call x0 -> x8, Pallas kernels: none -> 276 us  [the longest x1 62 us: per_device(): pl.pallas_call(functools.partial(expert_scatter_kernel, depth), in_specs=...]
    reduce_scatter x4 -> x0, waiting for transfers between devices: 266 us -> none  [the longest x1 71.8 us: per_device(): lax.psum_scatter(grad_down, 'dp', scatter_dimension=0, tiled=True)]
    dot_general x20 -> x0, matrix products: 106 us -> none  [the longest x1 11.6 us: per_device(): jnp.einsum('scd,df->scf', grad_recv, w_down, preferred_element_type=f32)]
    all_gather x4 -> x0, blocking collectives: 105 us -> none  [the longest x1 33.1 us: per_device(): lax.all_gather(proj_weight.astype(bf16), 'dp', axis=0, tiled=True)]
    gather x2 -> x0, local copies, waits for them, and re-layouts: 46 us -> none  [the longest x1 23.1 us: per_device(): grad_h2 = grad_h2 + grad_back[route_ids, slot_index].astype(f32)]
    all_to_all x3 -> x0, waiting for transfers between devices: 45.7 us -> none  [the longest x1 22 us: per_device(): lax.all_to_all(send, 'expert', split_axis=0, concat_axis=0, tiled=True)]
    reshape x10 -> x3, local copies, waits for them, and re-layouts: 41.8 us -> 1.67 us  [the longest x1 0.79 us: per_device(): region_w = shift_region.reshape(windows, WINDOW)]
    convert_element_type x10 -> x1, other arithmetic: 41.1 us -> 2.51 us  [per_device(): block_output = out3.reshape(rows_here, width).astype(bf16)]
  transfers between devices with their start and end apart: 12 -> 0, of which waited for: 9 -> 0; matrix products, arithmetic and copies ran while one was open for 29% -> 0% of each run, Pallas kernels for 0% -> 0%
where the time goes in v1:
time: 294 us; the launch traced here: 293 us
  Pallas kernels  276 us (94%)
  other arithmetic  9.64 us (3%)
  local copies, waits for them, and re-layouts  7.29 us (2%)
    pallas_call x1, Pallas kernels, per_device(): pl.pallas_call(functools.partial(expert_scatter_kernel, depth), in_specs=...  62 us
    pallas_call x1, Pallas kernels, per_device(): pl.pallas_call(functools.partial(expert_gather_kernel, depth), in_specs=[...  46.8 us
    pallas_call x1, Pallas kernels, per_device(): pl.pallas_call(functools.partial(expert_kernel, slots), grid_spec=pltpu.P...  40 us
    pallas_call x1, Pallas kernels, per_device(): pl.pallas_call(functools.partial(backward_kernel, experts, per_group), gr...  37.9 us
    pallas_call x1, Pallas kernels, per_device(): pl.pallas_call(functools.partial(shared_scatter_kernel, depth, experts),...  33.7 us
    pallas_call x1, Pallas kernels, per_device(): pl.pallas_call(functools.partial(forward_kernel, experts, slots, per_grou...  28.5 us
    pallas_call x1, Pallas kernels, per_device(): pl.pallas_call(functools.partial(shared_gather_kernel, depth), in_specs=[...  22.6 us

profile of v1, /device:TPU:0, one launch (start us, length us, event | category | flops | bytes accessed | tf_op | source)
XLA Modules:
  0.0 293.4 jit_solution(7565451534840457606)
XLA Ops:
  0.7 0.8 pad_maximum_fusion.4
  1.4 0.7 reduce
  2.4 0.8 reshape.85
  3.2 0.8 reshape.86
  4.3 0.7 tile.9.row_ref
  5.0 0.9 convert.22
  5.8 0.9 convert.20
  6.9 0.7 pad_maximum_fusion.1.sh_ref
  7.6 1.0 convert.23
  8.6 0.7 pad_maximum_fusion.ex_ref
  9.3 1.2 copy.55.meta_ref
  10.5 22.6 %shared_gather.1 = bf16[2,8,48,896]{3,2,1,0:T(8,128)(2,1)} custom-call(bf16[2,48,896]{2,1,0:T(8,128)(2,1)} %pad_maximum_fusion.1.sh_ref), custom_call_target="tpu_custom_call" | custom-call | tf_op jit(solution)/shard_map/shared_gather/pallas_call | solution.py:1116
  33.1 1.4 convert.25.x_ref
  34.5 46.8 %expert_gather.1 = bf16[4,2,8,48,1536]{4,3,2,1,0:T(8,128)(2,1)} custom-call(bf16[2,48,1536]{2,1,0:T(8,128)(2,1)} %pad_maximum_fusion.ex_ref), custom_call_target="tpu_custom_call" | custom-call | tf_op jit(solution)/shard_map/expert_gather/pallas_call | solution.py:1125
  81.3 28.5 %attention_forward.1 = (bf16[1536,768]{1,0:T(8,128)(2,1)}, f32[1536,384]{1,0:T(8,128)}, f32[1536,128]{1,0:T(8,128)}, bf16[1536,384]{1,0:T(8,128)(2,1)}, bf16[24,...) custom-call(f32[3,392,384]{2,1,0:T(8,128)} %convert.25.x_ref, ...), custom_call_target="tpu_custom_call" | custom-call | tf_op jit(solution)/shard_map/attention_forward/pallas_call | solution.py:1162
  109.8 1.4 slice_reduce_fusion
  111.2 0.6 reshape_squeeze.3.keyrow_ref
  111.8 40.0 %experts.1 = (bf16[4,2,384,1536]{3,2,1,0:T(8,128)(2,1)}, f32[1536,768]{1,0:T(8,128)}) custom-call(s32[128]{0:T(128)} %bitcast.73, bf16[1536,768]{1,0:T(8,128)(2,1)} %get-tuple-element.58.hz_ref, s32[1,1536]{1,0:T(1,128)} %reshape_squeeze.3.keyrow_ref, s32[1536,128]{1,0:T(8,128)} %get-tuple-element.59.keycol_ref, bf16[4,2,384,1536]{3,2,1,0:T(8,128)(2,1)} %bitcast.39), custom_call_target="tpu_custom_call" | custom-call | tf_op jit(solution)/shard_map/experts/pallas_call | solution.py:1198
  151.9 37.9 %attention_backward.1 = (f32[3,392,384]{2,1,0:T(8,128)}, f32[3,392,384]{2,1,0:T(8,128)}, bf16[4,384,384]{2,1,0:T(8,128)(2,1)}, f32[16,384]{1,0:T(8,128)}) custom-call(f32[3,392,384]{2,1,0:T(8,128)} %convert.25.x_ref, f32[3,392,384]{2,1,0:T(8,128)} %bitcast.44, s32[1536,3]{1,0:T(8,128)} %copy.55.meta_ref, bf16[2,384,896]{2,1,0:T(8,128)(2,1)} %bitcast.41, ...), custom_call_target="tpu_custom_call" | custom-call | tf_op jit(solution)/shard_map/attention_backward/pallas_call | solution.py:1223
  189.8 2.5 convert_element_type.11
  192.3 62.0 %expert_scatter.1.refs_2_ = f32[2,48,1536]{2,1,0:T(8,128)} custom-call(bf16[4,2,4,2,48,1536]{5,4,3,2,1,0:T(8,128)(2,1)} %bitcast.42), custom_call_target="tpu_custom_call" | custom-call | tf_op jit(solution)/shard_map/expert_scatter/pallas_call | solution.py:1271
  254.3 33.7 %shared_scatter.1 = (f32[4,48,384]{2,1,0:T(8,128)}, f32[16,48]{1,0:T(8,128)}, f32[8,128]{1,0:T(8,128)}) custom-call(bf16[2,2,4,2,48,384]{5,4,3,2,1,0:T(8,128)(2,1)} %bitcast.57, f32[16,384]{1,0:T(8,128)} %get-tuple-element.69.refs_1_, f32[2,48,1536]{2,1,0:T(8,128)} %expert_scatter.1.refs_2_, f32[48,1152]{1,0:T(8,128)} %refs_4_.3, f32[48,384]{1,0:T(8,128)} %refs_5_.1, ...), custom_call_target="tpu_custom_call" | custom-call | tf_op jit(solution)/shard_map/shared_scatter/pallas_call | solution.py:1280
  288.0 4.1 %lamb_update.1 = (f32[48,1152]{1,0:T(8,128)}, f32[48,384]{1,0:T(8,128)}, f32[4,48]{1,0:T(4,128)}, f32[4,48]{1,0:T(4,128)}, f32[48,1536]{1,0:T(8,128)}, /*index=5...) custom-call(f32[4,48,384]{2,1,0:T(8,128)} %get-tuple-element.71.refs, ...), custom_call_target="tpu_custom_call" | custom-call | tf_op jit(solution)/shard_map/lamb_update/pallas_call | solution.py:1313
  292.1 1.3 copy.56
  (21 shorter events, 0.6 us)
Async XLA Ops:
  0.7 7.9 %copy-start = (f32[1,48,1536]{2,1,0:T(8,128)S(1)}, f32[1,48,1536]{2,1,0:T(8,128)}, u32[]{:S(2)}) copy-start(f32[1,48,1536]{2,1,0:T(8,128)} %param.33) | copy-start | bytes 884740
  6.8 26.3 %copy-start.1 = (bf16[1176,384]{1,0:T(8,128)(2,1)S(1)}, bf16[1176,384]{1,0:T(8,128)(2,1)}, u32[]{:S(2)}) copy-start(bf16[1176,384]{1,0:T(8,128)(2,1)} %param.23) | copy-start | bytes 2709508

commit v2 on v1

--- a/solution.py
+++ b/solution.py
@@ -12,7 +12,7 @@
 WINDOW = 49
 PAD = 64
 STEP = 5
-TILE = 128
+TILE = 256
 NORM_EPS = 1e-05
 MASKED = -1e30
 BETA_ONE = 0.9
@@ -73,71 +73,150 @@
 
 
 def weight_part(w_ref, part):
-    width = w_ref.shape[1]
-    at = (part % 2) * width
-    return w_ref[part // 2, :, at : at + width]
-
-
-def load_windows(src_ref, dst_ref, per_group):
+    width = (w_ref.shape[-1] - 128) // 2
+    cols = slice((part % 2) * width, (part % 2 + 1) * width)
+    if len(w_ref.shape) == 4:
+        return w_ref[part // 2, :, :, cols].reshape(width, width)
+    return w_ref[part // 2, :, cols]
+
+
+def small_part(w_ref):
+    width = (w_ref.shape[-1] - 128) // 2
+    if len(w_ref.shape) == 4:
+        return w_ref[0, :, :, 2 * width :].reshape(width, 128)
+    return w_ref[0, :, 2 * width :]
+
+
+def load_windows(src_ref, wide_ref, dst_ref, per_group):
     width = dst_ref.shape[-1]
+    wide_ref[...] = src_ref[0].astype(f32)
     for k in range(per_group):
-        dst_ref[k * PAD : k * PAD + WINDOW, :] = src_ref[0, k * WINDOW : (k + 1) * WINDOW, :]
+        dst_ref[k * PAD : k * PAD + WINDOW, :] = wide_ref[k * WINDOW : (k + 1) * WINDOW, :]
         dst_ref[k * PAD + WINDOW : (k + 1) * PAD, :] = jnp.zeros((PAD - WINDOW, width), f32)
 
 
-def forward_kernel(
-    experts,
-    slots,
-    per_group,
-    x_ref,
-    g_ref,
-    meta_ref,
-    row_ref,
-    w_ref,
-    hz_ref,
-    y1_ref,
-    pr_ref,
-    attn_ref,
-    qkv_ref,
-    p_ref,
-    key_ref,
-    count_ref,
-    xp,
-    gp,
-    carry,
-):
+def store_windows(src_ref, wide_ref, out_ref, per_group):
+    for k in range(per_group):
+        wide_ref[k * WINDOW : (k + 1) * WINDOW, :] = src_ref[k * PAD : k * PAD + WINDOW, :]
+    out_ref[0] = wide_ref[...].astype(out_ref.dtype)
+
+
+def token_columns(combo_ref, per_group):
+    turned = jnp.transpose(combo_ref[...].astype(f32))
+    return jnp.concatenate([turned[0:PAD, k : k + 1] for k in range(per_group)], axis=0).astype(jnp.int32)
+
+
+def route_of(combo):
+    return jnp.where(combo >= 512, combo & 15, -1)
+
+
+def valid_of(combo):
+    return ((combo >> 8) & 1).astype(f32)
+
+
+def run_hooks(plan, step, index):
+    for (k, i), jobs in plan.items():
+        if i == index:
+
+            @pl.when(step == k)
+            def _():
+                for job in jobs:
+                    job()
+
+
+def forward_kernel(dims, experts, slots, per_group, fast, *refs):
+    depth = dims[0] // 2
+    plan = {}
     step = pl.program_id(0)
+    if fast:
+        x_ref, g_ref, combo_ref, qkv_w, proj_w, router_w, norm_w, in_w, out_w = refs[:9]
+        hz_ref, y1_ref, pr_ref, attn_ref, qkv_ref, p_ref, key_ref, keyrow_ref, count_ref, ws_out, we_ref = refs[9:20]
+        xp, gp, wide, codes, regions, carry, w_ref, sh, ex, ws_sem = refs[20:30]
+        shared_sems, gather_sems = refs[30:37], refs[37:]
+        gather = Gather(depth, ex, we_ref, gather_sems)
+        shared = SharedGather(depth, sh, w_ref, shared_sems)
+
+        def enter():
+            meet(gather.z, gather.x, gather.y, gather.c, depth)
+            width = qkv_w.shape[1] // 3
+            shard = qkv_w.shape[0]
+            small = jnp.concatenate([router_w[...], norm_w[...]], axis=0)
+            small = jnp.concatenate([small, jnp.zeros((128 - small.shape[0], shard), f32)], axis=0)
+            sh[0, :, 0 : 2 * width] = qkv_w[:, 0 : 2 * width].astype(bf16)
+            sh[0, :, 2 * width :] = jnp.transpose(small).astype(bf16)
+            sh[1, :, 0:width] = qkv_w[:, 2 * width :].astype(bf16)
+            sh[1, :, width : 2 * width] = proj_w[...].astype(bf16)
+            sh[1, :, 2 * width :] = jnp.zeros((shard, 128), bf16)
+            shared.begin()
+            ex[0] = in_w[0].astype(bf16)
+            ex[1] = out_w[0].astype(bf16)
+            gather.begin()
+
+        def store_shared():
+            pltpu.make_async_copy(w_ref, ws_out, ws_sem.at[0]).start()
+
+        def leave():
+            gather.finish()
+            shared.finish()
+            pltpu.make_async_copy(w_ref, ws_out, ws_sem.at[0]).wait()
+
+        g = gather
+        plan = {
+            (0, 0): [enter],
+            (0, 1): [shared.receive, store_shared, lambda: g.turns(0), lambda: g.line(1)],
+            (0, 2): [lambda: g.line(2)],
+            (0, 3): [lambda: g.turns(1)],
+            (0, 4): [lambda: g.line(3)],
+            (1, 2): [lambda: g.turns(2)],
+            (1, 4): [lambda: g.turns(3)],
+            (2, 3): [g.last],
+            (2, 4): [leave],
+        }
+    else:
+        x_ref, g_ref, combo_ref, w_ref = refs[:4]
+        hz_ref, y1_ref, pr_ref, attn_ref, qkv_ref, p_ref, key_ref, keyrow_ref, count_ref = refs[4:13]
+        xp, gp, wide, codes, regions, carry = refs[13:19]
     rows = per_group * PAD
     width = x_ref.shape[-1]
     groups = width // 128
-    load_windows(x_ref, xp, per_group)
-    load_windows(g_ref, gp, per_group)
+    run_hooks(plan, step, 0)
+    load_windows(x_ref, wide, xp, per_group)
+    load_windows(g_ref, wide, gp, per_group)
 
     @pl.when(step == 0)
     def _():
         carry[...] = jnp.zeros_like(carry)
 
-    small = w_ref[0, :, 2 * width :]
+    combo = token_columns(combo_ref, per_group)
+    valid = valid_of(combo)
+    route = route_of(combo)
+    codes[...] = jnp.where((combo >> 8) & 1 == 1, (combo >> 4) & 15, -1)
+    flat = combo_ref[...]
+    flat = jnp.where(flat >= 512, (flat >> 4) & 15, -3)
+    for k in range(per_group):
+        regions[k] = jnp.concatenate([flat[k : k + 1, :]] * 2, axis=1)
+
+    normed, _ = norm_stats(xp[...])
+    run_hooks(plan, step, 1)
+    small = small_part(w_ref)
     small_t = jnp.transpose(small.astype(f32))
     a1, b1, a2, b2 = (small_t[experts + i : experts + i + 1, :] for i in range(4))
-    normed, _ = norm_stats(xp[...])
     h1 = (normed * a1 + b1).astype(bf16)
     for part in range(3):
         raw = dot_nn(h1, weight_part(w_ref, part))
         if part == 0:
             raw = raw * (HEAD_DIM**-0.5)
         qkv_ref[:, :, part * width : (part + 1) * width] = raw.astype(bf16).reshape(per_group, PAD, width)
-
-    meta = meta_ref[...]
-    valid = meta[:, 2:3].astype(f32)
+    run_hooks(plan, step, 2)
+
     masks = head_masks()
     key_i = lax.broadcasted_iota(jnp.int32, (PAD, 4 * PAD), 0)
     lane_i = lax.broadcasted_iota(jnp.int32, (PAD, 4 * PAD), 1)
     diagonal = key_i == lax.rem(lane_i, PAD)
 
     def window(w, _):
-        code = meta_ref[pl.ds(pl.multiple_of(w * PAD, PAD), PAD), 0:1]
-        allowed = (code == row_ref[w]) | diagonal
+        at = pl.ds(pl.multiple_of(w * PAD, PAD), PAD)
+        allowed = (codes[at, :] == regions[w]) | diagonal
         for lg in range(groups):
             q = qkv_ref[w, :, lg * 128 : (lg + 1) * 128]
             k = qkv_ref[w, :, width + lg * 128 : width + (lg + 1) * 128]
@@ -148,12 +227,13 @@
             p = e * (1.0 / jnp.sum(e, axis=0, keepdims=True))
             p_ref[w, lg] = p
             o = dot_tn(p.astype(bf16), v)
-            attn_ref[pl.ds(pl.multiple_of(w * PAD, PAD), PAD), lg * 128 : (lg + 1) * 128] = gather_heads(
-                o, masks
-            ).astype(bf16)
+            attn_ref[at, lg * 128 : (lg + 1) * 128] = gather_heads(o, masks).astype(bf16)
         return 0
 
-    lax.fori_loop(0, per_group, window, 0)
+    half = per_group // 2
+    lax.fori_loop(0, half, window, 0)
+    run_hooks(plan, step, 3)
+    lax.fori_loop(half, per_group, window, 0)
 
     y1 = xp[...] + dot_nn(attn_ref[...], weight_part(w_ref, 3))
     y1_ref[...] = y1
@@ -164,7 +244,7 @@
     e = jnp.exp(logits - jnp.max(logits, axis=-1, keepdims=True))
     pr = e * (1.0 / jnp.sum(e, axis=-1, keepdims=True))
     pr_ref[...] = pr
-    chosen = lane == meta[:, 1:2]
+    chosen = lane == route
     gate = jnp.sum(jnp.where(chosen, pr, 0.0), axis=-1, keepdims=True)
     gv = gp[...] * valid
     hz_ref[:, 0:width] = h2
@@ -175,10 +255,13 @@
     ranks = dot_nn(jnp.where(before, 1.0, 0.0).astype(bf16), onehot.astype(bf16)) + carry[0:1, :]
     slot = jnp.sum(ranks * onehot, axis=-1, keepdims=True)
     seen = jnp.sum(onehot, axis=-1, keepdims=True)
-    key = (meta[:, 1:2].astype(f32) * slots + slot) * seen + (seen - 1.0)
-    key_ref[...] = jnp.broadcast_to(key, (rows, 128)).astype(jnp.int32)
+    key = (route.astype(f32) * slots + slot) * seen + (seen - 1.0)
+    key = jnp.broadcast_to(key, (rows, 128))
+    key_ref[...] = key.astype(jnp.int32)
+    keyrow_ref[...] = jnp.transpose(key)[0:1, :].astype(jnp.int32)
     carry[...] = carry[...] + jnp.sum(onehot, axis=0, keepdims=True)
     count_ref[...] = carry[...].astype(jnp.int32)
+    run_hooks(plan, step, 4)
 
 
 def expert_kernel(slots, counts_ref, hz_ref, keyrow_ref, keycol_ref, we_ref, grad_ref, tok_ref, acc):
@@ -207,7 +290,7 @@
         back = dot_nt(dup, we_ref[0, 0]).astype(bf16)
         acc[1] += dot_tn(dz, hidden)
         acc[0] += dot_tn(rows, dup)
-        put = keycol_ref[...] == base + lax.broadcasted_iota(jnp.int32, (total, TILE), 1)
+        put = jnp.concatenate([keycol_ref[...]] * (TILE // 128), axis=1) == base + lax.broadcasted_iota(jnp.int32, (total, TILE), 1)
         tok_ref[...] += dot_nn(jnp.where(put, 1.0, 0.0).astype(bf16), jnp.concatenate([ret, back], axis=1))
         return 0
 
@@ -215,33 +298,39 @@
     grad_ref[0] = acc[...].astype(bf16)
 
 
-def backward_kernel(
-    experts,
-    per_group,
-    x_ref,
-    g_ref,
-    meta_ref,
-    w_ref,
-    tok_ref,
-    hz_ref,
-    y1_ref,
-    pr_ref,
-    attn_ref,
-    qkv_ref,
-    p_ref,
-    out_ref,
-    dx_ref,
-    shared_ref,
-    small_ref,
-    xp,
-    gp,
-    outp,
-    dattn,
-    dqkv,
-    acc,
-    acc_s,
-):
+def backward_kernel(dims, experts, per_group, fast, *refs):
+    depth = dims[0] // 2
+    plan = {}
     step = pl.program_id(0)
+    x_ref, g_ref, combo_ref, w_ref, tok_ref, hz_ref, y1_ref, pr_ref, attn_ref, qkv_ref, p_ref = refs[:11]
+    refs = refs[11:]
+    if fast:
+        ge_ref, out_ref, dx_ref, shared_ref, small_ref, gexp_ref = refs[:6]
+        xp, gp, wide, outp, dattn, dqkv, acc, acc_s = refs[6:14]
+        sc = Scatter(depth, ge_ref, refs[14:19], refs[19:])
+
+        def enter():
+            meet(sc.z, sc.x, sc.y, sc.c, depth)
+            sc.begin()
+
+        def leave():
+            sc.third(depth - 1)
+            for s in range(2):
+                gexp_ref[s] = sc.result(s)
+            sc.finish()
+
+        plan = {
+            (0, 0): [enter],
+            (0, 1): [lambda: sc.merge(0)],
+            (0, 3): [lambda: sc.second(0), lambda: sc.merge(1)],
+            (1, 1): [lambda: sc.second(1), lambda: sc.third(0), lambda: sc.merge(2)],
+            (2, 0): [lambda: sc.second(2), lambda: sc.third(1), lambda: sc.merge(3)],
+            (2, 3): [lambda: sc.second(3), lambda: sc.third(2)],
+            (2, 4): [leave],
+        }
+    else:
+        out_ref, dx_ref, shared_ref, small_ref = refs[:4]
+        xp, gp, wide, outp, dattn, dqkv, acc, acc_s = refs[4:12]
     rows = per_group * PAD
     width = x_ref.shape[-1]
     groups = width // 128
@@ -252,23 +341,24 @@
         acc[...] = jnp.zeros_like(acc)
         acc_s[...] = jnp.zeros_like(acc_s)
 
-    load_windows(x_ref, xp, per_group)
-    load_windows(g_ref, gp, per_group)
-    meta = meta_ref[...]
-    valid = meta[:, 2:3].astype(f32)
-    small = w_ref[0, :, 2 * width :]
+    run_hooks(plan, step, 0)
+    load_windows(x_ref, wide, xp, per_group)
+    load_windows(g_ref, wide, gp, per_group)
+    combo = token_columns(combo_ref, per_group)
+    valid = valid_of(combo)
+    route = route_of(combo)
+    small = small_part(w_ref)
     small_t = jnp.transpose(small.astype(f32))
     a1, b1, a2, b2 = (small_t[experts + i : experts + i + 1, :] for i in range(4))
     y1 = y1_ref[...]
     gv = gp[...] * valid
     z = tok_ref[:, 0:width]
     lane = lax.broadcasted_iota(jnp.int32, (rows, 128), 1)
-    chosen = lane == meta[:, 1:2]
+    chosen = lane == route
     pr = pr_ref[...]
     gate = jnp.sum(jnp.where(chosen, pr, 0.0), axis=-1, keepdims=True)
     outp[...] = y1 + gate * z
-    for k in range(per_group):
-        out_ref[0, k * WINDOW : (k + 1) * WINDOW, :] = outp[k * PAD : k * PAD + WINDOW, :]
+    store_windows(outp, wide, out_ref, per_group)
     dgate = jnp.sum(gv * z, axis=-1, keepdims=True)
     kept = jnp.where(lane < experts, jnp.where(chosen, 1.0, 0.0) - pr, 0.0)
     dlogits = (dgate * gate * kept).astype(bf16)
@@ -283,6 +373,7 @@
     da = dy1.astype(bf16)
     acc[3] += dot_tn(attn_ref[...], da)
     dattn[...] = dot_nt(da, weight_part(w_ref, 3)).astype(bf16)
+    run_hooks(plan, step, 1)
 
     masks = head_masks()
 
@@ -306,7 +397,11 @@
             dqkv[2, at, cols] = dv.astype(bf16)
         return 0
 
-    lax.fori_loop(0, per_group, window, 0)
+    half = per_group // 2
+    lax.fori_loop(0, half, window, 0)
+    run_hooks(plan, step, 2)
+    lax.fori_loop(half, per_group, window, 0)
+    run_hooks(plan, step, 3)
 
     n1, r1 = norm_stats(xp[...])
     h1 = (n1 * a1 + b1).astype(bf16)
@@ -318,8 +413,7 @@
     acc_s[128:129] += jnp.sum(dh1 * n1, axis=0, keepdims=True)
     acc_s[129:130] += jnp.sum(dh1, axis=0, keepdims=True)
     outp[...] = gp[...] + norm_back(dh1, n1, r1, a1)
-    for k in range(per_group):
-        dx_ref[0, k * WINDOW : (k + 1) * WINDOW, :] = outp[k * PAD : k * PAD + WINDOW, :]
+    store_windows(outp, wide, dx_ref, per_group)
 
     @pl.when(step == pl.num_programs(0) - 1)
     def _():
@@ -327,6 +421,8 @@
             shared_ref[part] = acc[part].astype(bf16)
         small_ref[0:8] = acc_s[0:8]
         small_ref[8:16] = acc_s[128:136]
+
+    run_hooks(plan, step, 4)
 
 
 def place():
@@ -389,8 +485,8 @@
             dma((7, depth)),
         ]
 
-    def e(self, y, c):
-        return y * 2 + c
+    def local(self):
+        return pltpu.make_async_copy(self.ex, self.pair(self.y, self.c, self.z, self.x), self.loc.at[0])
 
     def block(self, y, c, s, z, x):
         return self.we.at[y * 2 + c, s, z * 2 + x]
@@ -445,8 +541,7 @@
 
     def begin(self):
         z = self.z
-        self.local = pltpu.make_async_copy(self.ex, self.pair(self.y, self.c, z, self.x), self.loc.at[0])
-        self.local.start()
+        self.local().start()
 
         @pl.when(z < self.depth - 1)
         def _():
@@ -517,7 +612,7 @@
         for zo in range(self.depth):
             for kind in range(7):
                 self.c_copy(kind, zo, 1 - self.c).wait_recv()
-        self.local.wait()
+        self.local().wait()
         for zo in range(self.depth):
             @pl.when((z < self.depth - 1) & (zo <= z))
             def _():
@@ -534,95 +629,77 @@
                 self.c_copy(kind, zo, self.c).wait_send()
 
 
-def shared_gather_kernel(depth, sh_ref, ws_ref, loc, zs, zr, xs, xr, cs, cr):
-    z, x, y, c = place()
-
-    def slot(h, zo, xo):
-        return ws_ref.at[h, zo * 2 + xo]
-
-    def z_copy(up, zo, first=False):
-        dst = slot(c, zo, x)
-        src = sh_ref.at[c] if first else dst
-        return push(src, dst, zs.at[0 if up else 1, zo], zr.at[zo], at(z + 1 if up else z - 1, x, y, c))
-
-    def x_copy(zo, first=False):
-        dst = slot(c, zo, x)
-        return push(sh_ref.at[c] if first else dst, dst, xs.at[zo], xr.at[zo], at(z, 1 - x, y, c))
-
-    def c_copy(zo, xo, first=False):
-        dst = slot(c, zo, xo)
+class SharedGather:
+    def __init__(self, depth, sh_ref, ws_ref, sems):
+        self.depth, self.sh, self.ws = depth, sh_ref, ws_ref
+        self.loc, self.zs, self.zr, self.xs, self.xr, self.cs, self.cr = sems
+        self.z, self.x, self.y, self.c = place()
+
+    @staticmethod
+    def semaphores(depth):
+        dma = pltpu.SemaphoreType.DMA
+        return [dma((1,)), dma((depth,)), dma((depth,)), dma((depth,)), dma((depth,)), dma((2, depth)), dma((2, depth))]
+
+    def slot(self, zo, xo):
+        return self.ws.at[self.c, zo * 2 + xo]
+
+    def local(self):
+        return pltpu.make_async_copy(self.sh.at[self.c], self.slot(self.z, self.x), self.loc.at[0])
+
+    def z_copy(self, target):
         return push(
-            sh_ref.at[c] if first else dst, dst, cs.at[xo, zo], cr.at[xo, zo], at(z, x, y, 1 - c)
+            self.sh.at[self.c],
+            self.slot(self.z, self.x),
+            self.zs.at[target],
+            self.zr.at[self.z],
+            at(target, self.x, self.y, self.c),
         )
 
-    meet(z, x, y, c, depth)
-    local = pltpu.make_async_copy(sh_ref.at[c], slot(c, z, x), loc.at[0])
-    local.start()
-
-    @pl.when(z < depth - 1)
-    def _():
-        z_copy(True, z, True).start()
-
-    @pl.when(z > 0)
-    def _():
-        z_copy(False, z, True).start()
-
-    x_copy(z, True).start()
-    c_copy(z, x, True).start()
-    for s in range(1, depth):
-
-        def step(zo, up, more):
-            z_copy(True, zo).wait_recv()
-
-            @pl.when(more)
-            def _():
-                z_copy(up, zo).start()
-
-            x_copy(zo).start()
-            c_copy(zo, x).start()
-
-        @pl.when(z - s >= 0)
-        def _():
-            step(z - s, True, z < depth - 1)
-
-        @pl.when(z + s < depth)
-        def _():
-            step(z + s, False, z > 0)
-
-    for j in range(depth):
-        zo = lax.rem(z + j, depth)
-        x_copy(zo).wait_recv()
-        c_copy(zo, 1 - x).start()
-    for zo in range(depth):
-        for xo in range(2):
-            c_copy(zo, xo).wait_recv()
-    local.wait()
-    for zo in range(depth):
-        @pl.when((z < depth - 1) & (zo <= z))
-        def _():
-            z_copy(True, zo).wait_send()
-
-        @pl.when((z > 0) & (zo >= z))
-        def _():
-            z_copy(False, zo).wait_send()
-
-        x_copy(zo).wait_send()
-        for xo in range(2):
-            c_copy(zo, xo).wait_send()
-
-
-def expert_gather_kernel(depth, ex_ref, we_ref, *sems):
-    gather = Gather(depth, ex_ref, we_ref, sems)
-    meet(gather.z, gather.x, gather.y, gather.c, depth)
-    gather.begin()
-    gather.turns(0)
-    for s in range(1, depth):
-        gather.line(s)
-        if s > 1:
-            gather.turns(s - 1)
-    gather.turns(depth - 1)
-    gather.last()
-    gather.finish()
+    def z_from(self, zo):
+        dst = self.slot(zo, self.x)
+        return push(dst, dst, self.zs.at[zo], self.zr.at[zo], at(zo, self.x, self.y, self.c))
+
+    def x_copy(self, zo, first=False):
+        dst = self.slot(zo, self.x)
+        src = self.sh.at[self.c] if first else dst
+        return push(src, dst, self.xs.at[zo], self.xr.at[zo], at(self.z, 1 - self.x, self.y, self.c))
+
+    def c_copy(self, zo, xo, first=False):
+        dst = self.slot(zo, xo)
+        src = self.sh.at[self.c] if first else dst
+        return push(src, dst, self.cs.at[xo, zo], self.cr.at[xo, zo], at(self.z, self.x, self.y, 1 - self.c))
+
+    def others(self):
+        return [lax.rem(self.z + j, self.depth) for j in range(1, self.depth)]
+
+    def begin(self):
+        self.local().start()
+        for zo in self.others():
+            self.z_copy(zo).start()
+        self.x_copy(self.z, True).start()
+        self.c_copy(self.z, self.x, True).start()
+
+    def receive(self):
+        for zo in self.others():
+            self.z_from(zo).wait_recv()
+            self.x_copy(zo).start()
+            self.c_copy(zo, self.x).start()
+        for j in range(self.depth):
+            zo = lax.rem(self.z + j, self.depth)
+            self.x_copy(zo).wait_recv()
+            self.c_copy(zo, 1 - self.x).start()
+        for zo in range(self.depth):
+            for xo in range(2):
+                self.c_copy(zo, xo).wait_recv()
+        self.local().wait()
+
+    def finish(self):
+        for zo in self.others():
+            self.z_copy(zo).wait_send()
+        for zo in range(self.depth):
+            self.x_copy(zo).wait_send()
+            for xo in range(2):
+                self.c_copy(zo, xo).wait_send()
 
 
 class Scatter:
@@ -644,9 +721,9 @@
             pltpu.VMEM((2, depth, shard, cols), bf16),
         ]
         sems = [
-            dma((2, 2)),
-            dma((2, 2)),
-            dma((2, 2)),
+            dma((2, 2, depth)),
+            dma((2, 2, depth)),
+            dma((2, 2, depth)),
             dma((2, depth, 2)),
             dma((2, depth, 2)),
             dma((2, depth)),
@@ -656,17 +733,17 @@
         ]
         return bufs + sems
 
-    def local(self, i, s):
+    def local(self, i, s, zo):
         y = self.y if i == 0 else 1 - self.y
-        return pltpu.make_async_copy(self.ge.at[y * 2 + self.c, s], self.t.at[i, s], self.ls.at[i, s])
-
-    def core(self, i, s):
+        return pltpu.make_async_copy(self.ge.at[y * 2 + self.c, s, zo], self.t.at[i, s, zo], self.ls.at[i, s, zo])
+
+    def core(self, i, s, zo):
         y = self.y if i == 0 else 1 - self.y
         return push(
-            self.ge.at[y * 2 + 1 - self.c, s],
-            self.rc.at[i, s],
-            self.cs.at[i, s],
-            self.cr.at[i, s],
+            self.ge.at[y * 2 + 1 - self.c, s, zo],
+            self.rc.at[i, s, zo],
+            self.cs.at[i, s, zo],
+            self.cr.at[i, s, zo],
             at(self.z, self.x, self.y, 1 - self.c),
         )
 
@@ -699,9 +776,14 @@
         )
 
     def begin(self):
-        for i, s in ((1, 0), (0, 1), (1, 1), (0, 0)):
-            self.core(i, s).start()
-            self.local(i, s).start()
+        def body(j, _):
+            zo = self.order(j)
+            for i, s in ((1, 0), (0, 1), (1, 1), (0, 0)):
+                self.core(i, s, zo).start()
+                self.local(i, s, zo).start()
+            return 0
+
+        lax.fori_loop(0, self.depth, body, 0)
 
     def order(self, j):
         return lax.rem(self.z + j + 1, self.depth)
@@ -709,12 +791,11 @@
     def fold(self, ref, other):
         ref[...] = (ref[...].astype(f32) + other[...].astype(f32)).astype(bf16)
 
-    def merge(self, i, s):
-        self.core(i, s).wait_recv()
-        self.local(i, s).wait()
-
-        def body(j, _):
-            zo = self.order(j)
+    def merge(self, j):
+        zo = self.order(j)
+        for i, s in ((1, 0), (0, 1), (1, 1), (0, 0)):
+            self.core(i, s, zo).wait_recv()
+            self.local(i, s, zo).wait()
             for xo in range(2):
                 self.fold(self.t.at[i, s, zo, xo], self.rc.at[i, s, zo, xo])
             if (i, s) == (1, 0):
@@ -722,39 +803,27 @@
                 self.one(0, zo, 1).start()
             if s == 1:
                 self.one(1, zo, i).start()
-            return 0
-
-        lax.fori_loop(0, self.depth, body, 0)
-
-    def second(self):
-        def body(j, _):
-            zo = self.order(j)
-            for k in range(2):
-                self.one(0, zo, k).wait_recv()
-                self.fold(self.t.at[0, 0, zo, k], self.r1.at[0, zo, k])
-            self.two(0, zo).start()
-            for k in range(2):
-                self.one(1, zo, k).wait_recv()
-                self.fold(self.t.at[k, 1, zo, self.x], self.r1.at[1, zo, k])
-            self.two(1, zo).start()
-            return 0
-
-        lax.fori_loop(0, self.depth, body, 0)
-
-    def third(self):
-        def body(j, _):
-            zo = self.order(j)
-            for s in range(2):
-                self.two(s, zo).wait_recv()
-                self.fold(self.t.at[0, s, zo, self.x], self.r2.at[s, zo])
-
-                @pl.when(zo != self.z)
-                def _():
-                    self.three(s, zo).start()
-
-            return 0
-
-        lax.fori_loop(0, self.depth, body, 0)
+
+    def second(self, j):
+        zo = self.order(j)
+        for k in range(2):
+            self.one(0, zo, k).wait_recv()
+            self.fold(self.t.at[0, 0, zo, k], self.r1.at[0, zo, k])
+        self.two(0, zo).start()
+        for k in range(2):
+            self.one(1, zo, k).wait_recv()
+            self.fold(self.t.at[k, 1, zo, self.x], self.r1.at[1, zo, k])
+        self.two(1, zo).start()
+
+    def third(self, j):
+        zo = self.order(j)
+        for s in range(2):
+            self.two(s, zo).wait_recv()
+            self.fold(self.t.at[0, s, zo, self.x], self.r2.at[s, zo])
+
+            @pl.when(zo != self.z)
+            def _():
+                self.three(s, zo).start()
 
     def result(self, s):
         total = self.t[0, s, self.z, self.x].astype(f32)
@@ -765,13 +834,11 @@
         return total
 
     def finish(self):
-        for i in range(2):
-            for s in range(2):
-                self.core(i, s).wait_send()
-
         def body(j, _):
             zo = self.order(j)
             for s in range(2):
+                for i in range(2):
+                    self.core(i, s, zo).wait_send()
                 for k in range(2):
                     self.one(s, zo, k).wait_send()
                 self.two(s, zo).wait_send()
@@ -783,21 +850,6 @@
             return 0
 
         lax.fori_loop(0, self.depth, body, 0)
-
-
-def expert_scatter_kernel(depth, ge_ref, out_ref, *scratch):
-    scatter = Scatter(depth, ge_ref, scratch[:5], scratch[5:])
-    meet(scatter.z, scatter.x, scatter.y, scatter.c, depth)
-    scatter.begin()
-    scatter.merge(1, 0)
-    scatter.merge(0, 1)
-    scatter.merge(1, 1)
-    scatter.merge(0, 0)
-    scatter.second()
-    scatter.third()
-    for s in range(2):
-        out_ref[s] = scatter.result(s)
-    scatter.finish()
 
 
 def lamb_parts(weight, grad, first, second):
@@ -1037,9 +1089,9 @@
     def pick(i):
         return jnp.sqrt(jnp.sum(jnp.where(lane == i, totals, 0.0), axis=-1, keepdims=True))
 
-    row = lax.broadcasted_iota(jnp.int32, (6, 2), 0)
-    col = lax.broadcasted_iota(jnp.int32, (6, 2), 1)
-    trust = jnp.zeros((6, 2), f32)
+    row = lax.broadcasted_iota(jnp.int32, (2, 6), 1)
+    col = lax.broadcasted_iota(jnp.int32, (2, 6), 0)
+    trust = jnp.zeros((2, 6), f32)
     whole = slice(None)
     jobs = [(0, slice(p * width, (p + 1) * width), lambda p=p: gsh_ref[p]) for p in range(3)]
     jobs += [(1, whole, lambda: gsh_ref[3]), (2, whole, lambda: gsm_ref[0:experts]), (3, whole, lambda: gsm_ref[8:12])]
@@ -1106,46 +1158,10 @@
             vmem_limit_bytes=VMEM_BYTES, collective_id=collective_id, has_side_effects=True
         )
 
-    pack = jnp.concatenate([router_weight, norm_params], axis=1)
-    pack = jnp.pad(pack, ((0, 0), (0, 128 - pack.shape[1])))
-    shared_shard = jnp.concatenate([qkv_weight[:, : 2 * width], pack, qkv_weight[:, 2 * width :], proj_weight, pack], axis=1)
-    shared_shard = jnp.stack(jnp.split(shared_shard.astype(bf16), 2, axis=1))
-    expert_shard = jnp.stack([expert_in[0], expert_out[0]]).astype(bf16)
-    if fast:
-        dma = pltpu.SemaphoreType.DMA
-        w_all = pl.pallas_call(
-            functools.partial(shared_gather_kernel, depth),
-            in_specs=[vmem],
-            out_specs=anywhere,
-            out_shape=jax.ShapeDtypeStruct((2, 2 * depth, shard, 2 * width + 128), bf16),
-            scratch_shapes=[dma((1,)), dma((2, depth)), dma((depth,)), dma((depth,)), dma((depth,)), dma((2, depth)), dma((2, depth))],
-            compiler_params=remote(0),
-            name="shared_gather",
-        )(shared_shard)
-        w_exp = pl.pallas_call(
-            functools.partial(expert_gather_kernel, depth),
-            in_specs=[vmem],
-            out_specs=anywhere,
-            out_shape=jax.ShapeDtypeStruct((experts, 2, 2 * depth, shard, hidden), bf16),
-            scratch_shapes=Gather.semaphores(depth),
-            compiler_params=remote(1),
-            name="expert_gather",
-        )(expert_shard)
-    else:
-        w_all = lax.all_gather(shared_shard, "dp", axis=1, tiled=True)
-        w_exp = lax.all_gather(lax.all_gather(expert_shard, "dp", axis=1, tiled=True), "expert", axis=0, tiled=False)
-    w_all = w_all.reshape(2, width, 2 * width + 128)
-    w_exp = w_exp.reshape(experts, 2, width, hidden)
-
-    x3 = tokens.astype(f32).reshape(steps, group_rows, width)
+    x3 = tokens.reshape(steps, group_rows, width)
     g3 = cotangent.reshape(steps, group_rows, width)
-    fill = ((0, 0), (0, PAD - WINDOW))
-    valid_w = valid_mask.reshape(windows, WINDOW)
-    region_w = shift_region.reshape(windows, WINDOW)
-    code = jnp.pad(jnp.where(valid_w == 1, region_w, -1), fill, constant_values=-2)
-    route_p = jnp.pad(routes.reshape(windows, WINDOW), fill, constant_values=-1)
-    meta = jnp.stack([code.reshape(-1), route_p.reshape(-1), jnp.pad(valid_w, fill).reshape(-1)], axis=1)
-    region_row = jnp.tile(jnp.pad(region_w, fill, constant_values=-3), (1, 4)).reshape(windows, 1, 4 * PAD)
+    combo = (routes[:, 0] + 16 * shift_region + 256 * valid_mask + 512).reshape(windows, WINDOW)
+    combo = jnp.tile(jnp.pad(combo, ((0, 0), (0, PAD - WINDOW))), (1, 2))
 
     rows = per_group * PAD
     params = pltpu.CompilerParams(vmem_limit_bytes=VMEM_BYTES, dimension_semantics=("arbitrary",))
@@ -1159,42 +1175,88 @@
         return pl.BlockSpec(shape, lambda i, *_: zeros)
 
     lanes = width // 128
-    hz, y1, pr, attn, qkv, probs, key, counts = pl.pallas_call(
-        functools.partial(forward_kernel, experts, slots, per_group),
-        grid=(steps,),
-        in_specs=[
-            by_step(1, group_rows, width),
-            by_step(1, group_rows, width),
-            by_step(rows, 3),
-            by_step(per_group, 1, 4 * PAD),
-            whole(2, width, 2 * width + 128),
-        ],
-        out_specs=[
-            by_step(rows, 2 * width),
-            by_step(rows, width),
-            by_step(rows, 128),
-            by_step(rows, width),
-            by_step(per_group, PAD, 3 * width),
-            by_step(per_group, lanes, PAD, 4 * PAD),
-            by_step(rows, 128),
-            whole(1, 128),
-        ],
-        out_shape=[
-            jax.ShapeDtypeStruct((padded, 2 * width), bf16),
-            jax.ShapeDtypeStruct((padded, width), f32),
-            jax.ShapeDtypeStruct((padded, 128), f32),
-            jax.ShapeDtypeStruct((padded, width), bf16),
-            jax.ShapeDtypeStruct((windows, PAD, 3 * width), bf16),
-            jax.ShapeDtypeStruct((windows, lanes, PAD, 4 * PAD), f32),
-            jax.ShapeDtypeStruct((padded, 128), jnp.int32),
-            jax.ShapeDtypeStruct((1, 128), jnp.int32),
-        ],
-        scratch_shapes=[pltpu.VMEM((rows, width), f32), pltpu.VMEM((rows, width), f32), pltpu.VMEM((1, 128), f32)],
-        compiler_params=params,
-        name="attention_forward",
-    )(x3, g3, meta, region_row, w_all)
-
-    key_row = key[:, 0].reshape(1, padded)
+    token_specs = [by_step(1, group_rows, width), by_step(1, group_rows, width), by_step(per_group, 128)]
+    forward_out = [
+        by_step(rows, 2 * width),
+        by_step(rows, width),
+        by_step(rows, 128),
+        by_step(rows, width),
+        by_step(per_group, PAD, 3 * width),
+        by_step(per_group, lanes, PAD, 4 * PAD),
+        by_step(rows, 128),
+        pl.BlockSpec((1, rows), lambda i: (0, i)),
+        whole(1, 128),
+    ]
+    forward_shape = [
+        jax.ShapeDtypeStruct((padded, 2 * width), bf16),
+        jax.ShapeDtypeStruct((padded, width), f32),
+        jax.ShapeDtypeStruct((padded, 128), f32),
+        jax.ShapeDtypeStruct((padded, width), bf16),
+        jax.ShapeDtypeStruct((windows, PAD, 3 * width), bf16),
+        jax.ShapeDtypeStruct((windows, lanes, PAD, 4 * PAD), f32),
+        jax.ShapeDtypeStruct((padded, 128), jnp.int32),
+        jax.ShapeDtypeStruct((1, padded), jnp.int32),
+        jax.ShapeDtypeStruct((1, 128), jnp.int32),
+    ]
+    forward_scratch = [
+        pltpu.VMEM((rows, width), f32),
+        pltpu.VMEM((rows, width), f32),
+        pltpu.VMEM((group_rows, width), f32),
+        pltpu.VMEM((rows, 1), jnp.int32),
+        pltpu.VMEM((per_group, 1, 4 * PAD), jnp.int32),
+        pltpu.VMEM((1, 128), f32),
+    ]
+    body = functools.partial(forward_kernel, dims, experts, slots, per_group, fast)
+    if fast:
+        own = (qkv_weight, proj_weight, router_weight.T, norm_params.T, expert_in, expert_out)
+        *forward, w_all, w_exp = pl.pallas_call(
+            body,
+            grid=(steps,),
+            in_specs=token_specs + [whole(*v.shape) for v in own],
+            out_specs=forward_out + [anywhere, anywhere],
+            out_shape=forward_shape
+            + [
+                jax.ShapeDtypeStruct((2, 2 * depth, shard, 2 * width + 128), bf16),
+                jax.ShapeDtypeStruct((experts, 2, 2 * depth, shard, hidden), bf16),
+            ],
+            scratch_shapes=forward_scratch
+            + [
+                pltpu.VMEM((2, 2 * depth, shard, 2 * width + 128), bf16),
+                pltpu.VMEM((2, shard, 2 * width + 128), bf16),
+                pltpu.VMEM((2, shard, hidden), bf16),
+                pltpu.SemaphoreType.DMA((1,)),
+            ]
+            + SharedGather.semaphores(depth)
+            + Gather.semaphores(depth),
+            compiler_params=remote(0),
+            name="attention_forward",
+        )(x3, g3, combo, *own)
+    else:
+        pack = jnp.concatenate([router_weight, norm_params], axis=1)
+        pack = jnp.pad(pack, ((0, 0), (0, 128 - pack.shape[1])))
+        shared_shard = jnp.stack(
+            [
+                jnp.concatenate([qkv_weight[:, : 2 * width], pack], axis=1),
+                jnp.concatenate([qkv_weight[:, 2 * width :], proj_weight, pack], axis=1),
+            ]
+        ).astype(bf16)
+        expert_shard = jnp.stack([expert_in[0], expert_out[0]]).astype(bf16)
+        w_all = lax.all_gather(shared_shard, "dp", axis=1, tiled=True)
+        w_exp = lax.all_gather(lax.all_gather(expert_shard, "dp", axis=1, tiled=True), "expert", axis=0, tiled=False)
+        forward = pl.pallas_call(
+            body,
+            grid=(steps,),
+            in_specs=token_specs + [whole(*w_all.shape)],
+            out_specs=forward_out,
+            out_shape=forward_shape,
+            scratch_shapes=forward_scratch,
+            compiler_params=params,
+            name="attention_forward",
+        )(x3, g3, combo, w_all)
+    hz, y1, pr, attn, qkv, probs, key, key_row, counts = forward
+    w_all = w_all.reshape(2, width, 2 * width + 128)
+    w_exp = w_exp.reshape(experts, 2, width, hidden)
+
     grads, tok = pl.pallas_call(
         functools.partial(expert_kernel, slots),
         grid_spec=pltpu.PrefetchScalarGridSpec(
@@ -1220,47 +1282,63 @@
         name="experts",
     )(counts[0], hz, key_row, key, w_exp)
 
-    out3, dx3, shared_grad, small_grad = pl.pallas_call(
-        functools.partial(backward_kernel, experts, per_group),
-        grid=(steps,),
-        in_specs=[
-            by_step(1, group_rows, width),
-            by_step(1, group_rows, width),
-            by_step(rows, 3),
-            whole(2, width, 2 * width + 128),
-            by_step(rows, 2 * width),
-            by_step(rows, 2 * width),
-            by_step(rows, width),
-            by_step(rows, 128),
-            by_step(rows, width),
-            by_step(per_group, PAD, 3 * width),
-            by_step(per_group, lanes, PAD, 4 * PAD),
-        ],
-        out_specs=[
-            by_step(1, group_rows, width),
-            by_step(1, group_rows, width),
-            whole(4, width, width),
-            whole(16, width),
-        ],
-        out_shape=[
-            jax.ShapeDtypeStruct((steps, group_rows, width), f32),
-            jax.ShapeDtypeStruct((steps, group_rows, width), f32),
-            jax.ShapeDtypeStruct((4, width, width), bf16),
-            jax.ShapeDtypeStruct((16, width), f32),
-        ],
-        scratch_shapes=[
-            pltpu.VMEM((rows, width), f32),
-            pltpu.VMEM((rows, width), f32),
-            pltpu.VMEM((rows, width), f32),
-            pltpu.VMEM((rows, width), bf16),
-            pltpu.VMEM((3, rows, width), bf16),
-            pltpu.VMEM((4, width, width), f32),
-            pltpu.VMEM((136, width), f32),
-        ],
-        compiler_params=params,
-        name="attention_backward",
-    )(x3, g3, meta, w_all, tok, hz, y1, pr, attn, qkv, probs)
-    block_output = out3.reshape(rows_here, width).astype(bf16)
+    backward_in = (x3, g3, combo, w_all, tok, hz, y1, pr, attn, qkv, probs)
+    backward_specs = token_specs + [
+        whole(*w_all.shape),
+        by_step(rows, 2 * width),
+        by_step(rows, 2 * width),
+        by_step(rows, width),
+        by_step(rows, 128),
+        by_step(rows, width),
+        by_step(per_group, PAD, 3 * width),
+        by_step(per_group, lanes, PAD, 4 * PAD),
+    ]
+    backward_out = [
+        by_step(1, group_rows, width),
+        by_step(1, group_rows, width),
+        whole(4, width, width),
+        whole(16, width),
+    ]
+    backward_shape = [
+        jax.ShapeDtypeStruct((steps, group_rows, width), bf16),
+        jax.ShapeDtypeStruct((steps, group_rows, width), f32),
+        jax.ShapeDtypeStruct((4, width, width), bf16),
+        jax.ShapeDtypeStruct((16, width), f32),
+    ]
+    backward_scratch = [
+        pltpu.VMEM((rows, width), f32),
+        pltpu.VMEM((rows, width), f32),
+        pltpu.VMEM((group_rows, width), f32),
+        pltpu.VMEM((rows, width), f32),
+        pltpu.VMEM((rows, width), bf16),
+        pltpu.VMEM((3, rows, width), bf16),
+        pltpu.VMEM((4, width, width), f32),
+        pltpu.VMEM((136, width), f32),
+    ]
+    body = functools.partial(backward_kernel, dims, experts, per_group, fast)
+    if fast:
+        out3, dx3, shared_grad, small_grad, g_exp = pl.pallas_call(
+            body,
+            grid=(steps,),
+            in_specs=backward_specs + [anywhere],
+            out_specs=backward_out + [whole(2, shard, hidden)],
+            out_shape=backward_shape + [jax.ShapeDtypeStruct((2, shard, hidden), f32)],
+            scratch_shapes=backward_scratch + Scatter.scratch(depth, hidden, shard),
+            compiler_params=remote(1),
+            name="attention_backward",
+        )(*backward_in, grads.reshape(experts, 2, depth, 2, shard, hidden))
+    else:
+        out3, dx3, shared_grad, small_grad = pl.pallas_call(
+            body,
+            grid=(steps,),
+            in_specs=backward_specs,
+            out_specs=backward_out,
+            out_shape=backward_shape,
+            scratch_shapes=backward_scratch,
+            compiler_params=params,
+            name="attention_backward",
+        )(*backward_in)
+    block_output = out3.reshape(rows_here, width)
     input_grad = dx3.reshape(rows_here, width)
 
     weights_now = (qkv_weight, proj_weight, router_weight.T, norm_params.T, expert_in[0], expert_out[0])
@@ -1268,15 +1346,6 @@
     seconds_now = (qkv_second, proj_second, router_second.T, norm_second.T, in_second[0], out_second[0])
     state = (*weights_now, *firsts_now, *seconds_now)
     if fast:
-        g_exp = pl.pallas_call(
-            functools.partial(expert_scatter_kernel, depth),
-            in_specs=[anywhere],
-            out_specs=vmem,
-            out_shape=jax.ShapeDtypeStruct((2, shard, hidden), f32),
-            scratch_shapes=Scatter.scratch(depth, hidden, shard),
-            compiler_params=remote(2),
-            name="expert_scatter",
-        )(grads.reshape(experts, 2, depth, 2, shard, hidden))
         shared, small, norms = pl.pallas_call(
             functools.partial(shared_scatter_kernel, depth, experts),
             in_specs=[vmem] * (3 + len(state)),
@@ -1287,7 +1356,7 @@
                 jax.ShapeDtypeStruct((8, 128), f32),
             ],
             scratch_shapes=shared_scatter_scratch(depth, shard, width),
-            compiler_params=remote(3),
+            compiler_params=remote(2),
             name="shared_scatter",
         )(shared_grad.reshape(2, 2, depth, 2, shard, width), small_grad, g_exp, *state)
     else:
@@ -1314,7 +1383,7 @@
         functools.partial(update_kernel, experts),
         in_specs=[vmem] * (4 + len(state)),
         out_specs=[vmem] * (len(state) + 1),
-        out_shape=[jax.ShapeDtypeStruct(v.shape, f32) for v in weights_now] * 3 + [jax.ShapeDtypeStruct((6, 2), f32)],
+        out_shape=[jax.ShapeDtypeStruct(v.shape, f32) for v in weights_now] * 3 + [jax.ShapeDtypeStruct((2, 6), f32)],
         compiler_params=pltpu.CompilerParams(vmem_limit_bytes=VMEM_BYTES),
         name="lamb_update",
     )(shared, small, g_exp, norms, *state)
@@ -1328,7 +1397,7 @@
         *restore(results[0:6]),
         *restore(results[6:12]),
         *restore(results[12:18]),
-        results[18][None],
+        results[18].T[None],
     )
 
 

time: 294 us -> 199 us (0.68)
  Pallas kernels: 276 us -> 194 us
  other arithmetic: 9.64 us -> 1.43 us
  local copies, waits for them, and re-layouts: 7.29 us -> 2.94 us
    pallas_call x5 -> x2, Pallas kernels: 198 us -> 127 us  [the longest x1 65.3 us: per_device(): pl.pallas_call(body, grid=(steps,), in_specs=token_specs + [whole(*v.shap...]
    pallas_call x1, Pallas kernels: 40 us -> 34.5 us  [per_device(): pl.pallas_call(functools.partial(expert_kernel, slots), grid_spec=pltpu.P...]
    pallas_call x1, Pallas kernels: 33.7 us -> 28.5 us  [per_device(): pl.pallas_call(functools.partial(shared_scatter_kernel, depth, experts),...]
    another operation x8 -> x0, other arithmetic: 4.3 us -> none
where the time goes in v2:
time: 199 us
  Pallas kernels  194 us (97%)
  local copies, waits for them, and re-layouts  2.94 us (1%)
    pallas_call x1, Pallas kernels, per_device(): pl.pallas_call(body, grid=(steps,), in_specs=token_specs + [whole(*v.shap...  65.3 us
    pallas_call x1, Pallas kernels, per_device(): pl.pallas_call(body, grid=(steps,), in_specs=backward_specs + [anywhere],...  61.4 us
    pallas_call x1, Pallas kernels, per_device(): pl.pallas_call(functools.partial(expert_kernel, slots), grid_spec=pltpu.P...  34.5 us
    pallas_call x1, Pallas kernels, per_device(): pl.pallas_call(functools.partial(shared_scatter_kernel, depth, experts),...  28.5 us
    pallas_call x1, Pallas kernels, per_device(): pl.pallas_call(functools.partial(update_kernel, experts), in_specs=[vmem]...  4.21 us

profile of v2, /device:TPU:0, one launch (start us, length us, event | category | flops | bytes accessed | tf_op | source)
XLA Modules:
  0.0 199.1 jit_solution(12460569202717171244)
XLA Ops:
  0.7 0.7 reduce
  1.4 0.7 add_add_fusion
  2.1 0.1 reshape.75
  2.2 0.7 tile.10.refs_2_
  2.9 65.3 %attention_forward.1 = (bf16[1536,768]{1,0:T(8,128)(2,1)}, f32[1536,384]{1,0:T(8,128)}, f32[1536,128]{1,0:T(8,128)}, bf16[1536,384]{1,0:T(8,128)(2,1)}, bf16[24,...) custom-call(bf16[3,392,384]{2,1,0:T(8,128)(2,1)} %bitcast.40, ...), custom_call_target="tpu_custom_call" | custom-call | tf_op jit(solution)/shard_map/attention_forward/pallas_call | solution.py:1212
  68.3 34.5 %experts.1 = (bf16[4,2,384,1536]{3,2,1,0:T(8,128)(2,1)}, f32[1536,768]{1,0:T(8,128)}) custom-call(s32[128]{0:T(128)} %bitcast.72, bf16[1536,768]{1,0:T(8,128)(2,1)} %get-tuple-element.63.hz_ref.refs_5_, s32[1,1536]{1,0:T(1,128)} %get-tuple-element.64.keyrow_ref, s32[1536,128]{1,0:T(8,128)} %get-tuple-element.65.keycol_ref, bf16[4,2,384,1536]{3,2,1,0:T(8,128)(2,1)} %bitcast.37), custom_call_target="tpu_custom_call" | custom-call | tf_op jit(solution)/shard_map/experts/pallas_call | solution.py:1260
  102.8 61.4 %attention_backward.1 = (bf16[3,392,384]{2,1,0:T(8,128)(2,1)}, f32[3,392,384]{2,1,0:T(8,128)}, bf16[4,384,384]{2,1,0:T(8,128)(2,1)}, f32[16,384]{1,0:T(8,128)}, f32[2,48,1536]{2,1,0:T(8,128)}) custom-call(bf16[3,392,384]{2,1,0:T(8,128)(2,1)} %bitcast.41, f32[3,392,384]{2,1,0:T(8,128)} %bitcast.39, s32[24,128]{1,0:T(8,128)} %tile.10.refs_2_, ...), custom_call_target="tpu_custom_call" | custom-call | tf_op jit(solution)/shard_map/attention_backward/pallas_call | solution.py:1320
  164.2 28.5 %shared_scatter.1 = (f32[4,48,384]{2,1,0:T(8,128)}, f32[16,48]{1,0:T(8,128)}, f32[8,128]{1,0:T(8,128)}) custom-call(bf16[2,2,4,2,48,384]{5,4,3,2,1,0:T(8,128)(2,1)} %bitcast.56, f32[16,384]{1,0:T(8,128)} %get-tuple-element.77.refs_1_, f32[2,48,1536]{2,1,0:T(8,128)} %get-tuple-element.78.refs_2_, f32[48,1152]{1,0:T(8,128)} %refs_4_.5, f32[48,384]{1,0:T(8,128)} %refs_5_.1, ...), custom_call_target="tpu_custom_call" | custom-call | tf_op jit(solution)/shard_map/shared_scatter/pallas_call | solution.py:1349
  192.7 0.0 copy-start.1
  192.7 0.0 copy-start
  192.7 4.2 %lamb_update.1 = (f32[48,1152]{1,0:T(8,128)}, f32[48,384]{1,0:T(8,128)}, f32[4,48]{1,0:T(4,128)}, f32[4,48]{1,0:T(4,128)}, f32[48,1536]{1,0:T(8,128)}, /*index=5...) custom-call(f32[4,48,384]{2,1,0:T(8,128)} %get-tuple-element.79.refs, ...), custom_call_target="tpu_custom_call" | custom-call | tf_op jit(solution)/shard_map/lamb_update/pallas_call | solution.py:1382
  196.9 0.0 copy-done.1
  196.9 0.9 copy.46
  197.8 0.0 copy-done
  197.8 1.2 copy.47
  (2 shorter events, 0.0 us)
Async XLA Ops:
  192.7 4.2 %copy-start.1 = (bf16[3,392,384]{2,1,0:T(8,128)(2,1)S(1)}, bf16[3,392,384]{2,1,0:T(8,128)(2,1)}, u32[]{:S(2)}) copy-start(bf16[3,392,384]{2,1,0:T(8,128)(2,1)} %get-tuple-element.74) | copy-start | bytes 2709508
  192.7 5.2 %copy-start = (f32[3,392,384]{2,1,0:T(8,128)S(1)}, f32[3,392,384]{2,1,0:T(8,128)}, u32[]{:S(2)}) copy-start(f32[3,392,384]{2,1,0:T(8,128)} %get-tuple-element.75) | copy-start | bytes 5419012

commit v3 on v2

--- a/solution.py
+++ b/solution.py
@@ -114,11 +114,12 @@
     return ((combo >> 8) & 1).astype(f32)
 
 
-def run_hooks(plan, step, index):
+def run_hooks(plan, step, index, w=None):
     for (k, i), jobs in plan.items():
         if i == index:
-
-            @pl.when(step == k)
+            due = step == k if w is None else (step == k) & (w == i)
+
+            @pl.when(due)
             def _():
                 for job in jobs:
                     job()
@@ -130,9 +131,9 @@
     step = pl.program_id(0)
     if fast:
         x_ref, g_ref, combo_ref, qkv_w, proj_w, router_w, norm_w, in_w, out_w = refs[:9]
-        hz_ref, y1_ref, pr_ref, attn_ref, qkv_ref, p_ref, key_ref, keyrow_ref, count_ref, ws_out, we_ref = refs[9:20]
-        xp, gp, wide, codes, regions, carry, w_ref, sh, ex, ws_sem = refs[20:30]
-        shared_sems, gather_sems = refs[30:37], refs[37:]
+        hz_ref, pr_ref, attn_ref, qkv_ref, p_ref, key_ref, keyrow_ref, count_ref, ws_out, we_ref = refs[9:19]
+        xp, gp, wide, codes, regions, carry, w_ref, sh, ex, ws_sem = refs[19:29]
+        shared_sems, gather_sems = refs[29:36], refs[36:]
         gather = Gather(depth, ex, we_ref, gather_sems)
         shared = SharedGather(depth, sh, w_ref, shared_sems)
 
@@ -161,25 +162,32 @@
             pltpu.make_async_copy(w_ref, ws_out, ws_sem.at[0]).wait()
 
         g = gather
+
+        def first_weights():
+            shared.along_z()
+            gather.turns(0)
+            shared.along_x()
+            store_shared()
+            gather.line(1)
+
         plan = {
-            (0, 0): [enter],
-            (0, 1): [shared.receive, store_shared, lambda: g.turns(0), lambda: g.line(1)],
-            (0, 2): [lambda: g.line(2)],
-            (0, 3): [lambda: g.turns(1)],
-            (0, 4): [lambda: g.line(3)],
-            (1, 2): [lambda: g.turns(2)],
-            (1, 4): [lambda: g.turns(3)],
-            (2, 3): [g.last],
-            (2, 4): [leave],
+            (0, "start"): [enter],
+            (0, "norm"): [first_weights],
+            (0, 7): [lambda: g.line(2)],
+            (0, "end"): [lambda: g.turns(1)],
+            (1, 1): [lambda: g.line(3)],
+            (1, 5): [lambda: g.turns(2)],
+            (2, "qkv"): [lambda: g.turns(3)],
+            (2, "end"): [g.last, leave],
         }
     else:
         x_ref, g_ref, combo_ref, w_ref = refs[:4]
-        hz_ref, y1_ref, pr_ref, attn_ref, qkv_ref, p_ref, key_ref, keyrow_ref, count_ref = refs[4:13]
-        xp, gp, wide, codes, regions, carry = refs[13:19]
+        hz_ref, pr_ref, attn_ref, qkv_ref, p_ref, key_ref, keyrow_ref, count_ref = refs[4:12]
+        xp, gp, wide, codes, regions, carry = refs[12:18]
     rows = per_group * PAD
     width = x_ref.shape[-1]
     groups = width // 128
-    run_hooks(plan, step, 0)
+    run_hooks(plan, step, "start")
     load_windows(x_ref, wide, xp, per_group)
     load_windows(g_ref, wide, gp, per_group)
 
@@ -197,7 +205,7 @@
         regions[k] = jnp.concatenate([flat[k : k + 1, :]] * 2, axis=1)
 
     normed, _ = norm_stats(xp[...])
-    run_hooks(plan, step, 1)
+    run_hooks(plan, step, "norm")
     small = small_part(w_ref)
     small_t = jnp.transpose(small.astype(f32))
     a1, b1, a2, b2 = (small_t[experts + i : experts + i + 1, :] for i in range(4))
@@ -207,7 +215,7 @@
         if part == 0:
             raw = raw * (HEAD_DIM**-0.5)
         qkv_ref[:, :, part * width : (part + 1) * width] = raw.astype(bf16).reshape(per_group, PAD, width)
-    run_hooks(plan, step, 2)
+    run_hooks(plan, step, "qkv")
 
     masks = head_masks()
     key_i = lax.broadcasted_iota(jnp.int32, (PAD, 4 * PAD), 0)
@@ -224,19 +232,17 @@
             s = dot_nt(k, spread_heads(q, masks))
             s = jnp.where(allowed, s, MASKED)
             e = jnp.exp(s - jnp.max(s, axis=0, keepdims=True))
-            p = e * (1.0 / jnp.sum(e, axis=0, keepdims=True))
+            p = (e * (1.0 / jnp.sum(e, axis=0, keepdims=True))).astype(bf16)
             p_ref[w, lg] = p
-            o = dot_tn(p.astype(bf16), v)
+            o = dot_tn(p, v)
             attn_ref[at, lg * 128 : (lg + 1) * 128] = gather_heads(o, masks).astype(bf16)
+        for i in range(per_group):
+            run_hooks(plan, step, i, w)
         return 0
 
-    half = per_group // 2
-    lax.fori_loop(0, half, window, 0)
-    run_hooks(plan, step, 3)
-    lax.fori_loop(half, per_group, window, 0)
+    lax.fori_loop(0, per_group, window, 0)
 
     y1 = xp[...] + dot_nn(attn_ref[...], weight_part(w_ref, 3))
-    y1_ref[...] = y1
     normed2, _ = norm_stats(y1)
     h2 = (normed2 * a2 + b2).astype(bf16)
     lane = lax.broadcasted_iota(jnp.int32, (rows, 128), 1)
@@ -261,24 +267,24 @@
     keyrow_ref[...] = jnp.transpose(key)[0:1, :].astype(jnp.int32)
     carry[...] = carry[...] + jnp.sum(onehot, axis=0, keepdims=True)
     count_ref[...] = carry[...].astype(jnp.int32)
-    run_hooks(plan, step, 4)
-
-
-def expert_kernel(slots, counts_ref, hz_ref, keyrow_ref, keycol_ref, we_ref, grad_ref, tok_ref, acc):
+    run_hooks(plan, step, "end")
+
+
+def expert_kernel(slots, counts_ref, hz_ref, keyrow_ref, keycol_ref, we_ref, grad_ref, tok_ref, acc, tok_acc):
     e = pl.program_id(0)
     width = hz_ref.shape[-1] // 2
     total = hz_ref.shape[0]
 
     @pl.when(e == 0)
     def _():
-        tok_ref[...] = jnp.zeros_like(tok_ref)
+        tok_acc[...] = jnp.zeros_like(tok_acc)
 
     acc[...] = jnp.zeros_like(acc)
     used = counts_ref[e]
 
-    def tile(t, _):
-        base = e * slots + t * TILE
-        pick = keyrow_ref[...] == base + lax.broadcasted_iota(jnp.int32, (TILE, total), 0)
+    def tile(offset, size):
+        base = e * slots + offset
+        pick = keyrow_ref[...] == base + lax.broadcasted_iota(jnp.int32, (size, total), 0)
         both = dot_nn(jnp.where(pick, 1.0, 0.0).astype(bf16), hz_ref[...]).astype(bf16)
         rows, dz = both[:, 0:width], both[:, width : 2 * width]
         up = dot_nn(rows, we_ref[0, 0])
@@ -290,49 +296,108 @@
         back = dot_nt(dup, we_ref[0, 0]).astype(bf16)
         acc[1] += dot_tn(dz, hidden)
         acc[0] += dot_tn(rows, dup)
-        put = jnp.concatenate([keycol_ref[...]] * (TILE // 128), axis=1) == base + lax.broadcasted_iota(jnp.int32, (total, TILE), 1)
-        tok_ref[...] += dot_nn(jnp.where(put, 1.0, 0.0).astype(bf16), jnp.concatenate([ret, back], axis=1))
+        keys = jnp.concatenate([keycol_ref[...]] * (size // 128), axis=1)
+        put = keys == base + lax.broadcasted_iota(jnp.int32, (total, size), 1)
+        tok_acc[...] += dot_nn(jnp.where(put, 1.0, 0.0).astype(bf16), jnp.concatenate([ret, back], axis=1))
+
+    def large(t, _):
+        tile(t * TILE, TILE)
         return 0
 
-    lax.fori_loop(0, (used + TILE - 1) // TILE, tile, 0)
+    count = (used + TILE // 2 - 1) // TILE
+    lax.fori_loop(0, count, large, 0)
+
+    @pl.when(used > count * TILE)
+    def _():
+        tile(count * TILE, TILE // 2)
+
     grad_ref[0] = acc[...].astype(bf16)
+
+    @pl.when(e == pl.num_programs(0) - 1)
+    def _():
+        tok_ref[...] = tok_acc[...].astype(bf16)
 
 
 def backward_kernel(dims, experts, per_group, fast, *refs):
     depth = dims[0] // 2
     plan = {}
     step = pl.program_id(0)
-    x_ref, g_ref, combo_ref, w_ref, tok_ref, hz_ref, y1_ref, pr_ref, attn_ref, qkv_ref, p_ref = refs[:11]
-    refs = refs[11:]
+    combo_ref, sources, refs = refs[0], refs[1:9], refs[9:]
     if fast:
-        ge_ref, out_ref, dx_ref, shared_ref, small_ref, gexp_ref = refs[:6]
-        xp, gp, wide, outp, dattn, dqkv, acc, acc_s = refs[6:14]
-        sc = Scatter(depth, ge_ref, refs[14:19], refs[19:])
+        ge_ref, state_hbm = refs[0], refs[1:19]
+        out_ref, dx_ref, gexp_ref = refs[19:22]
+        results = refs[22:25]
+        refs = refs[25:]
+    else:
+        out_ref, dx_ref, shared_ref, small_ref = refs[:4]
+        refs = refs[4:]
+    xp, gp, wide, outp, dattn, dqkv, acc, acc_s = refs[:8]
+    buffers, in_sem = refs[8:16], refs[16]
+    w_ref = buffers[0]
+    x_all, g_all, tok_all, pr_all, attn_all, qkv_all, p_all = buffers[1:]
+
+    def fetch(i, k):
+        if i == 0:
+            return pltpu.make_async_copy(sources[0], w_ref, in_sem.at[0, 0])
+        return pltpu.make_async_copy(sources[i].at[k], buffers[i].at[k], in_sem.at[i, k])
+
+    def fetch_all():
+        fetch(0, 0).start()
+        for k in range(x_all.shape[0]):
+            for i in range(1, 8):
+                fetch(i, k).start()
+
+    if fast:
+        sc = Scatter(depth, ge_ref, refs[17:22], refs[22:31])
+        state, state_sem, shared_ref, small_ref = refs[31:49], refs[49], refs[50], refs[51]
+
+        def load_state(i):
+            return pltpu.make_async_copy(state_hbm[i], state[i], state_sem.at[i])
 
         def enter():
-            meet(sc.z, sc.x, sc.y, sc.c, depth)
+            meet_all(depth, sc.z, sc.x, sc.y, sc.c)
             sc.begin()
-
-        def leave():
-            sc.third(depth - 1)
+            fetch_all()
+            sc.merge(0)
+
+        def start_state():
+            for i in range(18):
+                load_state(i).start()
+
+        def meanwhile():
             for s in range(2):
                 gexp_ref[s] = sc.result(s)
+            for i in range(18):
+                load_state(i).wait()
+
+        def leave():
+            for part in range(4):
+                shape = shared_ref.shape[2:]
+                shared_ref[part // 2, part % 2] = acc[part].astype(bf16).reshape(shape)
+            small_ref[0:8] = acc_s[0:8]
+            small_ref[8:16] = acc_s[128:136]
+            shared_scatter(
+                depth, experts, meanwhile, (shared_ref, small_ref, gexp_ref), state, results, refs[52:]
+            )
             sc.finish()
 
         plan = {
-            (0, 0): [enter],
-            (0, 1): [lambda: sc.merge(0)],
-            (0, 3): [lambda: sc.second(0), lambda: sc.merge(1)],
-            (1, 1): [lambda: sc.second(1), lambda: sc.third(0), lambda: sc.merge(2)],
-            (2, 0): [lambda: sc.second(2), lambda: sc.third(1), lambda: sc.merge(3)],
-            (2, 3): [lambda: sc.second(3), lambda: sc.third(2)],
-            (2, 4): [leave],
+            (0, "start"): [enter],
+            (0, "pre"): [lambda: sc.merge(1)],
+            (0, 3): [lambda: sc.second(0)],
+            (1, "start"): [lambda: sc.merge(2), lambda: sc.second(1)],
+            (1, "pre"): [lambda: sc.third(0), start_state],
+            (1, 3): [lambda: sc.second(2), lambda: sc.merge(3)],
+            (1, 7): [lambda: sc.third(1)],
+            (2, "start"): [lambda: sc.third(2)],
+            (2, "pre"): [lambda: sc.second(3)],
+            (2, 4): [lambda: sc.third(3)],
+            (2, "end"): [leave],
         }
     else:
-        out_ref, dx_ref, shared_ref, small_ref = refs[:4]
-        xp, gp, wide, outp, dattn, dqkv, acc, acc_s = refs[4:12]
+        plan = {(0, "start"): [fetch_all]}
     rows = per_group * PAD
-    width = x_ref.shape[-1]
+    width = x_all.shape[-1]
     groups = width // 128
     scale = HEAD_DIM**-0.5
 
@@ -341,39 +406,46 @@
         acc[...] = jnp.zeros_like(acc)
         acc_s[...] = jnp.zeros_like(acc_s)
 
-    run_hooks(plan, step, 0)
-    load_windows(x_ref, wide, xp, per_group)
-    load_windows(g_ref, wide, gp, per_group)
+    run_hooks(plan, step, "start")
+
+    @pl.when(step == 0)
+    def _():
+        fetch(0, 0).wait()
+
+    for i in range(1, 8):
+        fetch(i, step).wait()
+    load_windows(x_all.at[pl.ds(step, 1)], wide, xp, per_group)
+    load_windows(g_all.at[pl.ds(step, 1)], wide, gp, per_group)
     combo = token_columns(combo_ref, per_group)
     valid = valid_of(combo)
     route = route_of(combo)
     small = small_part(w_ref)
     small_t = jnp.transpose(small.astype(f32))
     a1, b1, a2, b2 = (small_t[experts + i : experts + i + 1, :] for i in range(4))
-    y1 = y1_ref[...]
+    y1 = xp[...] + dot_nn(attn_all[step], weight_part(w_ref, 3))
     gv = gp[...] * valid
-    z = tok_ref[:, 0:width]
+    z = tok_all[step, :, 0:width].astype(f32)
     lane = lax.broadcasted_iota(jnp.int32, (rows, 128), 1)
     chosen = lane == route
-    pr = pr_ref[...]
+    pr = pr_all[step]
     gate = jnp.sum(jnp.where(chosen, pr, 0.0), axis=-1, keepdims=True)
     outp[...] = y1 + gate * z
     store_windows(outp, wide, out_ref, per_group)
     dgate = jnp.sum(gv * z, axis=-1, keepdims=True)
     kept = jnp.where(lane < experts, jnp.where(chosen, 1.0, 0.0) - pr, 0.0)
     dlogits = (dgate * gate * kept).astype(bf16)
-    h2 = hz_ref[:, 0:width]
+    n2, r2 = norm_stats(y1)
+    h2 = (n2 * a2 + b2).astype(bf16)
     acc_s[0:128] += dot_tn(dlogits, h2)
-    dh2 = dot_nt(dlogits, small) + tok_ref[:, width : 2 * width]
-    n2, r2 = norm_stats(y1)
+    dh2 = dot_nt(dlogits, small) + tok_all[step, :, width : 2 * width].astype(f32)
     acc_s[130:131] += jnp.sum(dh2 * n2, axis=0, keepdims=True)
     acc_s[131:132] += jnp.sum(dh2, axis=0, keepdims=True)
     dy1 = gv + norm_back(dh2, n2, r2, a2)
     gp[...] = dy1
     da = dy1.astype(bf16)
-    acc[3] += dot_tn(attn_ref[...], da)
+    acc[3] += dot_tn(attn_all[step], da)
     dattn[...] = dot_nt(da, weight_part(w_ref, 3)).astype(bf16)
-    run_hooks(plan, step, 1)
+    run_hooks(plan, step, "pre")
 
     masks = head_masks()
 
@@ -381,27 +453,26 @@
         at = pl.ds(pl.multiple_of(w * PAD, PAD), PAD)
         for lg in range(groups):
             cols = slice(lg * 128, (lg + 1) * 128)
-            q = qkv_ref[w, :, lg * 128 : (lg + 1) * 128]
-            k = qkv_ref[w, :, width + lg * 128 : width + (lg + 1) * 128]
-            v = qkv_ref[w, :, 2 * width + lg * 128 : 2 * width + (lg + 1) * 128]
+            q = qkv_all[step, w, :, lg * 128 : (lg + 1) * 128]
+            k = qkv_all[step, w, :, width + lg * 128 : width + (lg + 1) * 128]
+            v = qkv_all[step, w, :, 2 * width + lg * 128 : 2 * width + (lg + 1) * 128]
             d_all = spread_heads(dattn[at, cols], masks)
             q_all = spread_heads(q, masks)
-            p = p_ref[w, lg]
+            p_low = p_all[step, w, lg]
+            p = p_low.astype(f32)
             dp = dot_nt(v, d_all)
             ds = (p * (dp - jnp.sum(dp * p, axis=0, keepdims=True))).astype(bf16)
-            dv = dot_nn(p.astype(bf16), d_all)
+            dv = dot_nn(p_low, d_all)
             dk = dot_nn(ds, q_all)
             dq = gather_heads(dot_tn(ds, k), masks) * scale
             dqkv[0, at, cols] = dq.astype(bf16)
             dqkv[1, at, cols] = dk.astype(bf16)
             dqkv[2, at, cols] = dv.astype(bf16)
+        for i in range(per_group):
+            run_hooks(plan, step, i, w)
         return 0
 
-    half = per_group // 2
-    lax.fori_loop(0, half, window, 0)
-    run_hooks(plan, step, 2)
-    lax.fori_loop(half, per_group, window, 0)
-    run_hooks(plan, step, 3)
+    lax.fori_loop(0, per_group, window, 0)
 
     n1, r1 = norm_stats(xp[...])
     h1 = (n1 * a1 + b1).astype(bf16)
@@ -415,14 +486,16 @@
     outp[...] = gp[...] + norm_back(dh1, n1, r1, a1)
     store_windows(outp, wide, dx_ref, per_group)
 
-    @pl.when(step == pl.num_programs(0) - 1)
-    def _():
-        for part in range(4):
-            shared_ref[part] = acc[part].astype(bf16)
-        small_ref[0:8] = acc_s[0:8]
-        small_ref[8:16] = acc_s[128:136]
-
-    run_hooks(plan, step, 4)
+    if not fast:
+
+        @pl.when(step == pl.num_programs(0) - 1)
+        def _():
+            for part in range(4):
+                shared_ref[part] = acc[part].astype(bf16)
+            small_ref[0:8] = acc_s[0:8]
+            small_ref[8:16] = acc_s[128:136]
+
+    run_hooks(plan, step, "end")
 
 
 def place():
@@ -679,11 +752,13 @@
         self.x_copy(self.z, True).start()
         self.c_copy(self.z, self.x, True).start()
 
-    def receive(self):
+    def along_z(self):
         for zo in self.others():
             self.z_from(zo).wait_recv()
             self.x_copy(zo).start()
             self.c_copy(zo, self.x).start()
+
+    def along_x(self):
         for j in range(self.depth):
             zo = lax.rem(self.z + j, self.depth)
             self.x_copy(zo).wait_recv()
@@ -869,30 +944,32 @@
     return out
 
 
-def shared_scatter_kernel(depth, experts, *refs):
-    (gs_ref, sm_ref, ge_ref), weights, firsts, seconds = refs[:3], refs[3:9], refs[9:15], refs[15:21]
-    fs_ref, gsm_ref, norm_ref = refs[21:24]
-    (t, rc, r1, r2, r3, src_c, src_y, src_x, sz, cur, wide, nb) = refs[24:36]
-    (ccs, ccr, s1, q1, s2, q2, s3, q3, s4, q4, ms, mr, zs, zr, ns, nr) = refs[36:]
+def peers(n, me):
+    return [lax.rem(me + j, n) for j in range(1, n)]
+
+
+def meet_all(depth, z, x, y, c):
+    barrier = pltpu.get_barrier_semaphore()
+    dp, ex = z * 2 + x, y * 2 + c
+    n_dp, n_ex = 2 * depth, 4
+    for other in peers(n_dp, dp):
+        pl.semaphore_signal(barrier, inc=1, device_id=(other, ex), device_id_type=pl.DeviceIdType.MESH)
+    for other in peers(n_ex, ex):
+        pl.semaphore_signal(barrier, inc=1, device_id=(dp, other), device_id_type=pl.DeviceIdType.MESH)
+    pl.semaphore_wait(barrier, n_dp + n_ex - 2)
+
+
+def shared_scatter(depth, experts, meanwhile, operands, state, outputs, scratch):
+    gs_ref, sm_ref, ge_ref = operands
+    weights, firsts, seconds = state[0:6], state[6:12], state[12:18]
+    fs_out, gsm_ref, norm_ref = outputs
+    (t, rc, r1, r2, r3, src_c, src_y, src_x, sz, cur, wide, nb, nq, fs_ref) = scratch[:14]
+    (ccs, ccr, s1, q1, s2, q2, s3, q3, s4, q4, ms, mr, zs, zr, ns, nr, es, er) = scratch[14:]
     z, x, y, c = place()
     dp, ex = z * 2 + x, y * 2 + c
+    n_dp, n_ex = 2 * depth, 4
     shard = fs_ref.shape[1]
     width = fs_ref.shape[2]
-
-    barrier = pltpu.get_barrier_semaphore()
-
-    def greet(device):
-        pl.semaphore_signal(barrier, inc=1, device_id=device, device_id_type=pl.DeviceIdType.MESH)
-
-    def peers(n, me):
-        return [lax.rem(me + j, n) for j in range(1, n)]
-
-    n_dp, n_ex = 2 * depth, 4
-    for other in peers(n_dp, dp):
-        greet((other, ex))
-    for other in peers(n_ex, ex):
-        greet((dp, other))
-    pl.semaphore_wait(barrier, n_dp + n_ex - 2)
 
     near = [at(z, x, y, 1 - c), at(z, x, 1 - y, c), at(z, 1 - x, y, c)]
     y_of = [y, 1 - y]
@@ -932,6 +1009,7 @@
     small_hop(0).start()
     core(1).start()
     core(0).start()
+    meanwhile()
     totals = row_norms([w[...] for w in weights], 0)
     for i in range(2):
         direction = lamb_parts(weights[4 + i][...], ge_ref[i], firsts[4 + i][...], seconds[4 + i][...])[2]
@@ -988,6 +1066,23 @@
     def four_from(e):
         return push(fs_ref.at[e], fs_ref.at[e], s4.at[e], q4.at[e], (dp, e))
 
+    def quarter(e):
+        return push(nq.at[ex], nq.at[ex], es.at[e], er.at[ex], (dp, e))
+
+    def quarter_from(e):
+        return push(nq.at[e], nq.at[e], es.at[e], er.at[e], (dp, e))
+
+    def part_of(refs):
+        out = refs[1][...]
+        for p in range(3):
+            out = jnp.where(ex == p, refs[0][:, p * width : (p + 1) * width], out)
+        return out
+
+    direction = lamb_parts(part_of(weights), total, part_of(firsts), part_of(seconds))[2]
+    lane = lax.broadcasted_iota(jnp.int32, (8, 128), 1)
+    nq[ex] = jnp.where(lane == jnp.where(ex == 3, 7, 6), jnp.sum(direction * direction), 0.0)
+    for e in peers(n_ex, ex):
+        quarter(e).start()
     for e in peers(n_ex, ex):
         four(e).start()
     for zo in peers(depth, z):
@@ -1002,13 +1097,11 @@
         direction = lamb_parts(weights[i][...], g, firsts[i][...], seconds[i][...])[2]
         totals = totals + row_norms([direction], 6 + i)
     for e in peers(n_ex, ex):
-        four_from(e).wait_recv()
-    for part in range(4):
-        i = 1 if part == 3 else 0
-        cols = slice(0, width) if part == 3 else slice(part * width, (part + 1) * width)
-        direction = lamb_parts(weights[i][:, cols], fs_ref[part], firsts[i][:, cols], seconds[i][:, cols])[2]
-        totals = totals + row_norms([direction], 6 + i)
-    nb[dp] = jnp.broadcast_to(totals, (8, 128))
+        quarter_from(e).wait_recv()
+    combined = jnp.broadcast_to(totals, (8, 128))
+    for e in range(n_ex):
+        combined = combined + nq[e]
+    nb[dp] = combined
 
     def norm_push(r):
         return push(nb.at[dp], nb.at[dp], ns.at[r], nr.at[dp], (r, ex))
@@ -1018,12 +1111,17 @@
 
     for r in peers(n_dp, dp):
         norm_push(r).start()
+    for e in peers(n_ex, ex):
+        four_from(e).wait_recv()
+    fs_out[...] = fs_ref[...]
     for r in peers(n_dp, dp):
         norm_from(r).wait_recv()
     summed = nb[0]
     for r in range(1, n_dp):
         summed = summed + nb[r]
     norm_ref[...] = summed
+    for e in peers(n_ex, ex):
+        quarter(e).wait_send()
 
     for r in peers(n_dp, dp):
         norm_push(r).wait_send()
@@ -1059,6 +1157,8 @@
         pltpu.VMEM((3, 16, width), f32),
         pltpu.VMEM((width, 128), f32),
         pltpu.VMEM((2 * depth, 8, 128), f32),
+        pltpu.VMEM((4, 8, 128), f32),
+        pltpu.VMEM((4, shard, width), f32),
         dma((2,)),
         dma((2,)),
         dma((depth, 2)),
@@ -1075,6 +1175,8 @@
         dma((depth,)),
         dma((2 * depth,)),
         dma((2 * depth,)),
+        dma((4,)),
+        dma((4,)),
     ]
 
 
@@ -1178,7 +1280,6 @@
     token_specs = [by_step(1, group_rows, width), by_step(1, group_rows, width), by_step(per_group, 128)]
     forward_out = [
         by_step(rows, 2 * width),
-        by_step(rows, width),
         by_step(rows, 128),
         by_step(rows, width),
         by_step(per_group, PAD, 3 * width),
@@ -1189,11 +1290,10 @@
     ]
     forward_shape = [
         jax.ShapeDtypeStruct((padded, 2 * width), bf16),
-        jax.ShapeDtypeStruct((padded, width), f32),
         jax.ShapeDtypeStruct((padded, 128), f32),
         jax.ShapeDtypeStruct((padded, width), bf16),
         jax.ShapeDtypeStruct((windows, PAD, 3 * width), bf16),
-        jax.ShapeDtypeStruct((windows, lanes, PAD, 4 * PAD), f32),
+        jax.ShapeDtypeStruct((windows, lanes, PAD, 4 * PAD), bf16),
         jax.ShapeDtypeStruct((padded, 128), jnp.int32),
         jax.ShapeDtypeStruct((1, padded), jnp.int32),
         jax.ShapeDtypeStruct((1, 128), jnp.int32),
@@ -1253,7 +1353,7 @@
             compiler_params=params,
             name="attention_forward",
         )(x3, g3, combo, w_all)
-    hz, y1, pr, attn, qkv, probs, key, key_row, counts = forward
+    hz, pr, attn, qkv, probs, key, key_row, counts = forward
     w_all = w_all.reshape(2, width, 2 * width + 128)
     w_exp = w_exp.reshape(experts, 2, width, hidden)
 
@@ -1272,27 +1372,28 @@
                 pl.BlockSpec((1, 2, width, hidden), lambda e, *_: (e, 0, 0, 0)),
                 whole(padded, 2 * width),
             ],
-            scratch_shapes=[pltpu.VMEM((2, width, hidden), f32)],
+            scratch_shapes=[pltpu.VMEM((2, width, hidden), f32), pltpu.VMEM((padded, 2 * width), f32)],
         ),
         out_shape=[
             jax.ShapeDtypeStruct((experts, 2, width, hidden), bf16),
-            jax.ShapeDtypeStruct((padded, 2 * width), f32),
+            jax.ShapeDtypeStruct((padded, 2 * width), bf16),
         ],
         compiler_params=params,
         name="experts",
     )(counts[0], hz, key_row, key, w_exp)
 
-    backward_in = (x3, g3, combo, w_all, tok, hz, y1, pr, attn, qkv, probs)
-    backward_specs = token_specs + [
-        whole(*w_all.shape),
-        by_step(rows, 2 * width),
-        by_step(rows, 2 * width),
-        by_step(rows, width),
-        by_step(rows, 128),
-        by_step(rows, width),
-        by_step(per_group, PAD, 3 * width),
-        by_step(per_group, lanes, PAD, 4 * PAD),
-    ]
+    staged = (
+        w_all,
+        x3,
+        g3,
+        tok.reshape(steps, rows, 2 * width),
+        pr.reshape(steps, rows, 128),
+        attn.reshape(steps, rows, width),
+        qkv.reshape(steps, per_group, PAD, 3 * width),
+        probs.reshape(steps, per_group, lanes, PAD, 4 * PAD),
+    )
+    backward_in = (combo, *staged)
+    backward_specs = [by_step(per_group, 128)] + [anywhere] * len(staged)
     backward_out = [
         by_step(1, group_rows, width),
         by_step(1, group_rows, width),
@@ -1314,19 +1415,39 @@
         pltpu.VMEM((3, rows, width), bf16),
         pltpu.VMEM((4, width, width), f32),
         pltpu.VMEM((136, width), f32),
+        *[pltpu.VMEM(v.shape, v.dtype) for v in staged],
+        pltpu.SemaphoreType.DMA((8, steps)),
     ]
+    weights_now = (qkv_weight, proj_weight, router_weight.T, norm_params.T, expert_in[0], expert_out[0])
+    firsts_now = (qkv_first, proj_first, router_first.T, norm_first.T, in_first[0], out_first[0])
+    seconds_now = (qkv_second, proj_second, router_second.T, norm_second.T, in_second[0], out_second[0])
+    state = (*weights_now, *firsts_now, *seconds_now)
     body = functools.partial(backward_kernel, dims, experts, per_group, fast)
     if fast:
-        out3, dx3, shared_grad, small_grad, g_exp = pl.pallas_call(
+        finals = [
+            jax.ShapeDtypeStruct((2, shard, hidden), f32),
+            jax.ShapeDtypeStruct((4, shard, width), f32),
+            jax.ShapeDtypeStruct((16, shard), f32),
+            jax.ShapeDtypeStruct((8, 128), f32),
+        ]
+        out3, dx3, g_exp, shared, small, norms = pl.pallas_call(
             body,
             grid=(steps,),
-            in_specs=backward_specs + [anywhere],
-            out_specs=backward_out + [whole(2, shard, hidden)],
-            out_shape=backward_shape + [jax.ShapeDtypeStruct((2, shard, hidden), f32)],
-            scratch_shapes=backward_scratch + Scatter.scratch(depth, hidden, shard),
+            in_specs=backward_specs + [anywhere] * (1 + len(state)),
+            out_specs=backward_out[:2] + [whole(*v.shape) for v in finals],
+            out_shape=backward_shape[:2] + finals,
+            scratch_shapes=backward_scratch
+            + Scatter.scratch(depth, hidden, shard)
+            + [pltpu.VMEM(v.shape, v.dtype) for v in state]
+            + [
+                pltpu.SemaphoreType.DMA((len(state),)),
+                pltpu.VMEM((2, 2, depth, 2, shard, width), bf16),
+                pltpu.VMEM((16, width), f32),
+            ]
+            + shared_scatter_scratch(depth, shard, width),
             compiler_params=remote(1),
             name="attention_backward",
-        )(*backward_in, grads.reshape(experts, 2, depth, 2, shard, hidden))
+        )(*backward_in, grads.reshape(experts, 2, depth, 2, shard, hidden), *state)
     else:
         out3, dx3, shared_grad, small_grad = pl.pallas_call(
             body,
@@ -1341,25 +1462,7 @@
     block_output = out3.reshape(rows_here, width)
     input_grad = dx3.reshape(rows_here, width)
 
-    weights_now = (qkv_weight, proj_weight, router_weight.T, norm_params.T, expert_in[0], expert_out[0])
-    firsts_now = (qkv_first, proj_first, router_first.T, norm_first.T, in_first[0], out_first[0])
-    seconds_now = (qkv_second, proj_second, router_second.T, norm_second.T, in_second[0], out_second[0])
-    state = (*weights_now, *firsts_now, *seconds_now)
-    if fast:
-        shared, small, norms = pl.pallas_call(
-            functools.partial(shared_scatter_kernel, depth, experts),
-            in_specs=[vmem] * (3 + len(state)),
-            out_specs=[vmem] * 3,
-            out_shape=[
-                jax.ShapeDtypeStruct((4, shard, width), f32),
-                jax.ShapeDtypeStruct((16, shard), f32),
-                jax.ShapeDtypeStruct((8, 128), f32),
-            ],
-            scratch_shapes=shared_scatter_scratch(depth, shard, width),
-            compiler_params=remote(2),
-            name="shared_scatter",
-        )(shared_grad.reshape(2, 2, depth, 2, shard, width), small_grad, g_exp, *state)
-    else:
+    if not fast:
         shared = lax.psum(shared_grad.astype(f32), ("expert", "dp"))
         small = lax.psum(small_grad, ("expert", "dp"))
         g_exp = lax.psum(grads.astype(f32), ("expert", "dp"))

time: 199 us -> 184 us (0.925)
  Pallas kernels: 194 us -> 179 us
    pallas_call x2 -> x1, Pallas kernels: 89.9 us -> 79.1 us  [per_device(): pl.pallas_call(body, grid=(steps,), in_specs=backward_specs + [anywhere]...]
    pallas_call x1, Pallas kernels: 34.5 us -> 32 us  [per_device(): pl.pallas_call(functools.partial(expert_kernel, slots), grid_spec=pltpu.P...]
where the time goes in v3:
time: 184 us
  Pallas kernels  179 us (97%)
  local copies, waits for them, and re-layouts  2.94 us (2%)
    pallas_call x1, Pallas kernels, per_device(): pl.pallas_call(body, grid=(steps,), in_specs=backward_specs + [anywhere]...  79.1 us
    pallas_call x1, Pallas kernels, per_device(): pl.pallas_call(body, grid=(steps,), in_specs=token_specs + [whole(*v.shap...  64 us
    pallas_call x1, Pallas kernels, per_device(): pl.pallas_call(functools.partial(expert_kernel, slots), grid_spec=pltpu.P...  32 us
    pallas_call x1, Pallas kernels, per_device(): pl.pallas_call(functools.partial(update_kernel, experts), in_specs=[vmem]...  4.21 us

profile of v3, /device:TPU:0, one launch (start us, length us, event | category | flops | bytes accessed | tf_op | source)
XLA Modules:
  0.0 184.3 jit_solution(2420436460212365114)
XLA Ops:
  0.7 0.7 reduce
  1.4 0.7 add_add_fusion
  2.1 0.1 reshape.85
  2.2 0.7 tile.10.refs_2_.refs_0_
  2.9 64.0 %attention_forward.1 = (bf16[1536,768]{1,0:T(8,128)(2,1)}, f32[1536,128]{1,0:T(8,128)}, bf16[1536,384]{1,0:T(8,128)(2,1)}, bf16[24,64,1152]{2,1,0:T(8,128)(2,1)}...) custom-call(bf16[3,392,384]{2,1,0:T(8,128)(2,1)} %bitcast.44, ...), custom_call_target="tpu_custom_call" | custom-call | tf_op jit(solution)/shard_map/attention_forward/pallas_call | solution.py:1312
  66.9 32.0 %experts.1 = (bf16[4,2,384,1536]{3,2,1,0:T(8,128)(2,1)}, bf16[1536,768]{1,0:T(8,128)(2,1)}) custom-call(s32[128]{0:T(128)} %bitcast.80, bf16[1536,768]{1,0:T(8,128)(2,1)} %get-tuple-element.60.hz_ref, s32[1,1536]{1,0:T(1,128)} %get-tuple-element.61.keyrow_ref, s32[1536,128]{1,0:T(8,128)} %get-tuple-element.62.keycol_ref, bf16[4,2,384,1536]{3,2,1,0:T(8,128)(2,1)} %bitcast.40), custom_call_target="tpu_custom_call" | custom-call | tf_op jit(solution)/shard_map/experts/pallas_call | solution.py:1360
  98.9 79.1 %attention_backward.1 = (bf16[3,392,384]{2,1,0:T(8,128)(2,1)}, f32[3,392,384]{2,1,0:T(8,128)}, f32[2,48,1536]{2,1,0:T(8,128)}, f32[4,48,384]{2,1,0:T(8,128)}, f32[16,48]{1,0:T(8,128)}, /*index=5*/f32[8,128]{1,0:T(8,128)}) custom-call(s32[24,128]{1,0:T(8,128)} %tile.10.refs_2_.refs_0_, bf16[2,384,896]{2,1,0:T(8,128)(2,1)} %bitcast.54, ...), custom_call_target="tpu_custom_call" | custom-call | tf_op jit(solution)/shard_map/attention_backward/pallas_call | solution.py:1433
  177.9 0.0 copy-start.1
  178.0 0.0 copy-start
  178.0 4.2 %lamb_update.1 = (f32[48,1152]{1,0:T(8,128)}, f32[48,384]{1,0:T(8,128)}, f32[4,48]{1,0:T(4,128)}, f32[4,48]{1,0:T(4,128)}, f32[48,1536]{1,0:T(8,128)}, /*index=5...) custom-call(f32[4,48,384]{2,1,0:T(8,128)} %get-tuple-element.72.refs, ...), custom_call_target="tpu_custom_call" | custom-call | tf_op jit(solution)/shard_map/lamb_update/pallas_call | solution.py:1485
  182.2 0.0 copy-done.1
  182.2 0.9 copy.46
  183.1 0.0 copy-done
  183.1 1.2 copy.47
  (2 shorter events, 0.0 us)
Async XLA Ops:
  177.9 4.2 %copy-start.1 = (bf16[3,392,384]{2,1,0:T(8,128)(2,1)S(1)}, bf16[3,392,384]{2,1,0:T(8,128)(2,1)}, u32[]{:S(2)}) copy-start(bf16[3,392,384]{2,1,0:T(8,128)(2,1)} %get-tuple-element.70) | copy-start | bytes 2709508
  178.0 5.2 %copy-start = (f32[3,392,384]{2,1,0:T(8,128)S(1)}, f32[3,392,384]{2,1,0:T(8,128)}, u32[]{:S(2)}) copy-start(f32[3,392,384]{2,1,0:T(8,128)} %get-tuple-element.71) | copy-start | bytes 5419012

commit v4 on v3

--- a/solution.py
+++ b/solution.py
@@ -13,6 +13,7 @@
 PAD = 64
 STEP = 5
 TILE = 256
+GROUP = 4
 NORM_EPS = 1e-05
 MASKED = -1e30
 BETA_ONE = 0.9
@@ -130,10 +131,11 @@
     plan = {}
     step = pl.program_id(0)
     if fast:
-        x_ref, g_ref, combo_ref, qkv_w, proj_w, router_w, norm_w, in_w, out_w = refs[:9]
-        hz_ref, pr_ref, attn_ref, qkv_ref, p_ref, key_ref, keyrow_ref, count_ref, ws_out, we_ref = refs[9:19]
-        xp, gp, wide, codes, regions, carry, w_ref, sh, ex, ws_sem = refs[19:29]
-        shared_sems, gather_sems = refs[29:36], refs[36:]
+        x_ref, g_ref, *token_rows = refs[:5]
+        qkv_w, proj_w, router_w, norm_w, in_w, out_w = refs[5:11]
+        hz_ref, pr_ref, attn_ref, qkv_ref, p_ref, key_ref, keyrow_ref, count_ref, combo_ref, ws_out, we_ref = refs[11:22]
+        combos, xp, gp, wide, codes, regions, carry, w_ref, sh, ex, ws_sem = refs[22:33]
+        shared_sems, gather_sems = refs[33:40], refs[40:]
         gather = Gather(depth, ex, we_ref, gather_sems)
         shared = SharedGather(depth, sh, w_ref, shared_sems)
 
@@ -175,15 +177,16 @@
             (0, "norm"): [first_weights],
             (0, 7): [lambda: g.line(2)],
             (0, "end"): [lambda: g.turns(1)],
-            (1, 1): [lambda: g.line(3)],
-            (1, 5): [lambda: g.turns(2)],
+            (1, 3): [lambda: g.line(3)],
+            (1, 7): [lambda: g.turns(2)],
             (2, "qkv"): [lambda: g.turns(3)],
             (2, "end"): [g.last, leave],
         }
     else:
-        x_ref, g_ref, combo_ref, w_ref = refs[:4]
-        hz_ref, pr_ref, attn_ref, qkv_ref, p_ref, key_ref, keyrow_ref, count_ref = refs[4:12]
-        xp, gp, wide, codes, regions, carry = refs[12:18]
+        x_ref, g_ref, *token_rows = refs[:5]
+        w_ref = refs[5]
+        hz_ref, pr_ref, attn_ref, qkv_ref, p_ref, key_ref, keyrow_ref, count_ref, combo_ref = refs[6:15]
+        combos, xp, gp, wide, codes, regions, carry = refs[15:22]
     rows = per_group * PAD
     width = x_ref.shape[-1]
     groups = width // 128
@@ -194,7 +197,14 @@
     @pl.when(step == 0)
     def _():
         carry[...] = jnp.zeros_like(carry)
-
+        packed = (16 * token_rows[1][...] + 256 * token_rows[2][...] + 512).reshape(1, -1) + token_rows[0][...]
+        combos[...] = jnp.zeros_like(combos)
+        for k in range(combos.shape[0]):
+            piece = packed[:, k * WINDOW : (k + 1) * WINDOW]
+            combos[k : k + 1, 0:WINDOW] = piece
+            combos[k : k + 1, PAD : PAD + WINDOW] = piece
+
+    combo_ref[...] = combos[pl.ds(pl.multiple_of(step * per_group, per_group), per_group), :]
     combo = token_columns(combo_ref, per_group)
     valid = valid_of(combo)
     route = route_of(combo)
@@ -222,7 +232,7 @@
     lane_i = lax.broadcasted_iota(jnp.int32, (PAD, 4 * PAD), 1)
     diagonal = key_i == lax.rem(lane_i, PAD)
 
-    def window(w, _):
+    def window(w):
         at = pl.ds(pl.multiple_of(w * PAD, PAD), PAD)
         allowed = (codes[at, :] == regions[w]) | diagonal
         for lg in range(groups):
@@ -236,11 +246,15 @@
             p_ref[w, lg] = p
             o = dot_tn(p, v)
             attn_ref[at, lg * 128 : (lg + 1) * 128] = gather_heads(o, masks).astype(bf16)
+
+    def windows(j, _):
+        for k in range(GROUP):
+            window(j * GROUP + k)
         for i in range(per_group):
-            run_hooks(plan, step, i, w)
+            run_hooks(plan, step, i, j * GROUP + GROUP - 1)
         return 0
 
-    lax.fori_loop(0, per_group, window, 0)
+    lax.fori_loop(0, per_group // GROUP, windows, 0)
 
     y1 = xp[...] + dot_nn(attn_ref[...], weight_part(w_ref, 3))
     normed2, _ = norm_stats(y1)
@@ -364,6 +378,13 @@
             for i in range(18):
                 load_state(i).start()
 
+        def early():
+            sc.second(depth - 1)
+            sc.third(depth - 2)
+
+        def middle():
+            sc.third(depth - 1)
+
         def meanwhile():
             for s in range(2):
                 gexp_ref[s] = sc.result(s)
@@ -377,21 +398,19 @@
             small_ref[0:8] = acc_s[0:8]
             small_ref[8:16] = acc_s[128:136]
             shared_scatter(
-                depth, experts, meanwhile, (shared_ref, small_ref, gexp_ref), state, results, refs[52:]
+                depth, experts, early, middle, meanwhile, (shared_ref, small_ref, gexp_ref), state, results, refs[52:]
             )
             sc.finish()
 
         plan = {
             (0, "start"): [enter],
             (0, "pre"): [lambda: sc.merge(1)],
-            (0, 3): [lambda: sc.second(0)],
-            (1, "start"): [lambda: sc.merge(2), lambda: sc.second(1)],
-            (1, "pre"): [lambda: sc.third(0), start_state],
-            (1, 3): [lambda: sc.second(2), lambda: sc.merge(3)],
-            (1, 7): [lambda: sc.third(1)],
-            (2, "start"): [lambda: sc.third(2)],
-            (2, "pre"): [lambda: sc.second(3)],
-            (2, 4): [lambda: sc.third(3)],
+            (0, 7): [lambda: sc.second(0)],
+            (1, "start"): [lambda: sc.merge(2)],
+            (1, "pre"): [lambda: sc.second(1), start_state],
+            (1, 3): [lambda: sc.merge(3), lambda: sc.third(0)],
+            (1, "end"): [lambda: sc.second(2)],
+            (2, "pre"): [lambda: sc.third(1)],
             (2, "end"): [leave],
         }
     else:
@@ -449,7 +468,7 @@
 
     masks = head_masks()
 
-    def window(w, _):
+    def window(w):
         at = pl.ds(pl.multiple_of(w * PAD, PAD), PAD)
         for lg in range(groups):
             cols = slice(lg * 128, (lg + 1) * 128)
@@ -468,11 +487,15 @@
             dqkv[0, at, cols] = dq.astype(bf16)
             dqkv[1, at, cols] = dk.astype(bf16)
             dqkv[2, at, cols] = dv.astype(bf16)
+
+    def windows(j, _):
+        for k in range(GROUP):
+            window(j * GROUP + k)
         for i in range(per_group):
-            run_hooks(plan, step, i, w)
+            run_hooks(plan, step, i, j * GROUP + GROUP - 1)
         return 0
 
-    lax.fori_loop(0, per_group, window, 0)
+    lax.fori_loop(0, per_group // GROUP, windows, 0)
 
     n1, r1 = norm_stats(xp[...])
     h1 = (n1 * a1 + b1).astype(bf16)
@@ -959,7 +982,7 @@
     pl.semaphore_wait(barrier, n_dp + n_ex - 2)
 
 
-def shared_scatter(depth, experts, meanwhile, operands, state, outputs, scratch):
+def shared_scatter(depth, experts, early, middle, meanwhile, operands, state, outputs, scratch):
     gs_ref, sm_ref, ge_ref = operands
     weights, firsts, seconds = state[0:6], state[6:12], state[12:18]
     fs_out, gsm_ref, norm_ref = outputs
@@ -977,13 +1000,17 @@
     def core(i):
         return push(gs_ref.at[y_of[i], 1 - c], rc.at[i], ccs.at[i], ccr.at[i], near[0])
 
-    def one(zo, k):
-        if zo % 2 == 0:
+    order = [lax.rem(z + 1 + j, depth) for j in range(depth)]
+
+    def one(j, k):
+        zo = order[j]
+        if j % 2 == 0:
             return push(t.at[1, zo, k], r1.at[zo, k], s1.at[zo, k], q1.at[zo, k], near[1])
         return push(t.at[k, zo, 1 - x], r1.at[zo, k], s1.at[zo, k], q1.at[zo, k], near[2])
 
-    def two(zo):
-        if zo % 2 == 0:
+    def two(j):
+        zo = order[j]
+        if j % 2 == 0:
             return push(t.at[0, zo, 1 - x], r2.at[zo], s2.at[zo], q2.at[zo], near[2])
         return push(t.at[1, zo, x], r2.at[zo], s2.at[zo], q2.at[zo], near[1])
 
@@ -1009,34 +1036,31 @@
     small_hop(0).start()
     core(1).start()
     core(0).start()
-    meanwhile()
-    totals = row_norms([w[...] for w in weights], 0)
-    for i in range(2):
-        direction = lamb_parts(weights[4 + i][...], ge_ref[i], firsts[4 + i][...], seconds[4 + i][...])[2]
-        totals = totals + row_norms([direction], 10 + i)
+    early()
     small_hop(0).wait_recv()
     cur[0] = sm_ref[...] + src_c[...]
     small_hop(1).start()
     for i in (1, 0):
         core(i).wait_recv()
-        for zo in range(depth):
+        for j, zo in enumerate(order):
             for k in range(2):
                 fold(t.at[i, zo, k], gs_ref.at[y_of[i], c, zo, k], rc.at[i, zo, k])
-            if zo % 2 == 0:
+            if j % 2 == 0:
                 if i == 1:
-                    one(zo, 0).start()
-                    one(zo, 1).start()
+                    one(j, 0).start()
+                    one(j, 1).start()
             else:
-                one(zo, i).start()
+                one(j, i).start()
+    middle()
     small_hop(1).wait_recv()
     cur[1] = cur[0] + src_y[...]
     small_hop(2).start()
-    for zo in range(depth):
+    for j, zo in enumerate(order):
         for k in range(2):
-            one(zo, k).wait_recv()
-            target = t.at[0, zo, k] if zo % 2 == 0 else t.at[k, zo, x]
+            one(j, k).wait_recv()
+            target = t.at[0, zo, k] if j % 2 == 0 else t.at[k, zo, x]
             fold(target, target, r1.at[zo, k])
-        two(zo).start()
+        two(j).start()
     small_hop(2).wait_recv()
     cur[2] = cur[1] + src_x[...]
     sz[z] = cur[2]
@@ -1045,15 +1069,18 @@
         def _():
             small_z(zo).start()
 
-    for zo in range(depth):
-        two(zo).wait_recv()
+    for j, zo in enumerate(order):
+        two(j).wait_recv()
         target = t.at[0, zo, x]
         fold(target, target, r2.at[zo])
-
-        @pl.when(zo != z)
-        def _():
+        if j < depth - 1:
             three(zo).start()
 
+    meanwhile()
+    totals = row_norms([w[...] for w in weights], 0)
+    for i in range(2):
+        direction = lamb_parts(weights[4 + i][...], ge_ref[i], firsts[4 + i][...], seconds[4 + i][...])[2]
+        totals = totals + row_norms([direction], 10 + i)
     total = t[0, z, x].astype(f32)
     for zo in peers(depth, z):
         arrived(zo).wait_recv()
@@ -1131,13 +1158,11 @@
         core(i).wait_send()
     for k in range(3):
         small_hop(k).wait_send()
-    for zo in range(depth):
+    for j, zo in enumerate(order):
         for k in range(2):
-            one(zo, k).wait_send()
-        two(zo).wait_send()
-
-        @pl.when(zo != z)
-        def _():
+            one(j, k).wait_send()
+        two(j).wait_send()
+        if j < depth - 1:
             three(zo).wait_send()
             small_z(zo).wait_send()
 
@@ -1262,8 +1287,7 @@
 
     x3 = tokens.reshape(steps, group_rows, width)
     g3 = cotangent.reshape(steps, group_rows, width)
-    combo = (routes[:, 0] + 16 * shift_region + 256 * valid_mask + 512).reshape(windows, WINDOW)
-    combo = jnp.tile(jnp.pad(combo, ((0, 0), (0, PAD - WINDOW))), (1, 2))
+    token_rows = (routes.reshape(1, rows_here), shift_region, valid_mask)
 
     rows = per_group * PAD
     params = pltpu.CompilerParams(vmem_limit_bytes=VMEM_BYTES, dimension_semantics=("arbitrary",))
@@ -1277,7 +1301,7 @@
         return pl.BlockSpec(shape, lambda i, *_: zeros)
 
     lanes = width // 128
-    token_specs = [by_step(1, group_rows, width), by_step(1, group_rows, width), by_step(per_group, 128)]
+    token_specs = [by_step(1, group_rows, width), by_step(1, group_rows, width)] + [whole(1, rows_here), whole(rows_here), whole(rows_here)]
     forward_out = [
         by_step(rows, 2 * width),
         by_step(rows, 128),
@@ -1287,6 +1311,7 @@
         by_step(rows, 128),
         pl.BlockSpec((1, rows), lambda i: (0, i)),
         whole(1, 128),
+        by_step(per_group, 128),
     ]
     forward_shape = [
         jax.ShapeDtypeStruct((padded, 2 * width), bf16),
@@ -1297,8 +1322,10 @@
         jax.ShapeDtypeStruct((padded, 128), jnp.int32),
         jax.ShapeDtypeStruct((1, padded), jnp.int32),
         jax.ShapeDtypeStruct((1, 128), jnp.int32),
+        jax.ShapeDtypeStruct((windows, 128), jnp.int32),
     ]
     forward_scratch = [
+        pltpu.VMEM((windows, 128), jnp.int32),
         pltpu.VMEM((rows, width), f32),
         pltpu.VMEM((rows, width), f32),
         pltpu.VMEM((group_rows, width), f32),
@@ -1330,7 +1357,7 @@
             + Gather.semaphores(depth),
             compiler_params=remote(0),
             name="attention_forward",
-        )(x3, g3, combo, *own)
+        )(x3, g3, *token_rows, *own)
     else:
         pack = jnp.concatenate([router_weight, norm_params], axis=1)
         pack = jnp.pad(pack, ((0, 0), (0, 128 - pack.shape[1])))
@@ -1352,8 +1379,8 @@
             scratch_shapes=forward_scratch,
             compiler_params=params,
             name="attention_forward",
-        )(x3, g3, combo, w_all)
-    hz, pr, attn, qkv, probs, key, key_row, counts = forward
+        )(x3, g3, *token_rows, w_all)
+    hz, pr, attn, qkv, probs, key, key_row, counts, combo = forward
     w_all = w_all.reshape(2, width, 2 * width + 128)
     w_exp = w_exp.reshape(experts, 2, width, hidden)
 
@@ -1482,14 +1509,25 @@
         steps_now = [lamb_parts(*entry)[2] for entry in zip(weights_now, reduced, firsts_now, seconds_now)]
         sums = jnp.stack([jnp.sum(v * v) for v in (*weights_now, *steps_now)])
         norms = jnp.broadcast_to(jnp.pad(lax.psum(sums, "dp"), (0, 128 - 12)), (8, 128))
+    cuts, part = 1, shard
+
+    def rows_of(v):
+        if v.shape[-2] != shard:
+            return whole(*v.shape)
+        lead = v.shape[:-2]
+        return pl.BlockSpec((*lead, part, v.shape[-1]), lambda i: (0,) * len(lead) + (i, 0))
+
+    grads_now = (shared, small, g_exp, norms)
     results = pl.pallas_call(
         functools.partial(update_kernel, experts),
-        in_specs=[vmem] * (4 + len(state)),
-        out_specs=[vmem] * (len(state) + 1),
-        out_shape=[jax.ShapeDtypeStruct(v.shape, f32) for v in weights_now] * 3 + [jax.ShapeDtypeStruct((2, 6), f32)],
-        compiler_params=pltpu.CompilerParams(vmem_limit_bytes=VMEM_BYTES),
+        grid=(cuts,),
+        in_specs=[rows_of(v) for v in (*grads_now, *state)],
+        out_specs=[rows_of(v) for v in weights_now] * 3 + [whole(2, 6)],
+        out_shape=[jax.ShapeDtypeStruct(v.shape, f32) for v in weights_now] * 3
+        + [jax.ShapeDtypeStruct((2, 6), f32)],
+        compiler_params=params,
         name="lamb_update",
-    )(shared, small, g_exp, norms, *state)
+    )(*grads_now, *state)
 
     def restore(values):
         return (values[0], values[1], values[2].T, values[3].T, values[4][None], values[5][None])

time: 184 us -> 173 us (0.940)
  Pallas kernels: 179 us -> 170 us
    pallas_call x1, Pallas kernels: 79.1 us -> 73.4 us  [per_device(): pl.pallas_call(body, grid=(steps,), in_specs=backward_specs + [anywhere]...]
    pallas_call x1, Pallas kernels: 32 us -> 30 us  [per_device(): pl.pallas_call(functools.partial(expert_kernel, slots), grid_spec=pltpu.P...]
where the time goes in v4:
time: 173 us
  Pallas kernels  170 us (98%)
  local copies, waits for them, and re-layouts  2.15 us (1%)
    pallas_call x1, Pallas kernels, per_device(): pl.pallas_call(body, grid=(steps,), in_specs=backward_specs + [anywhere]...  73.4 us
    pallas_call x1, Pallas kernels, per_device(): pl.pallas_call(body, grid=(steps,), in_specs=token_specs + [whole(*v.shap...  62.8 us
    pallas_call x1, Pallas kernels, per_device(): pl.pallas_call(functools.partial(expert_kernel, slots), grid_spec=pltpu.P...  30 us
    pallas_call x1, Pallas kernels, per_device(): pl.pallas_call(functools.partial(update_kernel, experts), grid=(cuts,), i...  4.21 us

profile of v4, /device:TPU:0, one launch (start us, length us, event | category | flops | bytes accessed | tf_op | source)
XLA Modules:
  0.0 173.2 jit_solution(11856598085200457730)
XLA Ops:
  0.7 62.8 %attention_forward.1 = (bf16[1536,768]{1,0:T(8,128)(2,1)}, f32[1536,128]{1,0:T(8,128)}, bf16[1536,384]{1,0:T(8,128)(2,1)}, bf16[24,64,1152]{2,1,0:T(8,128)(2,1)}...) custom-call(bf16[3,392,384]{2,1,0:T(8,128)(2,1)} %bitcast.45, ...), custom_call_target="tpu_custom_call" | custom-call | tf_op jit(solution)/shard_map/attention_forward/pallas_call | solution.py:1339
  63.4 30.0 %experts.1 = (bf16[4,2,384,1536]{3,2,1,0:T(8,128)(2,1)}, bf16[1536,768]{1,0:T(8,128)(2,1)}) custom-call(s32[128]{0:T(128)} %bitcast.82, bf16[1536,768]{1,0:T(8,128)(2,1)} %get-tuple-element.62.hz_ref, s32[1,1536]{1,0:T(1,128)} %get-tuple-element.63.keyrow_ref, s32[1536,128]{1,0:T(8,128)} %get-tuple-element.64.keycol_ref, bf16[4,2,384,1536]{3,2,1,0:T(8,128)(2,1)} %bitcast.41), custom_call_target="tpu_custom_call" | custom-call | tf_op jit(solution)/shard_map/experts/pallas_call | solution.py:1387
  93.4 73.4 %attention_backward.1 = (bf16[3,392,384]{2,1,0:T(8,128)(2,1)}, f32[3,392,384]{2,1,0:T(8,128)}, f32[2,48,1536]{2,1,0:T(8,128)}, f32[4,48,384]{2,1,0:T(8,128)}, f32[16,48]{1,0:T(8,128)}, /*index=5*/f32[8,128]{1,0:T(8,128)}) custom-call(s32[24,128]{1,0:T(8,128)} %get-tuple-element.59.refs_0_, bf16[2,384,896]{2,1,0:T(8,128)(2,1)} %bitcast.55, ...), custom_call_target="tpu_custom_call" | custom-call | tf_op jit(solution)/shard_map/attention_backward/pallas_call | solution.py:1460
  166.8 0.0 copy-start.1
  166.8 0.0 copy-start
  166.8 4.2 %lamb_update.1 = (f32[48,1152]{1,0:T(8,128)}, f32[48,384]{1,0:T(8,128)}, f32[4,48]{1,0:T(4,128)}, f32[4,48]{1,0:T(4,128)}, f32[48,1536]{1,0:T(8,128)}, /*index=5...) custom-call(f32[4,48,384]{2,1,0:T(8,128)} %get-tuple-element.74.refs, ...), custom_call_target="tpu_custom_call" | custom-call | tf_op jit(solution)/shard_map/lamb_update/pallas_call | solution.py:1521
  171.0 0.0 copy-done.1
  171.0 0.9 copy.46
  171.9 0.0 copy-done
  171.9 1.2 copy.47
Async XLA Ops:
  166.8 4.2 %copy-start.1 = (bf16[3,392,384]{2,1,0:T(8,128)(2,1)S(1)}, bf16[3,392,384]{2,1,0:T(8,128)(2,1)}, u32[]{:S(2)}) copy-start(bf16[3,392,384]{2,1,0:T(8,128)(2,1)} %get-tuple-element.72) | copy-start | bytes 2709508
  166.8 5.2 %copy-start = (f32[3,392,384]{2,1,0:T(8,128)S(1)}, f32[3,392,384]{2,1,0:T(8,128)}, u32[]{:S(2)}) copy-start(f32[3,392,384]{2,1,0:T(8,128)} %get-tuple-element.73) | copy-start | bytes 5419012

commit v5 on v4

--- a/solution.py
+++ b/solution.py
@@ -134,8 +134,8 @@
         x_ref, g_ref, *token_rows = refs[:5]
         qkv_w, proj_w, router_w, norm_w, in_w, out_w = refs[5:11]
         hz_ref, pr_ref, attn_ref, qkv_ref, p_ref, key_ref, keyrow_ref, count_ref, combo_ref, ws_out, we_ref = refs[11:22]
-        combos, xp, gp, wide, codes, regions, carry, w_ref, sh, ex, ws_sem = refs[22:33]
-        shared_sems, gather_sems = refs[33:40], refs[40:]
+        combos, xp_all, gp_all, normed_all, xb, gb, in_sem, wide, codes, regions, carry, w_ref, sh, ex, ws_sem = refs[22:37]
+        shared_sems, gather_sems = refs[37:44], refs[44:]
         gather = Gather(depth, ex, we_ref, gather_sems)
         shared = SharedGather(depth, sh, w_ref, shared_sems)
 
@@ -165,34 +165,61 @@
 
         g = gather
 
-        def first_weights():
+        def from_z():
             shared.along_z()
             gather.turns(0)
+
+        def first_weights():
+            gather.line(1)
             shared.along_x()
             store_shared()
-            gather.line(1)
 
         plan = {
             (0, "start"): [enter],
+            (0, "prepared"): [from_z],
             (0, "norm"): [first_weights],
             (0, 7): [lambda: g.line(2)],
             (0, "end"): [lambda: g.turns(1)],
             (1, 3): [lambda: g.line(3)],
             (1, 7): [lambda: g.turns(2)],
             (2, "qkv"): [lambda: g.turns(3)],
-            (2, "end"): [g.last, leave],
+            (2, 7): [lambda: g.last(0, 2)],
+            (2, "end"): [lambda: g.last(2, depth), leave],
         }
     else:
         x_ref, g_ref, *token_rows = refs[:5]
         w_ref = refs[5]
         hz_ref, pr_ref, attn_ref, qkv_ref, p_ref, key_ref, keyrow_ref, count_ref, combo_ref = refs[6:15]
-        combos, xp, gp, wide, codes, regions, carry = refs[15:22]
+        combos, xp_all, gp_all, normed_all, xb, gb, in_sem, wide, codes, regions, carry = refs[15:26]
     rows = per_group * PAD
     width = x_ref.shape[-1]
     groups = width // 128
+    steps = xb.shape[0]
     run_hooks(plan, step, "start")
-    load_windows(x_ref, wide, xp, per_group)
-    load_windows(g_ref, wide, gp, per_group)
+
+    def fetch(k):
+        return (
+            pltpu.make_async_copy(x_ref.at[k], xb.at[k], in_sem.at[0, k]),
+            pltpu.make_async_copy(g_ref.at[k], gb.at[k], in_sem.at[1, k]),
+        )
+
+    @pl.when(step == 0)
+    def _():
+        for k in range(steps):
+            for copy in fetch(k):
+                copy.start()
+
+        def prepare(k, _):
+            for copy in fetch(k):
+                copy.wait()
+            load_windows(xb.at[pl.ds(k, 1)], wide, xp_all.at[k], per_group)
+            load_windows(gb.at[pl.ds(k, 1)], wide, gp_all.at[k], per_group)
+            normed_all[k] = norm_stats(xp_all[k])[0]
+            return 0
+
+        lax.fori_loop(0, steps, prepare, 0)
+
+    run_hooks(plan, step, "prepared")
 
     @pl.when(step == 0)
     def _():
@@ -203,6 +230,21 @@
             piece = packed[:, k * WINDOW : (k + 1) * WINDOW]
             combos[k : k + 1, 0:WINDOW] = piece
             combos[k : k + 1, PAD : PAD + WINDOW] = piece
+        lane = lax.broadcasted_iota(jnp.int32, (rows, 128), 1)
+        before = lax.broadcasted_iota(jnp.int32, (rows, rows), 1) < lax.broadcasted_iota(jnp.int32, (rows, rows), 0)
+        before = jnp.where(before, 1.0, 0.0).astype(bf16)
+        for k in range(steps):
+            route = route_of(token_columns(combos.at[k * per_group : (k + 1) * per_group], per_group))
+            onehot = jnp.where(lane == route, 1.0, 0.0)
+            ranks = dot_nn(before, onehot.astype(bf16)) + carry[0:1, :]
+            slot = jnp.sum(ranks * onehot, axis=-1, keepdims=True)
+            seen = jnp.sum(onehot, axis=-1, keepdims=True)
+            key = (route.astype(f32) * slots + slot) * seen + (seen - 1.0)
+            key = jnp.broadcast_to(key, (rows, 128))
+            key_ref[k * rows : (k + 1) * rows, :] = key.astype(jnp.int32)
+            keyrow_ref[:, k * rows : (k + 1) * rows] = jnp.transpose(key)[0:1, :].astype(jnp.int32)
+            carry[...] = carry[...] + jnp.sum(onehot, axis=0, keepdims=True)
+        count_ref[...] = carry[...].astype(jnp.int32)
 
     combo_ref[...] = combos[pl.ds(pl.multiple_of(step * per_group, per_group), per_group), :]
     combo = token_columns(combo_ref, per_group)
@@ -214,8 +256,8 @@
     for k in range(per_group):
         regions[k] = jnp.concatenate([flat[k : k + 1, :]] * 2, axis=1)
 
-    normed, _ = norm_stats(xp[...])
     run_hooks(plan, step, "norm")
+    normed = normed_all[step]
     small = small_part(w_ref)
     small_t = jnp.transpose(small.astype(f32))
     a1, b1, a2, b2 = (small_t[experts + i : experts + i + 1, :] for i in range(4))
@@ -256,7 +298,7 @@
 
     lax.fori_loop(0, per_group // GROUP, windows, 0)
 
-    y1 = xp[...] + dot_nn(attn_ref[...], weight_part(w_ref, 3))
+    y1 = xp_all[step] + dot_nn(attn_ref[...], weight_part(w_ref, 3))
     normed2, _ = norm_stats(y1)
     h2 = (normed2 * a2 + b2).astype(bf16)
     lane = lax.broadcasted_iota(jnp.int32, (rows, 128), 1)
@@ -266,21 +308,10 @@
     pr_ref[...] = pr
     chosen = lane == route
     gate = jnp.sum(jnp.where(chosen, pr, 0.0), axis=-1, keepdims=True)
-    gv = gp[...] * valid
+    gv = gp_all[step] * valid
     hz_ref[:, 0:width] = h2
     hz_ref[:, width : 2 * width] = (gate * gv).astype(bf16)
 
-    onehot = jnp.where(chosen, 1.0, 0.0)
-    before = lax.broadcasted_iota(jnp.int32, (rows, rows), 1) < lax.broadcasted_iota(jnp.int32, (rows, rows), 0)
-    ranks = dot_nn(jnp.where(before, 1.0, 0.0).astype(bf16), onehot.astype(bf16)) + carry[0:1, :]
-    slot = jnp.sum(ranks * onehot, axis=-1, keepdims=True)
-    seen = jnp.sum(onehot, axis=-1, keepdims=True)
-    key = (route.astype(f32) * slots + slot) * seen + (seen - 1.0)
-    key = jnp.broadcast_to(key, (rows, 128))
-    key_ref[...] = key.astype(jnp.int32)
-    keyrow_ref[...] = jnp.transpose(key)[0:1, :].astype(jnp.int32)
-    carry[...] = carry[...] + jnp.sum(onehot, axis=0, keepdims=True)
-    count_ref[...] = carry[...].astype(jnp.int32)
     run_hooks(plan, step, "end")
 
 
@@ -694,8 +725,10 @@
         def _():
             self.turn(z + s)
 
-    def last(self):
-        for zo in range(self.depth):
+    def last(self, first, end):
+        turn = 1 - 2 * lax.div(self.z, self.depth // 2)
+        for j in range(first, end):
+            zo = lax.rem(self.z + j * turn + self.depth, self.depth)
             for kind, ck in ((1, 3), (2, 4)):
                 self.y_copy(kind, zo, self.x).wait_recv()
                 self.c_copy(ck, zo, self.c).start()
@@ -1301,15 +1334,15 @@
         return pl.BlockSpec(shape, lambda i, *_: zeros)
 
     lanes = width // 128
-    token_specs = [by_step(1, group_rows, width), by_step(1, group_rows, width)] + [whole(1, rows_here), whole(rows_here), whole(rows_here)]
+    token_specs = [anywhere] * 2 + [whole(1, rows_here), whole(rows_here), whole(rows_here)]
     forward_out = [
         by_step(rows, 2 * width),
         by_step(rows, 128),
         by_step(rows, width),
         by_step(per_group, PAD, 3 * width),
         by_step(per_group, lanes, PAD, 4 * PAD),
-        by_step(rows, 128),
-        pl.BlockSpec((1, rows), lambda i: (0, i)),
+        whole(padded, 128),
+        whole(1, padded),
         whole(1, 128),
         by_step(per_group, 128),
     ]
@@ -1326,8 +1359,12 @@
     ]
     forward_scratch = [
         pltpu.VMEM((windows, 128), jnp.int32),
-        pltpu.VMEM((rows, width), f32),
-        pltpu.VMEM((rows, width), f32),
+        pltpu.VMEM((steps, rows, width), f32),
+        pltpu.VMEM((steps, rows, width), f32),
+        pltpu.VMEM((steps, rows, width), f32),
+        pltpu.VMEM(x3.shape, x3.dtype),
+        pltpu.VMEM(g3.shape, g3.dtype),
+        pltpu.SemaphoreType.DMA((2, steps)),
         pltpu.VMEM((group_rows, width), f32),
         pltpu.VMEM((rows, 1), jnp.int32),
         pltpu.VMEM((per_group, 1, 4 * PAD), jnp.int32),

time: 173 us -> 167 us (0.965)
  Pallas kernels: 170 us -> 164 us
    pallas_call x1, Pallas kernels: 73.4 us -> 69.2 us  [per_device(): pl.pallas_call(body, grid=(steps,), in_specs=backward_specs + [anywhere]...]
    pallas_call x1, Pallas kernels: 62.8 us -> 58.7 us  [per_device(): pl.pallas_call(body, grid=(steps,), in_specs=token_specs + [whole(*v.shap...]
    pallas_call x1, Pallas kernels: 30 us -> 32 us  [per_device(): pl.pallas_call(functools.partial(expert_kernel, slots), grid_spec=pltpu.P...]
where the time goes in v5:
time: 167 us
  Pallas kernels  164 us (98%)
  local copies, waits for them, and re-layouts  2.15 us (1%)
    pallas_call x1, Pallas kernels, per_device(): pl.pallas_call(body, grid=(steps,), in_specs=backward_specs + [anywhere]...  69.2 us
    pallas_call x1, Pallas kernels, per_device(): pl.pallas_call(body, grid=(steps,), in_specs=token_specs + [whole(*v.shap...  58.7 us
    pallas_call x1, Pallas kernels, per_device(): pl.pallas_call(functools.partial(expert_kernel, slots), grid_spec=pltpu.P...  32 us
    pallas_call x1, Pallas kernels, per_device(): pl.pallas_call(functools.partial(update_kernel, experts), grid=(cuts,), i...  4.21 us

profile of v5, /device:TPU:0, one launch (start us, length us, event | category | flops | bytes accessed | tf_op | source)
XLA Modules:
  0.0 166.9 jit_solution(7230046124984400069)
XLA Ops:
  0.7 58.7 %attention_forward.1 = (bf16[1536,768]{1,0:T(8,128)(2,1)}, f32[1536,128]{1,0:T(8,128)}, bf16[1536,384]{1,0:T(8,128)(2,1)}, bf16[24,64,1152]{2,1,0:T(8,128)(2,1)}...) custom-call(bf16[3,392,384]{2,1,0:T(8,128)(2,1)} %bitcast.45, ...), custom_call_target="tpu_custom_call" | custom-call | tf_op jit(solution)/shard_map/attention_forward/pallas_call | solution.py:1376
  59.4 32.0 %experts.1 = (bf16[4,2,384,1536]{3,2,1,0:T(8,128)(2,1)}, bf16[1536,768]{1,0:T(8,128)(2,1)}) custom-call(s32[128]{0:T(128)} %bitcast.82, bf16[1536,768]{1,0:T(8,128)(2,1)} %get-tuple-element.62.hz_ref, s32[1,1536]{1,0:T(1,128)} %get-tuple-element.63.keyrow_ref, s32[1536,128]{1,0:T(8,128)} %get-tuple-element.64.keycol_ref, bf16[4,2,384,1536]{3,2,1,0:T(8,128)(2,1)} %bitcast.41), custom_call_target="tpu_custom_call" | custom-call | tf_op jit(solution)/shard_map/experts/pallas_call | solution.py:1424
  91.3 69.2 %attention_backward.1 = (bf16[3,392,384]{2,1,0:T(8,128)(2,1)}, f32[3,392,384]{2,1,0:T(8,128)}, f32[2,48,1536]{2,1,0:T(8,128)}, f32[4,48,384]{2,1,0:T(8,128)}, f32[16,48]{1,0:T(8,128)}, /*index=5*/f32[8,128]{1,0:T(8,128)}) custom-call(s32[24,128]{1,0:T(8,128)} %get-tuple-element.59.refs_0_, bf16[2,384,896]{2,1,0:T(8,128)(2,1)} %bitcast.55, ...), custom_call_target="tpu_custom_call" | custom-call | tf_op jit(solution)/shard_map/attention_backward/pallas_call | solution.py:1497
  160.5 0.0 copy-start.1
  160.5 0.0 copy-start
  160.5 4.2 %lamb_update.1 = (f32[48,1152]{1,0:T(8,128)}, f32[48,384]{1,0:T(8,128)}, f32[4,48]{1,0:T(4,128)}, f32[4,48]{1,0:T(4,128)}, f32[48,1536]{1,0:T(8,128)}, /*index=5...) custom-call(f32[4,48,384]{2,1,0:T(8,128)} %get-tuple-element.74.refs, ...), custom_call_target="tpu_custom_call" | custom-call | tf_op jit(solution)/shard_map/lamb_update/pallas_call | solution.py:1558
  164.7 0.0 copy-done.1
  164.8 0.9 copy.46
  165.7 0.0 copy-done
  165.7 1.2 copy.47
Async XLA Ops:
  160.5 4.2 %copy-start.1 = (bf16[3,392,384]{2,1,0:T(8,128)(2,1)S(1)}, bf16[3,392,384]{2,1,0:T(8,128)(2,1)}, u32[]{:S(2)}) copy-start(bf16[3,392,384]{2,1,0:T(8,128)(2,1)} %get-tuple-element.72) | copy-start | bytes 2709508
  160.5 5.2 %copy-start = (f32[3,392,384]{2,1,0:T(8,128)S(1)}, f32[3,392,384]{2,1,0:T(8,128)}, u32[]{:S(2)}) copy-start(f32[3,392,384]{2,1,0:T(8,128)} %get-tuple-element.73) | copy-start | bytes 5419012

commit v6 on v5

--- a/solution.py
+++ b/solution.py
@@ -133,9 +133,9 @@
     if fast:
         x_ref, g_ref, *token_rows = refs[:5]
         qkv_w, proj_w, router_w, norm_w, in_w, out_w = refs[5:11]
-        hz_ref, pr_ref, attn_ref, qkv_ref, p_ref, key_ref, keyrow_ref, count_ref, combo_ref, ws_out, we_ref = refs[11:22]
-        combos, xp_all, gp_all, normed_all, xb, gb, in_sem, wide, codes, regions, carry, w_ref, sh, ex, ws_sem = refs[22:37]
-        shared_sems, gather_sems = refs[37:44], refs[44:]
+        hz_ref, pr_ref, attn_ref, qkv_ref, p_ref, key_ref, keyrow_ref, count_ref, combo_ref, x_out, g_out, ws_out, we_ref = refs[11:24]
+        combos, xp_all, gp_all, normed_all, xb, gb, in_sem, wide, codes, regions, carry, w_ref, sh, ex, ws_sem = refs[24:39]
+        shared_sems, gather_sems = refs[39:46], refs[46:]
         gather = Gather(depth, ex, we_ref, gather_sems)
         shared = SharedGather(depth, sh, w_ref, shared_sems)
 
@@ -189,8 +189,8 @@
     else:
         x_ref, g_ref, *token_rows = refs[:5]
         w_ref = refs[5]
-        hz_ref, pr_ref, attn_ref, qkv_ref, p_ref, key_ref, keyrow_ref, count_ref, combo_ref = refs[6:15]
-        combos, xp_all, gp_all, normed_all, xb, gb, in_sem, wide, codes, regions, carry = refs[15:26]
+        hz_ref, pr_ref, attn_ref, qkv_ref, p_ref, key_ref, keyrow_ref, count_ref, combo_ref, x_out, g_out = refs[6:17]
+        combos, xp_all, gp_all, normed_all, xb, gb, in_sem, wide, codes, regions, carry = refs[17:28]
     rows = per_group * PAD
     width = x_ref.shape[-1]
     groups = width // 128
@@ -309,6 +309,8 @@
     chosen = lane == route
     gate = jnp.sum(jnp.where(chosen, pr, 0.0), axis=-1, keepdims=True)
     gv = gp_all[step] * valid
+    g_out[...] = gv
+    x_out[...] = xp_all[step]
     hz_ref[:, 0:width] = h2
     hz_ref[:, width : 2 * width] = (gate * gv).astype(bf16)
 
@@ -376,7 +378,7 @@
     else:
         out_ref, dx_ref, shared_ref, small_ref = refs[:4]
         refs = refs[4:]
-    xp, gp, wide, outp, dattn, dqkv, acc, acc_s = refs[:8]
+    gp, wide, outp, dattn, dqkv, acc, acc_w, acc_s = refs[:8]
     buffers, in_sem = refs[8:16], refs[16]
     w_ref = buffers[0]
     x_all, g_all, tok_all, pr_all, attn_all, qkv_all, p_all = buffers[1:]
@@ -425,7 +427,7 @@
         def leave():
             for part in range(4):
                 shape = shared_ref.shape[2:]
-                shared_ref[part // 2, part % 2] = acc[part].astype(bf16).reshape(shape)
+                shared_ref[part // 2, part % 2] = shared_grad(part).reshape(shape)
             small_ref[0:8] = acc_s[0:8]
             small_ref[8:16] = acc_s[128:136]
             shared_scatter(
@@ -447,6 +449,11 @@
     else:
         plan = {(0, "start"): [fetch_all]}
     rows = per_group * PAD
+
+    def shared_grad(part):
+        width = acc.shape[0]
+        return (acc[...] if part == 3 else acc_w[:, part * width : (part + 1) * width]).astype(bf16)
+
     width = x_all.shape[-1]
     groups = width // 128
     scale = HEAD_DIM**-0.5
@@ -454,6 +461,7 @@
     @pl.when(step == 0)
     def _():
         acc[...] = jnp.zeros_like(acc)
+        acc_w[...] = jnp.zeros_like(acc_w)
         acc_s[...] = jnp.zeros_like(acc_s)
 
     run_hooks(plan, step, "start")
@@ -464,16 +472,13 @@
 
     for i in range(1, 8):
         fetch(i, step).wait()
-    load_windows(x_all.at[pl.ds(step, 1)], wide, xp, per_group)
-    load_windows(g_all.at[pl.ds(step, 1)], wide, gp, per_group)
     combo = token_columns(combo_ref, per_group)
-    valid = valid_of(combo)
     route = route_of(combo)
     small = small_part(w_ref)
     small_t = jnp.transpose(small.astype(f32))
     a1, b1, a2, b2 = (small_t[experts + i : experts + i + 1, :] for i in range(4))
-    y1 = xp[...] + dot_nn(attn_all[step], weight_part(w_ref, 3))
-    gv = gp[...] * valid
+    y1 = x_all[step] + dot_nn(attn_all[step], weight_part(w_ref, 3))
+    gv = g_all[step]
     z = tok_all[step, :, 0:width].astype(f32)
     lane = lax.broadcasted_iota(jnp.int32, (rows, 128), 1)
     chosen = lane == route
@@ -493,7 +498,7 @@
     dy1 = gv + norm_back(dh2, n2, r2, a2)
     gp[...] = dy1
     da = dy1.astype(bf16)
-    acc[3] += dot_tn(attn_all[step], da)
+    acc[...] += dot_tn(attn_all[step], da)
     dattn[...] = dot_nt(da, weight_part(w_ref, 3)).astype(bf16)
     run_hooks(plan, step, "pre")
 
@@ -515,9 +520,9 @@
             dv = dot_nn(p_low, d_all)
             dk = dot_nn(ds, q_all)
             dq = gather_heads(dot_tn(ds, k), masks) * scale
-            dqkv[0, at, cols] = dq.astype(bf16)
-            dqkv[1, at, cols] = dk.astype(bf16)
-            dqkv[2, at, cols] = dv.astype(bf16)
+            dqkv[at, 0 * width + lg * 128 : 0 * width + (lg + 1) * 128] = dq.astype(bf16)
+            dqkv[at, 1 * width + lg * 128 : 1 * width + (lg + 1) * 128] = dk.astype(bf16)
+            dqkv[at, 2 * width + lg * 128 : 2 * width + (lg + 1) * 128] = dv.astype(bf16)
 
     def windows(j, _):
         for k in range(GROUP):
@@ -528,13 +533,10 @@
 
     lax.fori_loop(0, per_group // GROUP, windows, 0)
 
-    n1, r1 = norm_stats(xp[...])
+    n1, r1 = norm_stats(x_all[step])
     h1 = (n1 * a1 + b1).astype(bf16)
-    dh1 = jnp.zeros((rows, width), f32)
-    for part in range(3):
-        dpart = dqkv[part]
-        acc[part] += dot_tn(h1, dpart)
-        dh1 = dh1 + dot_nt(dpart, weight_part(w_ref, part))
+    acc_w[...] += dot_tn(h1, dqkv[...])
+    dh1 = dot_nt(dqkv[:, 0 : 2 * width], w_ref[0, :, 0 : 2 * width]) + dot_nt(dqkv[:, 2 * width :], weight_part(w_ref, 2))
     acc_s[128:129] += jnp.sum(dh1 * n1, axis=0, keepdims=True)
     acc_s[129:130] += jnp.sum(dh1, axis=0, keepdims=True)
     outp[...] = gp[...] + norm_back(dh1, n1, r1, a1)
@@ -545,7 +547,7 @@
         @pl.when(step == pl.num_programs(0) - 1)
         def _():
             for part in range(4):
-                shared_ref[part] = acc[part].astype(bf16)
+                shared_ref[part] = shared_grad(part)
             small_ref[0:8] = acc_s[0:8]
             small_ref[8:16] = acc_s[128:136]
 
@@ -1345,6 +1347,8 @@
         whole(1, padded),
         whole(1, 128),
         by_step(per_group, 128),
+        by_step(rows, width),
+        by_step(rows, width),
     ]
     forward_shape = [
         jax.ShapeDtypeStruct((padded, 2 * width), bf16),
@@ -1356,6 +1360,8 @@
         jax.ShapeDtypeStruct((1, padded), jnp.int32),
         jax.ShapeDtypeStruct((1, 128), jnp.int32),
         jax.ShapeDtypeStruct((windows, 128), jnp.int32),
+        jax.ShapeDtypeStruct((padded, width), f32),
+        jax.ShapeDtypeStruct((padded, width), f32),
     ]
     forward_scratch = [
         pltpu.VMEM((windows, 128), jnp.int32),
@@ -1417,7 +1423,7 @@
             compiler_params=params,
             name="attention_forward",
         )(x3, g3, *token_rows, w_all)
-    hz, pr, attn, qkv, probs, key, key_row, counts, combo = forward
+    hz, pr, attn, qkv, probs, key, key_row, counts, combo, x_pad, g_pad = forward
     w_all = w_all.reshape(2, width, 2 * width + 128)
     w_exp = w_exp.reshape(experts, 2, width, hidden)
 
@@ -1448,8 +1454,8 @@
 
     staged = (
         w_all,
-        x3,
-        g3,
+        x_pad.reshape(steps, rows, width),
+        g_pad.reshape(steps, rows, width),
         tok.reshape(steps, rows, 2 * width),
         pr.reshape(steps, rows, 128),
         attn.reshape(steps, rows, width),
@@ -1472,12 +1478,12 @@
     ]
     backward_scratch = [
         pltpu.VMEM((rows, width), f32),
-        pltpu.VMEM((rows, width), f32),
         pltpu.VMEM((group_rows, width), f32),
         pltpu.VMEM((rows, width), f32),
         pltpu.VMEM((rows, width), bf16),
-        pltpu.VMEM((3, rows, width), bf16),
-        pltpu.VMEM((4, width, width), f32),
+        pltpu.VMEM((rows, 3 * width), bf16),
+        pltpu.VMEM((width, width), f32),
+        pltpu.VMEM((width, 3 * width), f32),
         pltpu.VMEM((136, width), f32),
         *[pltpu.VMEM(v.shape, v.dtype) for v in staged],
         pltpu.SemaphoreType.DMA((8, steps)),

time: 167 us -> 167 us (level)
  no operation moved by 1% of the time
where the time goes in v6:
time: 167 us
  Pallas kernels  164 us (98%)
  local copies, waits for them, and re-layouts  2.15 us (1%)
    pallas_call x1, Pallas kernels, per_device(): pl.pallas_call(body, grid=(steps,), in_specs=backward_specs + [anywhere]...  69.2 us
    pallas_call x1, Pallas kernels, per_device(): pl.pallas_call(body, grid=(steps,), in_specs=token_specs + [whole(*v.shap...  59.2 us
    pallas_call x1, Pallas kernels, per_device(): pl.pallas_call(functools.partial(expert_kernel, slots), grid_spec=pltpu.P...  31.8 us
    pallas_call x1, Pallas kernels, per_device(): pl.pallas_call(functools.partial(update_kernel, experts), grid=(cuts,), i...  4.21 us

profile of v6, /device:TPU:0, one launch (start us, length us, event | category | flops | bytes accessed | tf_op | source)
XLA Modules:
  0.0 167.2 jit_solution(11146211682468581627)
XLA Ops:
  0.7 59.2 %attention_forward.1 = (bf16[1536,768]{1,0:T(8,128)(2,1)}, f32[1536,128]{1,0:T(8,128)}, bf16[1536,384]{1,0:T(8,128)(2,1)}, bf16[24,64,1152]{2,1,0:T(8,128)(2,1)}...) custom-call(bf16[3,392,384]{2,1,0:T(8,128)(2,1)} %bitcast.67, ...), custom_call_target="tpu_custom_call" | custom-call | tf_op jit(solution)/shard_map/attention_forward/pallas_call | solution.py:1382
  59.8 31.8 %experts.1 = (bf16[4,2,384,1536]{3,2,1,0:T(8,128)(2,1)}, bf16[1536,768]{1,0:T(8,128)(2,1)}) custom-call(s32[128]{0:T(128)} %bitcast.84, bf16[1536,768]{1,0:T(8,128)(2,1)} %get-tuple-element.66.hz_ref, s32[1,1536]{1,0:T(1,128)} %get-tuple-element.67.keyrow_ref, s32[1536,128]{1,0:T(8,128)} %get-tuple-element.68.keycol_ref, bf16[4,2,384,1536]{3,2,1,0:T(8,128)(2,1)} %bitcast.43), custom_call_target="tpu_custom_call" | custom-call | tf_op jit(solution)/shard_map/experts/pallas_call | solution.py:1430
  91.6 69.2 %attention_backward.1 = (bf16[3,392,384]{2,1,0:T(8,128)(2,1)}, f32[3,392,384]{2,1,0:T(8,128)}, f32[2,48,1536]{2,1,0:T(8,128)}, f32[4,48,384]{2,1,0:T(8,128)}, f32[16,48]{1,0:T(8,128)}, /*index=5*/f32[8,128]{1,0:T(8,128)}) custom-call(s32[24,128]{1,0:T(8,128)} %get-tuple-element.61.refs_0_, bf16[2,384,896]{2,1,0:T(8,128)(2,1)} %bitcast.56, ...), custom_call_target="tpu_custom_call" | custom-call | tf_op jit(solution)/shard_map/attention_backward/pallas_call | solution.py:1503
  160.8 0.0 copy-start.1
  160.8 0.0 copy-start
  160.8 4.2 %lamb_update.1 = (f32[48,1152]{1,0:T(8,128)}, f32[48,384]{1,0:T(8,128)}, f32[4,48]{1,0:T(4,128)}, f32[4,48]{1,0:T(4,128)}, f32[48,1536]{1,0:T(8,128)}, /*index=5...) custom-call(f32[4,48,384]{2,1,0:T(8,128)} %get-tuple-element.78.refs, ...), custom_call_target="tpu_custom_call" | custom-call | tf_op jit(solution)/shard_map/lamb_update/pallas_call | solution.py:1564
  165.0 0.0 copy-done.1
  165.0 0.9 copy.46
  165.9 0.0 copy-done
  166.0 1.2 copy.47
Async XLA Ops:
  160.8 4.2 %copy-start.1 = (bf16[3,392,384]{2,1,0:T(8,128)(2,1)S(1)}, bf16[3,392,384]{2,1,0:T(8,128)(2,1)}, u32[]{:S(2)}) copy-start(bf16[3,392,384]{2,1,0:T(8,128)(2,1)} %get-tuple-element.76) | copy-start | bytes 2709508
  160.8 5.2 %copy-start = (f32[3,392,384]{2,1,0:T(8,128)S(1)}, f32[3,392,384]{2,1,0:T(8,128)}, u32[]{:S(2)}) copy-start(f32[3,392,384]{2,1,0:T(8,128)} %get-tuple-element.77) | copy-start | bytes 5419012
